TPU v7x, 128 devices: a whole 4x4x4 slice. The times are simulated.
128 devices in a mesh: prow: 8 (over z, core), pcol: 16 (over x, y).
Axes of the slice: x: 4, y: 4, z: 4, core: 2. Of those that a mesh axis runs over, the one named last changes fastest.
Arguments:
- factors: bfloat16 [4, 4096, 512], P(None, ('prow', 'pcol')), may hold values from -0.25 to 0.25
- x_factor: bfloat16 [512, 512], replicated, may hold values from -0.25 to 0.25
- zinv_factor: bfloat16 [512, 512], replicated, may hold values from -0.25 to 0.25
- placement: int32 [4096], replicated, may hold values from 0 to 4095, as said below
Outputs:
- trailing: float32 [4096, 4096], P('prow', 'pcol')
- panels: float32 [4096, 1024], P('prow', 'pcol')
Inputs may be any that keep to these rules, and one draw needn't show every extreme that they name: placement is a permutation of the Schur rows; device d (grid rows slowest) assembles the rows placement[d * 32] to placement[d * 32 + 31]; among one device's rows at most 8 share the same owner grid row (natural row i belongs to grid row (i div 64) mod 8), and some device has exactly 8 such rows.
All inputs are finite; a program needn't handle non-finite values.
Results may differ from a plain program's by a relative error of at most 0.003.
Values may be sent and summed in bfloat16 or wider, within the bound.
A program may use at most 128 MiB of HBM per device.

v0:
```python
import jax
import jax.numpy as jnp
from jax import lax
from jax.sharding import PartitionSpec as P

RANK = 4
NB = 64
K = 1024


rank_signs = (1.0, 1.0, -1.0, -1.0)


def project(segment, factor_mat):
    span_cols = segment.shape[1]
    flat_rows = segment.reshape(RANK * span_cols, segment.shape[2])
    images = jnp.dot(flat_rows, factor_mat, preferred_element_type=jnp.float32).astype(jnp.bfloat16)
    return images.reshape(RANK, span_cols, factor_mat.shape[1])


def pair_terms(left_x, left_z, right_x, right_z):
    weights = jnp.array(rank_signs, jnp.float32)
    contract = (((1,), (1,)), ((), ()))
    span_rows = left_x.shape[1]
    span_cols = right_x.shape[1]
    width = left_x.shape[2]
    inner_x = lax.dot_general(
        left_x.reshape(RANK * span_rows, width),
        right_x.reshape(RANK * span_cols, width),
        contract,
        preferred_element_type=jnp.float32,
    )
    inner_z = lax.dot_general(
        left_z.reshape(RANK * span_rows, width),
        right_z.reshape(RANK * span_cols, width),
        contract,
        preferred_element_type=jnp.float32,
    )
    product = (inner_x * inner_z).reshape(RANK, span_rows, RANK, span_cols)
    return jnp.einsum("r,riqj,q->ij", weights, product, weights)


def per_device(factors, x_factor, zinv_factor, placement):
    prow_count = lax.axis_size("prow")
    pcol_count = lax.axis_size("pcol")
    devices_all = prow_count * pcol_count
    rows_dev = factors.shape[1]
    total_rows = placement.shape[0]
    local_rows = total_rows // prow_count
    local_cols = total_rows // pcol_count
    prow_id = lax.axis_index("prow")
    pcol_id = lax.axis_index("pcol")
    inverse = (
        jnp.zeros((total_rows,), jnp.int32)
        .at[placement]
        .set(jnp.arange(total_rows, dtype=jnp.int32))
    )
    slot_k = jnp.arange(local_rows)
    natural_k = slot_k // NB * NB * prow_count + prow_id * NB + slot_k % NB
    own_x = project(factors, x_factor)
    own_z = project(factors, zinv_factor)
    blank_rows = jnp.zeros((rows_dev, total_rows), jnp.float32)
    schur_rows = blank_rows.at[:, placement].set(
        pair_terms(
            own_x,
            own_z,
            lax.all_gather(own_x, ("prow", "pcol"), axis=1, tiled=True),
            lax.all_gather(own_z, ("prow", "pcol"), axis=1, tiled=True),
        )
    )
    device_id = lax.axis_index(("prow", "pcol"))
    my_rows = lax.dynamic_slice_in_dim(placement, device_id * rows_dev, rows_dev)
    capacity = 2 * rows_dev // prow_count
    target = my_rows // NB % prow_count
    prow_ids = jnp.arange(prow_count)
    onehot = (target[:, None] == prow_ids[None, :]).astype(jnp.int32)
    rank_in = jnp.sum((jnp.cumsum(onehot, axis=0) - onehot) * onehot, axis=1)
    select = (
        (target[None, None, :] == prow_ids[:, None, None])
        & (rank_in[None, None, :] == jnp.arange(capacity)[None, :, None])
    ).astype(jnp.float32)
    packed = jnp.dot(
        select.reshape(prow_count * capacity, rows_dev), schur_rows, precision=lax.Precision.HIGHEST
    )
    packed = packed.reshape(prow_count, capacity, total_rows // (NB * pcol_count), pcol_count, NB)
    packed = packed.transpose(0, 3, 1, 2, 4).reshape(prow_count, pcol_count, capacity, local_cols)
    received = lax.all_to_all(
        packed.reshape(devices_all, capacity, local_cols),
        ("prow", "pcol"),
        split_axis=0,
        concat_axis=0,
        tiled=True,
    )
    received = received.reshape(devices_all * capacity, local_cols)
    all_target = (placement // NB % prow_count).reshape(devices_all, rows_dev)
    earlier = jnp.arange(rows_dev)[None, :, None] > jnp.arange(rows_dev)[None, None, :]
    slot_ranks = jnp.sum(
        ((all_target[:, :, None] == all_target[:, None, :]) & earlier).astype(jnp.int32), axis=2
    ).reshape(total_rows)
    position = inverse[natural_k]
    flat_index = position // rows_dev * capacity + slot_ranks[position]
    schur_local = received[flat_index]
    lead_cols = K // pcol_count
    front_cols = schur_local[:, :lead_cols]
    row_panel = lax.all_gather(front_cols, "pcol", axis=1, tiled=True)
    row_panel = (
        row_panel.reshape(local_rows, pcol_count, lead_cols // NB, NB)
        .transpose(0, 2, 1, 3)
        .reshape(local_rows, K)
    )
    lead_rows = K // prow_count
    top_panel, top_cols = (
        lax.all_gather(row_panel[:lead_rows], "prow", axis=0, tiled=True),
        lax.all_gather(schur_local[:lead_rows], "prow", axis=0, tiled=True),
    )

    def natural_rows(stacked):
        return (
            stacked.reshape(prow_count, lead_rows // NB, NB, stacked.shape[1])
            .transpose(1, 0, 2, 3)
            .reshape(K, stacked.shape[1])
        )

    leading = jnp.linalg.cholesky(natural_rows(top_panel))
    panel_rows = lax.linalg.triangular_solve(
        leading, row_panel, left_side=False, lower=True, transpose_a=True
    )
    panel_cols = lax.linalg.triangular_solve(
        leading, natural_rows(top_cols).T, left_side=False, lower=True, transpose_a=True
    )
    trailing = schur_local - jnp.dot(panel_rows, panel_cols.T, precision=lax.Precision.HIGHEST)
    own_panel = lax.dynamic_index_in_dim(
        panel_rows.reshape(local_rows, K // (NB * pcol_count), pcol_count, NB),
        pcol_id,
        2,
        keepdims=False,
    )
    return (trailing, own_panel.reshape(local_rows, K // pcol_count))


def solution(mesh):
    in_specs = (P(None, ("prow", "pcol"), None), P(), P(), P())
    out_specs = (P("prow", "pcol"), P("prow", "pcol"))
    return jax.shard_map(
        per_device, mesh=mesh, in_specs=in_specs, out_specs=out_specs, check_vma=False
    )
```

profile of v0, /device:TPU:1, one launch (start us, length us, event | category | flops | bytes accessed | tf_op | source)
XLA Modules:
  0.0 744.1 jit_solution(3466437488755991065)
XLA Ops:
  14.9 80.7 %all-gather.6.cloned.1.call-done = bf16[4,4096,512]{2,1,0:T(8,128)(2,1)} async-done(((bf16[4,32,512]{2,1,0:T(8,128)(2,1)}), bf16[4,4096,512]{2,1,0:T(8,128)(2,1)}) %all-gather.6.cloned.1.call-update) | async-done | bytes 16777232 | tf_op jit(solution)/shard_map/all_gather | solution.py:67
  95.5 14.6 %fusion.113 = f32[128,16384]{1,0:T(8,128)} fusion(bf16[128,512]{1,0:T(8,128)(2,1)} %convolution_convert_fusion.1, bf16[16384,512]{1,0:T(8,128)(2,1)} %bitcast.189), kind=kOutput, calls=%fused_computation.289 | convolution fusion | flops 2147483648 | bytes 25296896 | tf_op jit(solution)/shard_map/dot_general | solution.py:27
  110.1 68.9 %all-gather.8.cloned.1.call-done = bf16[4,4096,512]{2,1,0:T(8,128)(2,1)} async-done(((bf16[4,32,512]{2,1,0:T(8,128)(2,1)}), bf16[4,4096,512]{2,1,0:T(8,128)(2,1)}) %all-gather.8.cloned.1.call-update) | async-done | bytes 16777232 | tf_op jit(solution)/shard_map/all_gather | solution.py:68
  179.0 12.9 %convolution_multiply_fusion = f32[128,16384]{1,0:T(8,128)} fusion(f32[128,16384]{1,0:T(8,128)} %fusion.113, bf16[128,512]{1,0:T(8,128)(2,1)S(1)} %copy-done.4, bf16[16384,512]{1,0:T(8,128)(2,1)} %bitcast.187), kind=kOutput, calls=%fused_computation.7 | convolution fusion | flops 2149580800 | bytes 33685504 | tf_op jit(solution)/shard_map/dot_general | solution.py:33
  191.9 10.8 %reshape.351 = f32[4,32,4,4096]{3,2,1,0:T(4,128)} reshape(f32[128,16384]{1,0:T(8,128)} %convolution_multiply_fusion) | data formatting | bytes 16777216 | tf_op jit(solution)/shard_map/reshape | solution.py:39
  202.7 6.4 multiply_reduce_fusion
  209.8 12.2 %scatter_custom_fusion = f32[32,4096]{0,1:T(8,128)} fusion(s32[4096]{0:T(1024)S(1)} %get-tuple-element.100, f32[32,4096]{0,1:T(8,128)S(1)} %copy.66, f32[]{:T(128)} %constant.382.clone.1), kind=kCustom, calls=%fused_computation.13 | custom fusion | bytes 2621444 | tf_op jit(solution)/shard_map/scatter | solution.py:63
  222.0 4.7 convolution_bitcast_fusion
  230.2 7.4 all-to-all-start
  237.7 15.5 %scatter_custom_fusion.1 = s32[4096]{0:T(1024)S(1)} fusion(s32[4096]{0:T(1024)S(1)} %get-tuple-element.100, s32[4096]{0:T(1024)S(1)} %iota.176, s32[]{:T(128)} %copy.145), kind=kCustom, calls=%fused_computation.235 | custom fusion | bytes 16388 | tf_op jit(solution)/shard_map/scatter | solution.py:56
  253.8 3.1 gather_fusion
  257.0 3.1 gather_fusion.1
  263.4 44.1 %all-gather.10.cloned.1.call-done = f32[512,1024]{0,1:T(8,128)} async-done(((f32[512,64]{0,1:T(8,128)}), f32[512,1024]{0,1:T(8,128)}) %all-gather.10.cloned.1.call-update) | async-done | bytes 2097168 | tf_op jit(solution)/shard_map/all_gather | solution.py:105
  309.6 24.3 %all-gather.14.cloned.1.call-done = f32[1024,256]{1,0:T(8,128)} async-done(((f32[128,256]{1,0:T(8,128)}), f32[1024,256]{1,0:T(8,128)}) %all-gather.14.cloned.1.call-update) | async-done | bytes 1048592 | tf_op jit(solution)/shard_map/all_gather | solution.py:114
  340.8 27.4 %all-gather.12.cloned.1.call-done = f32[1024,1024]{1,0:T(8,128)} async-done(((f32[128,1024]{1,0:T(8,128)}), f32[1024,1024]{1,0:T(8,128)}) %all-gather.12.cloned.1.call-update) | async-done | bytes 4194320 | tf_op jit(solution)/shard_map/all_gather | solution.py:113
  368.2 4.7 copy.50
  372.9 5.5 copy.51
  378.5 4.4 fusion
  384.9 11.7 %cholesky.223 = f32[128,128]{1,0:T(8,128)S(1)} custom-call(f32[128,128]{1,0:T(8,128)S(1)} %cholesky.580), custom_call_target="Cholesky" | custom-call | tf_op jit(solution)/shard_map/jit(cholesky)/cholesky | solution.py:124
  396.6 2.5 cholesky.255
  399.1 9.8 %custom-call.64 = f32[1,128,128]{1,2,0:T(8,128)S(1)} custom-call(f32[1,128,128]{2,1,0:T(8,128)S(1)} %get-tuple-element.98), custom_call_target="InvertDiagBlocksLowerTriangular" | custom-call | tf_op jit(solution)/shard_map/jit(cholesky)/cholesky | solution.py:124
  412.9 12.1 %cholesky.244 = f32[128,128]{1,0:T(8,128)S(1)} custom-call(f32[128,128]{1,0:T(8,128)S(1)} %cholesky.584), custom_call_target="Cholesky" | custom-call | tf_op jit(solution)/shard_map/jit(cholesky)/cholesky | solution.py:124
  426.9 9.8 %custom-call.65 = f32[1,128,128]{1,2,0:T(8,128)S(1)} custom-call(f32[1,128,128]{2,1,0:T(8,128)S(1)} %get-tuple-element.95), custom_call_target="InvertDiagBlocksLowerTriangular" | custom-call | tf_op jit(solution)/shard_map/jit(cholesky)/cholesky | solution.py:124
  440.0 11.7 %cholesky.468 = f32[128,128]{1,0:T(8,128)S(1)} custom-call(f32[128,128]{1,0:T(8,128)S(1)} %cholesky.589), custom_call_target="Cholesky" | custom-call | tf_op jit(solution)/shard_map/jit(cholesky)/cholesky | solution.py:124
  453.1 9.8 %custom-call.66 = f32[1,128,128]{1,2,0:T(8,128)S(1)} custom-call(f32[1,128,128]{2,1,0:T(8,128)S(1)} %get-tuple-element.92), custom_call_target="InvertDiagBlocksLowerTriangular" | custom-call | tf_op jit(solution)/shard_map/jit(cholesky)/cholesky | solution.py:124
  466.4 11.9 %cholesky.487 = f32[128,128]{1,0:T(8,128)S(1)} custom-call(f32[128,128]{1,0:T(8,128)S(1)} %cholesky.594), custom_call_target="Cholesky" | custom-call | tf_op jit(solution)/shard_map/jit(cholesky)/cholesky | solution.py:124
  479.6 9.8 %custom-call.67 = f32[1,128,128]{1,2,0:T(8,128)S(1)} custom-call(f32[1,128,128]{2,1,0:T(8,128)S(1)} %get-tuple-element.89), custom_call_target="InvertDiagBlocksLowerTriangular" | custom-call | tf_op jit(solution)/shard_map/jit(cholesky)/cholesky | solution.py:124
  492.9 11.7 %cholesky.506 = f32[128,128]{1,0:T(8,128)S(1)} custom-call(f32[128,128]{1,0:T(8,128)S(1)} %cholesky.599), custom_call_target="Cholesky" | custom-call | tf_op jit(solution)/shard_map/jit(cholesky)/cholesky | solution.py:124
  506.0 10.0 %custom-call.68 = f32[1,128,128]{1,2,0:T(8,128)S(1)} custom-call(f32[1,128,128]{2,1,0:T(8,128)S(1)} %get-tuple-element.86), custom_call_target="InvertDiagBlocksLowerTriangular" | custom-call | tf_op jit(solution)/shard_map/jit(cholesky)/cholesky | solution.py:124
  519.3 11.7 %cholesky.526 = f32[128,128]{1,0:T(8,128)S(1)} custom-call(f32[128,128]{1,0:T(8,128)S(1)} %cholesky.604), custom_call_target="Cholesky" | custom-call | tf_op jit(solution)/shard_map/jit(cholesky)/cholesky | solution.py:124
  532.3 9.8 %custom-call.69 = f32[1,128,128]{1,2,0:T(8,128)S(1)} custom-call(f32[1,128,128]{2,1,0:T(8,128)S(1)} %get-tuple-element.83), custom_call_target="InvertDiagBlocksLowerTriangular" | custom-call | tf_op jit(solution)/shard_map/jit(cholesky)/cholesky | solution.py:124
  545.1 12.1 %cholesky.546 = f32[128,128]{1,0:T(8,128)S(1)} custom-call(f32[128,128]{1,0:T(8,128)S(1)} %cholesky.609), custom_call_target="Cholesky" | custom-call | tf_op jit(solution)/shard_map/jit(cholesky)/cholesky | solution.py:124
  558.5 9.8 %custom-call.70 = f32[1,128,128]{1,2,0:T(8,128)S(1)} custom-call(f32[1,128,128]{2,1,0:T(8,128)S(1)} %get-tuple-element.80), custom_call_target="InvertDiagBlocksLowerTriangular" | custom-call | tf_op jit(solution)/shard_map/jit(cholesky)/cholesky | solution.py:124
  570.9 11.7 %cholesky.564 = f32[128,128]{1,0:T(8,128)S(1)} custom-call(f32[128,128]{1,0:T(8,128)S(1)} %convolution_subtract_fusion.21), custom_call_target="Cholesky" | custom-call | tf_op jit(solution)/shard_map/jit(cholesky)/cholesky | solution.py:124
  589.1 4.8 select_select_fusion
  593.9 28.0 %while.1 = (s32[]{:T(128)}, f32[1024,1024]{1,0:T(8,128)}, s32[8,2]{0,1:T(2,128)S(1)}, f32[8,128,128]{2,1,0:T(8,128)}, s32[]{:T(128)}) while((s32[]{:T(128)}, f32[1024,1024]{1,0:T(8,128)}, s32[8,2]{0,1:T(2,128)S(1)}, f32[8,128,128]{2,1,0:T(8,128)}, s32[]{:T(128)}) %tuple.90), condition=%wide.while_cond, body=%wide.while_body.sunk | while | flops 2 | bytes 132705 | solution.py:125
  594.5 2.9 bitcast_dynamic-update-slice_fusion.2
  598.0 2.9 bitcast_dynamic-update-slice_fusion.2
  601.5 2.9 bitcast_dynamic-update-slice_fusion.2
  605.0 2.9 bitcast_dynamic-update-slice_fusion.2
  608.6 2.9 bitcast_dynamic-update-slice_fusion.2
  612.1 2.9 bitcast_dynamic-update-slice_fusion.2
  615.6 2.9 bitcast_dynamic-update-slice_fusion.2
  619.1 2.8 bitcast_dynamic-update-slice_fusion.2
  621.9 79.6 %custom-call.71 = f32[8,128,128]{1,2,0:T(8,128)S(1)} custom-call(f32[8,128,128]{2,1,0:T(8,128)} %get-tuple-element.9), custom_call_target="InvertDiagBlocksLowerTriangular" | custom-call | tf_op jit(solution)/shard_map/triangular_solve | solution.py:125
  725.4 2.6 convolution_subtract_fusion.8
  728.4 3.1 convolution_subtract_fusion.4
  731.9 4.5 convolution_subtract_fusion
  (156 shorter events, 89.4 us)
Async XLA Ops:
  7.2 1.1 copy-start
  7.2 88.4 %all-gather.6.cloned.1.call-start = ((), (), s32[]{:S(2)}) async-start(), calls=%async_computation.1 | async-start | bytes 16908288 | tf_op jit(solution)/shard_map/all_gather | solution.py:67
  10.0 168.9 %all-gather.8.cloned.1.call-start = ((), (), s32[]{:S(2)}) async-start(), calls=%async_computation.2 | async-start | bytes 16908288 | tf_op jit(solution)/shard_map/all_gather | solution.py:68
  95.5 83.4 %copy-start.4 = (bf16[128,512]{1,0:T(8,128)(2,1)S(1)}, bf16[128,512]{1,0:T(8,128)(2,1)}, u32[]{:S(2)}) copy-start(bf16[128,512]{1,0:T(8,128)(2,1)} %convolution_convert_fusion) | copy-start | bytes 393220
  230.2 30.0 %all-to-all-start = ((f32[128,8,256]{2,1,0:T(8,128)}), f32[128,8,256]{2,1,0:T(8,128)S(1)}, u32[]{:S(2)}, u32[]{:S(2)}) async-start(f32[128,8,256]{2,1,0:T(8,128)} %reshape_reshape.3), calls=%async_computation | async-start | bytes 2097152 | tf_op jit(solution)/shard_map/all_to_all | solution.py:87
  237.6 69.8 %all-gather.10.cloned.1.call-start = ((), (), s32[]{:S(2)}) async-start(), calls=%async_computation.3 | async-start | bytes 2228224 | tf_op jit(solution)/shard_map/all_gather | solution.py:105
  262.6 71.2 %all-gather.14.cloned.1.call-start = ((), (), s32[]{:S(2)}) async-start(), calls=%async_computation.5 | async-start | bytes 1179648 | tf_op jit(solution)/shard_map/all_gather | solution.py:114
  263.3 104.9 %all-gather.12.cloned.1.call-start = ((), (), s32[]{:S(2)}) async-start(), calls=%async_computation.4 | async-start | bytes 4718592 | tf_op jit(solution)/shard_map/all_gather | solution.py:113
  382.9 1.9 copy-start.3
  701.5 6.0 copy-start.2
  708.5 7.1 copy-start.5
  710.1 6.6 copy-start.6
  715.7 4.7 copy-start.8
  722.2 6.2 copy-start.7
  728.0 9.1 %copy-start.1 = (bf16[512,512]{1,0:T(8,128)(2,1)S(1)}, bf16[512,512]{1,0:T(8,128)(2,1)}, u32[]{:S(2)}) copy-start(bf16[512,512]{1,0:T(8,128)(2,1)} %param.6) | copy-start | bytes 1572868
Sparse Core Ops, SparseCore 0:
  11.6 83.9 all-gather.5
  99.1 79.8 all-gather.7
  262.7 44.6 all-gather.9
  309.0 24.7 all-gather.13
  336.0 32.1 all-gather.11
where the time goes:
time: 754 us; the launch traced here: 744 us
  other arithmetic  272 us (36%)
  waiting for transfers between devices  245 us (32%)
  local copies, waits for them, and re-layouts  106 us (14%)
  matrix products  93.7 us (12%)
  between operations  20.1 us (3%)
  starting transfers between devices  7.58 us (1%)
    another operation x31, other arithmetic, per_device(): leading = jnp.linalg.cholesky(natural_rows(top_panel))  173 us
    another operation x3, other arithmetic, per_device(): lax.linalg.triangular_solve(leading, row_panel, left_side=False, lower=Tr...  84.4 us
    all_gather x1, waiting for transfers between devices, per_device(): lax.all_gather(own_x, ('prow', 'pcol'), axis=1, tiled=True)  80.7 us
    all_gather x1, waiting for transfers between devices, per_device(): lax.all_gather(own_z, ('prow', 'pcol'), axis=1, tiled=True)  68.9 us
    all_gather x1, waiting for transfers between devices, per_device(): row_panel = lax.all_gather(front_cols, 'pcol', axis=1, tiled=True)  44.1 us
    another operation x24, local copies, waits for them, and re-layouts  28 us
    all_gather x1, waiting for transfers between devices, per_device(): lax.all_gather(row_panel[:lead_rows], 'prow', axis=0, tiled=True)  27.4 us
    all_gather x1, waiting for transfers between devices, per_device(): lax.all_gather(schur_local[:lead_rows], 'prow', axis=0, tiled=True)  24.3 us
  transfers between devices with their start and end apart: 6, of which 5 were waited for; matrix products, arithmetic and copies ran while one was open for 7% of the time, Pallas kernels for 0%

commit v1 on v0

v1 whole, which is shorter than its diff:
```python
import functools
import jax
import jax.numpy as jnp
from jax import lax
from jax.experimental import pallas as pl
from jax.experimental.pallas import tpu as pltpu
from jax.sharding import PartitionSpec as P

RANK = 4
NB = 64
KK = 1024
F32, BF16 = jnp.float32, jnp.bfloat16
SIGNS = (1.0, 1.0, -1.0, -1.0)
TN = (((1,), (1,)), ((), ()))


def split(v):
    hi = v.astype(BF16)
    return hi, (v - hi.astype(F32)).astype(BF16)


def spread(v):
    return jnp.broadcast_to(v, (8, 128))


def invert_block(block_ref, inv_ref):
    lane = lax.broadcasted_iota(jnp.int32, (8, 128), 1)
    sub = lax.broadcasted_iota(jnp.int32, (8, 128), 0)
    rows = [block_ref[8 * i:8 * i + 8, :] for i in range(16)]
    aug = [(lane == sub + 8 * i).astype(F32) for i in range(16)]
    for j in range(16):
        mine, extra = rows[j], aug[j]
        cols = [spread(mine[:, 8 * j + q:8 * j + q + 1]) for q in range(8)]
        a = [[None] * 8 for _ in range(8)]
        for q in range(8):
            for s in range(q, 8):
                a[s][q] = spread(cols[q][s:s + 1, :])
        r = [spread(mine[t:t + 1, :]) for t in range(8)] if j < 15 else None
        e = [spread(extra[t:t + 1, :]) for t in range(8)]
        rinv = [None] * 8
        low = [[None] * 8 for _ in range(8)]
        for t in range(8):
            rinv[t] = 1.0 / a[t][t]
            for s in range(t + 1, 8):
                low[s][t] = a[s][t] * rinv[t]
            for s in range(t + 1, 8):
                for k in range(t + 1, s + 1):
                    a[s][k] = a[s][k] - low[s][t] * a[k][t]
            for s in range(t + 1, 8):
                if r is not None:
                    r[s] = r[s] - low[s][t] * r[t]
                e[s] = e[s] - low[s][t] * e[t]
        packed_d = a[0][0]
        packed_e = e[0]
        for t in range(1, 8):
            packed_d = jnp.where(sub == t, a[t][t], packed_d)
            packed_e = jnp.where(sub == t, e[t], packed_e)
        inv_ref[8 * j:8 * j + 8, :] = packed_e * lax.rsqrt(packed_d)
        if j == 15:
            break
        w = [r[t] * rinv[t] for t in range(8)]
        we = [e[t] * rinv[t] for t in range(8)]
        for s in range(7, 0, -1):
            for t in range(s):
                w[t] = w[t] - low[s][t] * w[s]
                we[t] = we[t] - low[s][t] * we[s]
        for i in range(j + 1, 16):
            c = [spread(rows[i][:, 8 * j + q:8 * j + q + 1]) for q in range(8)]
            acc = c[0] * w[0]
            acce = c[0] * we[0]
            for q in range(1, 8):
                acc = acc + c[q] * w[q]
                acce = acce + c[q] * we[q]
            rows[i] = rows[i] - acc
            aug[i] = aug[i] - acce


def chol_kernel(lead_ref, rest_ref, out_ref, a_ref, diag_ref, inv_ref, icat_ref, pcat_ref, qcat_ref):
    n = KK // 128
    total = (KK + rest_ref.shape[0]) // 256
    a_ref[:KK, :] = lead_ref[...]
    a_ref[KK:, :] = rest_ref[...]

    def step(j, carry):
        off = pl.multiple_of(j * 128, 128)
        diag_ref[...] = a_ref[pl.ds(off, 128), pl.ds(off, 128)]
        invert_block(diag_ref, inv_ref)
        hi, lo = split(inv_ref[...])
        icat_ref[:, 0:128] = hi
        icat_ref[:, 128:256] = hi
        icat_ref[:, 256:384] = lo
        first = (j + 1) // 2

        def panel(r, c):
            base = pl.multiple_of(r * 256, 256)
            hi, lo = split(a_ref[pl.ds(base, 256), pl.ds(off, 128)])
            v = lax.dot_general(jnp.concatenate([hi, lo, hi], axis=1), icat_ref[...], TN, preferred_element_type=F32)
            hi, lo = split(v)
            pcat_ref[pl.ds(base, 256), 0:128] = hi
            pcat_ref[pl.ds(base, 256), 128:256] = lo
            pcat_ref[pl.ds(base, 256), 256:384] = hi

            @pl.when(r < KK // 256)
            def _():
                qcat_ref[pl.ds(base, 256), 0:128] = hi
                qcat_ref[pl.ds(base, 256), 128:256] = hi
                qcat_ref[pl.ds(base, 256), 256:384] = lo

            @pl.when(r >= KK // 256)
            def _():
                out_ref[pl.ds(base - KK, 256), pl.ds(off, 128)] = v
            return c
        lax.fori_loop(first, total, panel, 0)

        def update(r, c):
            base = pl.multiple_of(r * 256, 256)

            def inner(k, c):
                cb = pl.multiple_of(k * 256, 256)
                a_ref[pl.ds(base, 256), pl.ds(cb, 256)] -= lax.dot_general(
                    pcat_ref[pl.ds(base, 256), :], qcat_ref[pl.ds(cb, 256), :], TN, preferred_element_type=F32)
                return c
            return lax.fori_loop(first, jnp.minimum(r + 1, KK // 256), inner, c)
        lax.fori_loop(first, total, update, 0)
        return carry
    lax.fori_loop(0, n, step, 0)


def chol_panels(lead, rest):
    m = rest.shape[0]
    return pl.pallas_call(
        chol_kernel,
        out_shape=jax.ShapeDtypeStruct((m, KK), F32),
        in_specs=[pl.BlockSpec(memory_space=pltpu.VMEM)] * 2,
        out_specs=pl.BlockSpec(memory_space=pltpu.VMEM),
        scratch_shapes=[
            pltpu.VMEM((KK + m, KK), F32),
            pltpu.VMEM((128, 128), F32),
            pltpu.VMEM((128, 128), F32),
            pltpu.VMEM((128, 384), BF16),
            pltpu.VMEM((KK + m, 384), BF16),
            pltpu.VMEM((KK, 384), BF16),
        ],
        compiler_params=pltpu.CompilerParams(vmem_limit_bytes=48 << 20),
        name="panels",
    )(lead, rest)


def pair_kernel(rows_ref, cols_ref, x_ref, z_ref, out_ref, rx_ref, rz_ref, cx_ref, cz_ref):
    depth = x_ref.shape[0]
    count = rows_ref.shape[1]
    for src, mat, dst in ((cols_ref, x_ref, cx_ref), (cols_ref, z_ref, cz_ref), (rows_ref, x_ref, rx_ref), (rows_ref, z_ref, rz_ref)):
        for r in range(RANK):
            dst[r] = jnp.dot(src[r], mat[...], preferred_element_type=F32).astype(BF16)

    def chunk(i, carry):
        base = pl.multiple_of(i * 128, 128)
        acc = None
        for r in range(RANK):
            for q in range(RANK):
                inner_x = lax.dot_general(rx_ref[r, pl.ds(base, 128), :], cx_ref[q], TN, preferred_element_type=F32)
                inner_z = lax.dot_general(rz_ref[r, pl.ds(base, 128), :], cz_ref[q], TN, preferred_element_type=F32)
                term = inner_x * inner_z
                if acc is None:
                    acc = term
                elif SIGNS[r] * SIGNS[q] > 0:
                    acc = acc + term
                else:
                    acc = acc - term
        out_ref[pl.ds(base, 128), :] = acc
        return carry
    lax.fori_loop(0, count // 128, chunk, 0)


def pair_block(rows, cols, x_factor, z_factor):
    m, n, d = rows.shape[1], cols.shape[1], rows.shape[2]
    return pl.pallas_call(
        pair_kernel,
        out_shape=jax.ShapeDtypeStruct((m, n), F32),
        in_specs=[pl.BlockSpec(memory_space=pltpu.VMEM)] * 4,
        out_specs=pl.BlockSpec(memory_space=pltpu.VMEM),
        scratch_shapes=[pltpu.VMEM((RANK, m, d), BF16)] * 2 + [pltpu.VMEM((RANK, n, d), BF16)] * 2,
        compiler_params=pltpu.CompilerParams(vmem_limit_bytes=48 << 20),
        name="pairs",
    )(rows, cols, x_factor, z_factor)


def per_device(factors, x_factor, zinv_factor, placement):
    prow_count = lax.axis_size("prow")
    pcol_count = lax.axis_size("pcol")
    total_rows = placement.shape[0]
    local_rows = total_rows // prow_count
    local_cols = total_rows // pcol_count
    prow_id = lax.axis_index("prow")
    pcol_id = lax.axis_index("pcol")
    inverse = jnp.zeros((total_rows,), jnp.int32).at[placement].set(jnp.arange(total_rows, dtype=jnp.int32))

    def natural(length, groups, which):
        k = jnp.arange(length)
        return k // NB * NB * groups + which * NB + k % NB
    everything = lax.all_gather(factors, ("prow", "pcol"), axis=1, tiled=True)
    rows = everything[:, inverse[natural(local_rows, prow_count, prow_id)]]
    cols = everything[:, inverse[natural(local_cols, pcol_count, pcol_id)]]
    schur_local = pair_block(rows, cols, x_factor, zinv_factor)
    lead_cols = KK // pcol_count
    front_cols = schur_local[:, :lead_cols]
    row_panel = lax.all_gather(front_cols, "pcol", axis=1, tiled=True)
    lead_rows = KK // prow_count
    top_panel = lax.all_gather(row_panel[:lead_rows], "prow", axis=0, tiled=True)
    top_cols = lax.all_gather(schur_local[:lead_rows], "prow", axis=0, tiled=True)

    def natural_rows(stacked):
        return (
            stacked.reshape(prow_count, lead_rows // NB, NB, stacked.shape[1])
            .transpose(1, 0, 2, 3)
            .reshape(KK, stacked.shape[1])
        )
    lead = natural_rows(top_panel)
    rest = jnp.concatenate([row_panel, natural_rows(top_cols).T], axis=0)
    solved = chol_panels(lead, rest)
    panel_rows, panel_cols = solved[:local_rows], solved[local_rows:]
    trailing = schur_local - jnp.dot(panel_rows, panel_cols.T, precision=lax.Precision.HIGHEST)
    own_panel = lax.dynamic_index_in_dim(panel_rows.reshape(local_rows, pcol_count, NB), pcol_id, 1, keepdims=False)
    return (trailing, own_panel)


def solution(mesh):
    in_specs = (P(None, ("prow", "pcol"), None), P(), P(), P())
    out_specs = (P("prow", "pcol"), P("prow", "pcol"))
    return jax.shard_map(per_device, mesh=mesh, in_specs=in_specs, out_specs=out_specs, check_vma=False)
```

time: 754 us -> 325 us (0.43); the launches traced: 744 us -> 325 us
  other arithmetic: 272 us -> 4.05 us
  matrix products: 93.7 us -> 2.63 us
  waiting for transfers between devices: 245 us -> 157 us
  Pallas kernels: 0 us -> 85.5 us
  local copies, waits for them, and re-layouts: 106 us -> 61.7 us
    another operation x35 -> x0, other arithmetic: 258 us -> none  [the longest x31 173 us: per_device(): leading = jnp.linalg.cholesky(natural_rows(top_panel))]
    pallas_call x0 -> x2, Pallas kernels: none -> 85.5 us  [the longest x1 70.8 us: chol_panels(): pl.pallas_call(chol_kernel, out_shape=jax.ShapeDtypeStruct((m, KK), F32),...]
    all_gather x2 -> x1, waiting for transfers between devices: 150 us -> 65.1 us  [per_device(): everything = lax.all_gather(factors, ('prow', 'pcol'), axis=1, tiled=True)]
    another operation x44 -> x0, matrix products: 53.2 us -> none  [the longest x14 23.1 us: per_device(): leading = jnp.linalg.cholesky(natural_rows(top_panel))]
    dot_general x5 -> x0, matrix products: 36 us -> none  [the longest x1 14.6 us: pair_terms(): lax.dot_general(left_x.reshape(RANK * span_rows, width), right_x.reshape(...]
    another operation x35 -> x0, local copies, waits for them, and re-layouts: 34.2 us -> none
    gather x3 -> x6, local copies, waits for them, and re-layouts: 7.86 us -> 26.1 us  [the longest x3 14.7 us: per_device(): rows = everything[:, inverse[natural(local_rows, prow_count, prow_id)]]]
    scatter x2 -> x1, local copies, waits for them, and re-layouts: 27.8 us -> 15.5 us  [per_device(): jnp.zeros((total_rows,), jnp.int32).at[placement]]
  transfers between devices with their start and end apart: 6 -> 4, of which waited for: 5 -> 4; matrix products, arithmetic and copies ran while one was open for 7% -> 10% of each run, Pallas kernels for 0% -> 0%
where the time goes in v1:
time: 325 us
  waiting for transfers between devices  157 us (48%)
  Pallas kernels  85.5 us (26%)
  local copies, waits for them, and re-layouts  61.7 us (19%)
  between operations  13.9 us (4%)
  other arithmetic  4.05 us (1%)
    pallas_call x1, Pallas kernels, chol_panels(): pl.pallas_call(chol_kernel, out_shape=jax.ShapeDtypeStruct((m, KK), F32),...  70.8 us
    all_gather x1, waiting for transfers between devices, per_device(): everything = lax.all_gather(factors, ('prow', 'pcol'), axis=1, tiled=True)  65.1 us
    all_gather x1, waiting for transfers between devices, per_device(): row_panel = lax.all_gather(front_cols, 'pcol', axis=1, tiled=True)  41.5 us
    all_gather x1, waiting for transfers between devices, per_device(): lax.all_gather(row_panel[:lead_rows], 'prow', axis=0, tiled=True)  26.3 us
    all_gather x1, waiting for transfers between devices, per_device(): lax.all_gather(schur_local[:lead_rows], 'prow', axis=0, tiled=True)  23.8 us
    scatter x1, local copies, waits for them, and re-layouts, per_device(): jnp.zeros((total_rows,), jnp.int32).at[placement]  15.5 us
    gather x3, local copies, waits for them, and re-layouts, per_device(): rows = everything[:, inverse[natural(local_rows, prow_count, prow_id)]]  14.7 us
    pallas_call x1, Pallas kernels, pair_block(): pl.pallas_call(pair_kernel, out_shape=jax.ShapeDtypeStruct((m, n), F32),...  14.7 us
  transfers between devices with their start and end apart: 4, of which 4 were waited for; matrix products, arithmetic and copies ran while one was open for 10% of the time, Pallas kernels for 0%

profile of v1, /device:TPU:1, one launch (start us, length us, event | category | flops | bytes accessed | tf_op | source)
XLA Modules:
  0.0 324.8 jit_solution(15755474601425635333)
XLA Ops:
  7.2 0.0 all-gather.5.cloned.1.call-start
  7.2 1.7 copy.25
  8.9 0.0 all-gather.5.cloned.1.call-update
  8.9 0.0 all-gather.7.cloned.1.call-start
  9.0 0.7 compare_select_fusion
  9.7 15.5 %scatter_custom_fusion = s32[4096]{0:T(1024)S(1)} fusion(s32[4096]{0:T(1024)S(1)} %compare_select_fusion, s32[4096]{0:T(1024)S(1)} %iota.15, s32[]{:T(128)} %constant.67.clone.1), kind=kCustom, calls=%fused_computation.14 | custom fusion | bytes 16388 | tf_op jit(solution)/shard_map/scatter | solution.py:196
  25.2 1.7 gather_fusion.2
  27.0 3.1 gather_fusion
  30.2 65.1 %all-gather.5.cloned.1.call-done = bf16[4,4096,512]{2,0,1:T(4,128)(2,1)} async-done(((bf16[4,32,512]{2,0,1:T(4,128)(2,1)}), bf16[4,4096,512]{2,0,1:T(4,128)(2,1)}) %all-gather.5.cloned.1.call-update) | async-done | bytes 16777232 | tf_op jit(solution)/shard_map/all_gather | solution.py:201
  95.3 9.6 %gather_fusion.1 = bf16[512,4,512]{2,1,0:T(4,128)(2,1)} fusion(bf16[4,4096,512]{2,0,1:T(4,128)(2,1)} %all-gather.5.cloned.1.call-done, s32[1024]{0:T(1024)S(1)} %pad_clamp_fusion.2), kind=kCustom, calls=%fused_computation.1 | custom fusion | bytes 4196352 | tf_op jit(solution)/shard_map/gather | solution.py:202
  104.9 2.0 copy.37
  106.9 0.0 copy-start
  106.9 8.3 %gather_fusion.3 = bf16[256,4,512]{2,1,0:T(4,128)(2,1)} fusion(bf16[4,4096,512]{2,0,1:T(4,128)(2,1)} %all-gather.5.cloned.1.call-done, s32[1024]{0:T(1024)S(1)} %pad_clamp_fusion), kind=kCustom, calls=%fused_computation.3 | custom fusion | bytes 2098176 | tf_op jit(solution)/shard_map/gather | solution.py:203
  115.1 1.4 copy.38
  116.6 0.0 copy-done
  116.6 0.0 copy-start.1
  116.6 1.0 copy-done.1
  117.6 14.7 %pairs.1 = f32[512,256]{1,0:T(8,128)S(1)} custom-call(bf16[4,512,512]{2,1,0:T(8,128)(2,1)S(1)} %bitcast.25, bf16[4,256,512]{2,1,0:T(8,128)(2,1)S(1)} %bitcast.26, bf16[512,512]{1,0:T(8,128)(2,1)S(1)} %copy-done, bf16[512,512]{1,0:T(8,128)(2,1)S(1)} %copy-done.1), custom_call_target="tpu_custom_call" | custom-call | tf_op jit(solution)/shard_map/pairs/pallas_call | solution.py:177
  132.4 0.8 copy.28
  133.2 0.0 all-gather.7.cloned.1.call-update
  133.2 0.0 all-gather.11.cloned.1.call-start
  133.2 0.7 slice.30
  133.9 0.0 all-gather.11.cloned.1.call-update
  133.9 0.2 all-gather.9.cloned.1.call-start
  134.1 41.5 %all-gather.7.cloned.1.call-done = f32[512,1024]{0,1:T(8,128)} async-done(((f32[512,64]{0,1:T(8,128)}), f32[512,1024]{0,1:T(8,128)}) %all-gather.7.cloned.1.call-update) | async-done | bytes 2097168 | tf_op jit(solution)/shard_map/all_gather | solution.py:207
  175.6 1.9 copy.29
  177.5 0.8 slice.29
  178.4 0.0 all-gather.9.cloned.1.call-update
  178.4 23.8 %all-gather.11.cloned.1.call-done = f32[1024,256]{1,0:T(8,128)} async-done(((f32[128,256]{1,0:T(8,128)}), f32[1024,256]{1,0:T(8,128)}) %all-gather.11.cloned.1.call-update) | async-done | bytes 1048592 | tf_op jit(solution)/shard_map/all_gather | solution.py:210
  202.2 2.3 copy.31
  204.5 2.5 copy.32
  207.0 3.3 %pad_maximum_fusion.rest_ref = f32[768,1024]{1,0:T(8,128)} fusion(f32[256,1024]{1,0:T(8,128)} %bitcast.30, f32[512,1024]{1,0:T(8,128)S(1)} %copy.29), kind=kLoop, calls=%fused_computation.5 | loop fusion | flops 786432 | bytes 6291456 | tf_op jit(solution)/shard_map/concatenate | solution.py:219
  210.3 26.3 %all-gather.9.cloned.1.call-done = f32[1024,1024]{1,0:T(8,128)} async-done(((f32[128,1024]{1,0:T(8,128)}), f32[1024,1024]{1,0:T(8,128)}) %all-gather.9.cloned.1.call-update) | async-done | bytes 4194320 | tf_op jit(solution)/shard_map/all_gather | solution.py:209
  236.5 4.7 %copy.30 = f32[2,8,64,1024]{3,2,1,0:T(8,128)} copy(f32[2,8,64,1024]{3,2,0,1:T(8,128)} %bitcast.28) | data formatting | bytes 8388608 | tf_op jit(solution)/shard_map/transpose | solution.py:215
  241.3 70.8 %panels.1 = f32[768,1024]{1,0:T(8,128)S(1)} custom-call(f32[1024,1024]{1,0:T(8,128)} %bitcast.27, f32[768,1024]{1,0:T(8,128)} %pad_maximum_fusion.rest_ref), custom_call_target="tpu_custom_call" | custom-call | tf_op jit(solution)/shard_map/panels/pallas_call | solution.py:131
  312.0 2.6 convolution_subtract_fusion
  314.7 0.1 slice.31
  314.8 1.8 copy.34
  316.7 1.6 dynamic-slice_bitcast_fusion
  (10 shorter events, 0.1 us)
Async XLA Ops:
  7.2 88.1 %all-gather.5.cloned.1.call-start = ((), (), s32[]{:S(2)}) async-start(), calls=%async_computation | async-start | bytes 16908288 | tf_op jit(solution)/shard_map/all_gather | solution.py:201
  8.9 166.7 %all-gather.7.cloned.1.call-start = ((), (), s32[]{:S(2)}) async-start(), calls=%async_computation.1 | async-start | bytes 2228224 | tf_op jit(solution)/shard_map/all_gather | solution.py:207
  106.9 9.7 %copy-start = (bf16[512,512]{1,0:T(8,128)(2,1)S(1)}, bf16[512,512]{1,0:T(8,128)(2,1)}, u32[]{:S(2)}) copy-start(bf16[512,512]{1,0:T(8,128)(2,1)} %x_ref.1) | copy-start | bytes 1572868
  116.6 1.0 copy-start.1
  133.2 69.0 %all-gather.11.cloned.1.call-start = ((), (), s32[]{:S(2)}) async-start(), calls=%async_computation.3 | async-start | bytes 1179648 | tf_op jit(solution)/shard_map/all_gather | solution.py:210
  133.9 102.6 %all-gather.9.cloned.1.call-start = ((), (), s32[]{:S(2)}) async-start(), calls=%async_computation.2 | async-start | bytes 4718592 | tf_op jit(solution)/shard_map/all_gather | solution.py:209
Sparse Core Ops, SparseCore 0:
  11.7 83.5 all-gather.4
  133.3 42.2 all-gather.6
  177.3 24.7 all-gather.10
  204.3 32.1 all-gather.8

commit v2 on v1

v2 whole, which is shorter than its diff:
```python
import functools
import jax
import jax.numpy as jnp
from jax import lax
from jax.experimental import pallas as pl
from jax.experimental.pallas import tpu as pltpu
from jax.sharding import PartitionSpec as P

RANK = 4
NB = 64
KK = 1024
F32, BF16 = jnp.float32, jnp.bfloat16
SIGNS = (1.0, 1.0, -1.0, -1.0)
MESH = pl.DeviceIdType.MESH
TN = (((1,), (1,)), ((), ()))
NN = (((1,), (0,)), ((), ()))
TT = (((0,), (0,)), ((), ()))


def split(v):
    hi = v.astype(BF16)
    return hi, (v - hi.astype(F32)).astype(BF16)


def spread(v):
    return jnp.broadcast_to(v, (8, 128))


def invert_block(block_ref, inv_ref):
    lane = lax.broadcasted_iota(jnp.int32, (8, 128), 1)
    sub = lax.broadcasted_iota(jnp.int32, (8, 128), 0)
    rows = [block_ref[8 * i:8 * i + 8, :] for i in range(16)]
    aug = [(lane == sub + 8 * i).astype(F32) for i in range(16)]
    for j in range(16):
        mine, extra = rows[j], aug[j]
        cols = [spread(mine[:, 8 * j + q:8 * j + q + 1]) for q in range(8)]
        a = [[None] * 8 for _ in range(8)]
        for q in range(8):
            for s in range(q, 8):
                a[s][q] = spread(cols[q][s:s + 1, :])
        r = [spread(mine[t:t + 1, :]) for t in range(8)] if j < 15 else None
        e = [spread(extra[t:t + 1, :]) for t in range(8)]
        rinv = [None] * 8
        low = [[None] * 8 for _ in range(8)]
        for t in range(8):
            rinv[t] = 1.0 / a[t][t]
            for s in range(t + 1, 8):
                low[s][t] = a[s][t] * rinv[t]
            for s in range(t + 1, 8):
                for k in range(t + 1, s + 1):
                    a[s][k] = a[s][k] - low[s][t] * a[k][t]
            for s in range(t + 1, 8):
                if r is not None:
                    r[s] = r[s] - low[s][t] * r[t]
                e[s] = e[s] - low[s][t] * e[t]
        packed_d = a[0][0]
        packed_e = e[0]
        for t in range(1, 8):
            packed_d = jnp.where(sub == t, a[t][t], packed_d)
            packed_e = jnp.where(sub == t, e[t], packed_e)
        inv_ref[8 * j:8 * j + 8, :] = packed_e * lax.rsqrt(packed_d)
        if j == 15:
            break
        w = [r[t] * rinv[t] for t in range(8)]
        we = [e[t] * rinv[t] for t in range(8)]
        for s in range(7, 0, -1):
            for t in range(s):
                w[t] = w[t] - low[s][t] * w[s]
                we[t] = we[t] - low[s][t] * we[s]
        for i in range(j + 1, 16):
            c = [spread(rows[i][:, 8 * j + q:8 * j + q + 1]) for q in range(8)]
            acc = c[0] * w[0]
            acce = c[0] * we[0]
            for q in range(1, 8):
                acc = acc + c[q] * w[q]
                acce = acce + c[q] * we[q]
            rows[i] = rows[i] - acc
            aug[i] = aug[i] - acce


ORDERS = ((0, 1, 2), (1, 2, 0), (2, 0, 1))


def gather_kernel(colors, in_ref, out_ref, own_sem, send, recv, psend, precv):
    prow, pcol = lax.axis_index("prow"), lax.axis_index("pcol")
    me = (pcol // 4, pcol % 4, prow // 2)
    core = prow % 2

    def device(dim, shift):
        at = [lax.rem(v + shift + 4, 4) if d == dim else v for d, v in enumerate(me)]
        return (at[2] * 2 + core, at[0] * 4 + at[1])
    partner = (me[2] * 2 + 1 - core, pcol)
    barrier = pltpu.get_barrier_semaphore()
    for dim in range(3):
        for shift in (1, -1):
            pl.semaphore_signal(barrier, inc=1, device_id=device(dim, shift), device_id_type=MESH)
    pl.semaphore_signal(barrier, inc=1, device_id=partner, device_id_type=MESH)
    own = pltpu.make_async_copy(in_ref, out_ref.at[me[0], me[1], me[2], core], own_sem)
    own.start()
    pl.semaphore_wait(barrier, 7)

    def view(c, phase, shift, half, whose=core):
        order = ORDERS[c]
        (r0, rm, r1), (c0, c1) = colors[c]
        at = list(me)
        for j in range(phase):
            at[order[j]] = slice(None)
        at[order[phase]] = lax.rem(me[order[phase]] + shift + 4, 4)
        rows = {0: (r0, rm), 1: (rm, r1), 2: (r0, r1)}[half]
        return out_ref.at[at[0], at[1], at[2], whose, pl.ds(rows[0], rows[1] - rows[0]), pl.ds(c0, c1 - c0)]

    def ring(c, phase, which):
        dim = ORDERS[c][phase]
        shift, half, to = ((0, 2, 1), (0, 2, -1), (-1, 0, 1), (1, 1, -1))[which]
        src = view(c, phase, shift, half)
        dst = src
        if phase == 0 and which < 2:
            (r0, rm, r1), (c0, c1) = colors[c]
            src = in_ref.at[pl.ds(r0, r1 - r0), pl.ds(c0, c1 - c0)]
        n = (c * 3 + phase) * 4 + which
        return pltpu.make_async_remote_copy(src, dst, send.at[n], recv.at[n], device_id=device(dim, to), device_id_type=MESH)

    def landed(c, phase, which):
        dim = ORDERS[c][phase]
        shift, half = ((-1, 2), (1, 2), (2, 0), (2, 1))[which]
        got = view(c, phase, shift, half)
        n = (c * 3 + phase) * 4 + which
        pltpu.make_async_remote_copy(got, got, send.at[n], recv.at[n], device_id=device(dim, 1), device_id_type=MESH).wait_recv()

    def across(c, which, whose):
        shift, half = ((0, 2), (-1, 2), (1, 2), (2, 0), (2, 1))[which]
        part = view(c, 2, shift, half, whose)
        n = c * 5 + which
        return pltpu.make_async_remote_copy(part, part, psend.at[n], precv.at[n], device_id=partner, device_id_type=MESH)

    for c in range(3):
        ring(c, 0, 0).start()
        ring(c, 0, 1).start()
    for phase in range(3):
        for c in range(3):
            landed(c, phase, 0)
            ring(c, phase, 2).start()
            if phase == 2:
                across(c, 1, core).start()
            landed(c, phase, 1)
            ring(c, phase, 3).start()
            if phase == 2:
                across(c, 2, core).start()
        if phase == 0:
            own.wait()
        for c in range(3):
            landed(c, phase, 2)
            if phase == 2:
                across(c, 3, core).start()
            landed(c, phase, 3)
            if phase == 2:
                across(c, 4, core).start()
            else:
                ring(c, phase + 1, 0).start()
                ring(c, phase + 1, 1).start()
                if phase == 1:
                    across(c, 0, core).start()
    for c in range(3):
        for which in range(5):
            across(c, which, core).wait_send()
            across(c, which, 1 - core).wait_recv()
        for phase in range(3):
            for which in range(4):
                ring(c, phase, which).wait_send()


def gather_all(block, colors, ident):
    return pl.pallas_call(
        functools.partial(gather_kernel, colors),
        out_shape=jax.ShapeDtypeStruct((4, 4, 4, 2) + block.shape, block.dtype),
        in_specs=[pl.BlockSpec(memory_space=pltpu.VMEM)],
        out_specs=pl.BlockSpec(memory_space=pl.ANY),
        scratch_shapes=[
            pltpu.SemaphoreType.DMA,
            pltpu.SemaphoreType.DMA((36,)),
            pltpu.SemaphoreType.DMA((36,)),
            pltpu.SemaphoreType.DMA((15,)),
            pltpu.SemaphoreType.DMA((15,)),
        ],
        compiler_params=pltpu.CompilerParams(collective_id=ident, has_side_effects=True),
        name="gather_all_%d" % ident,
    )(block)


F_COLORS = (((0, 16, 32), (0, 640)), ((0, 16, 32), (640, 1280)), ((0, 16, 32), (1280, 2048)))
S_COLORS = (((0, 16, 24), (0, 128)), ((24, 32, 48), (0, 128)), ((48, 56, 64), (0, 128)))


def factor_kernel(tiles_ref, front_ref, top_ref, rest_ref, inv_hi_ref, inv_lo_ref, low_hi_ref, low_lo_ref,
                  a_ref, diag_ref, inv_ref, pcat_ref, qcat_ref, icat_ref, own_sem, send, recv):
    prow, pcol = lax.axis_index("prow"), lax.axis_index("pcol")
    barrier = pltpu.get_barrier_semaphore()
    for s in range(1, 16):
        pl.semaphore_signal(barrier, inc=1, device_id=(prow, lax.rem(pcol + s, 16)), device_id_type=MESH)
    for s in range(1, 8):
        pl.semaphore_signal(barrier, inc=1, device_id=(lax.rem(prow + s, 8), pcol), device_id_type=MESH)
    pl.semaphore_wait(barrier, 22)

    def front_place(c):
        return rest_ref.at[pl.ds(pl.multiple_of(c * NB, NB), NB), pl.ds(0, 512)]

    def top_place(p, h):
        return rest_ref.at[pl.ds(pl.multiple_of(h * 512 + p * NB, NB), NB), pl.ds(512, 256)]

    def front_copy(s):
        return pltpu.make_async_remote_copy(
            front_ref, front_place(pcol), send.at[s - 1], recv.at[s - 1],
            device_id=(prow, lax.rem(pcol + s, 16)), device_id_type=MESH)

    def top_copy(s, h):
        n = 15 + (s - 1) * 2 + h
        return pltpu.make_async_remote_copy(
            top_ref.at[pl.ds(h * NB, NB)], top_place(prow, h), send.at[n], recv.at[n],
            device_id=(lax.rem(prow + s, 8), pcol), device_id_type=MESH)
    own = [pltpu.make_async_copy(front_ref, front_place(pcol), own_sem.at[0])]
    for h in range(2):
        own.append(pltpu.make_async_copy(top_ref.at[pl.ds(h * NB, NB)], top_place(prow, h), own_sem.at[1 + h]))
    for c in own:
        c.start()
    for s in range(1, 16):
        front_copy(s).start()
    for s in range(1, 8):
        for h in range(2):
            top_copy(s, h).start()

    def fill(i, carry):
        for k in range(8):
            a_ref[pl.ds(pl.multiple_of(i * NB, NB), NB), 128 * k:128 * k + 128] = tiles_ref[i * 8 + k]
        return carry
    lax.fori_loop(0, 16, fill, 0)

    def step(j, carry):
        off = pl.multiple_of(j * 128, 128)
        diag_ref[...] = a_ref[pl.ds(off, 128), pl.ds(off, 128)]
        invert_block(diag_ref, inv_ref)
        hi, lo = split(inv_ref[...])
        inv_hi_ref[pl.ds(off, 128), :] = hi
        inv_lo_ref[pl.ds(off, 128), :] = lo
        icat_ref[:, 0:128] = hi
        icat_ref[:, 128:256] = hi
        icat_ref[:, 256:384] = lo
        first = (j + 1) // 2

        def panel(r, c):
            base = pl.multiple_of(r * 256, 256)
            hi, lo = split(a_ref[pl.ds(base, 256), pl.ds(off, 128)])
            v = lax.dot_general(jnp.concatenate([hi, lo, hi], axis=1), icat_ref[...], TN, preferred_element_type=F32)
            hi, lo = split(v)
            pcat_ref[pl.ds(base, 256), 0:128] = hi
            pcat_ref[pl.ds(base, 256), 128:256] = lo
            pcat_ref[pl.ds(base, 256), 256:384] = hi
            qcat_ref[pl.ds(base, 256), 0:128] = hi
            qcat_ref[pl.ds(base, 256), 128:256] = hi
            qcat_ref[pl.ds(base, 256), 256:384] = lo
            low_hi_ref[pl.ds(base, 256), pl.ds(off, 128)] = hi
            low_lo_ref[pl.ds(base, 256), pl.ds(off, 128)] = lo
            return c
        lax.fori_loop(first, KK // 256, panel, 0)

        def update(r, c):
            base = pl.multiple_of(r * 256, 256)

            def inner(k, c):
                cb = pl.multiple_of(k * 256, 256)
                a_ref[pl.ds(base, 256), pl.ds(cb, 256)] -= lax.dot_general(
                    pcat_ref[pl.ds(base, 256), :], qcat_ref[pl.ds(cb, 256), :], TN, preferred_element_type=F32)
                return c
            return lax.fori_loop(first, r + 1, inner, c)
        lax.fori_loop(first, KK // 256, update, 0)
        return carry
    lax.fori_loop(0, KK // 128, step, 0)
    for c in own:
        c.wait()
    for s in range(1, 16):
        front_copy(s).wait_send()
        place = front_place(lax.rem(pcol + 16 - s, 16))
        pltpu.make_async_remote_copy(place, place, send.at[s - 1], recv.at[s - 1],
                                     device_id=(prow, pcol), device_id_type=MESH).wait_recv()
    for s in range(1, 8):
        for h in range(2):
            n = 15 + (s - 1) * 2 + h
            top_copy(s, h).wait_send()
            place = top_place(lax.rem(prow + 8 - s, 8), h)
            pltpu.make_async_remote_copy(place, place, send.at[n], recv.at[n],
                                         device_id=(prow, pcol), device_id_type=MESH).wait_recv()


def factor(tiles, front, top):
    return pl.pallas_call(
        factor_kernel,
        out_shape=(
            jax.ShapeDtypeStruct((KK, 768), F32),
            jax.ShapeDtypeStruct((KK, 128), BF16),
            jax.ShapeDtypeStruct((KK, 128), BF16),
            jax.ShapeDtypeStruct((KK, KK), BF16),
            jax.ShapeDtypeStruct((KK, KK), BF16),
        ),
        in_specs=[pl.BlockSpec(memory_space=pltpu.VMEM)] * 3,
        out_specs=[pl.BlockSpec(memory_space=pltpu.VMEM)] * 5,
        scratch_shapes=[
            pltpu.VMEM((KK, KK), F32),
            pltpu.VMEM((128, 128), F32),
            pltpu.VMEM((128, 128), F32),
            pltpu.VMEM((KK, 384), BF16),
            pltpu.VMEM((KK, 384), BF16),
            pltpu.VMEM((128, 384), BF16),
            pltpu.SemaphoreType.DMA((3,)),
            pltpu.SemaphoreType.DMA((29,)),
            pltpu.SemaphoreType.DMA((29,)),
        ],
        compiler_params=pltpu.CompilerParams(collective_id=3, has_side_effects=True, vmem_limit_bytes=40 << 20),
        name="factor",
    )(tiles, front, top)


def solve_kernel(rest_ref, inv_hi_ref, inv_lo_ref, low_hi_ref, low_lo_ref, local_ref, trail_ref, panel_ref,
                 hi_ref, lo_ref, p_ref):
    for j in range(KK // 128):
        x = rest_ref[128 * j:128 * j + 128, :]
        if j:
            lh, ll = low_hi_ref[128 * j:128 * j + 128, :128 * j], low_lo_ref[128 * j:128 * j + 128, :128 * j]
            ph, pw = hi_ref[:128 * j, :], lo_ref[:128 * j, :]
            x = x - (lax.dot_general(lh, ph, NN, preferred_element_type=F32)
                     + lax.dot_general(lh, pw, NN, preferred_element_type=F32)
                     + lax.dot_general(ll, ph, NN, preferred_element_type=F32))
        xh, xl = split(x)
        ih, il = inv_hi_ref[128 * j:128 * j + 128, :], inv_lo_ref[128 * j:128 * j + 128, :]
        v = (lax.dot_general(ih, xh, NN, preferred_element_type=F32)
             + lax.dot_general(ih, xl, NN, preferred_element_type=F32)
             + lax.dot_general(il, xh, NN, preferred_element_type=F32))
        p_ref[128 * j:128 * j + 128, :] = v[:, :512]
        vh, vl = split(v)
        hi_ref[128 * j:128 * j + 128, :] = vh
        lo_ref[128 * j:128 * j + 128, :] = vl
    rh, rl = hi_ref[:, :512], lo_ref[:, :512]
    ch, cl = hi_ref[:, 512:], lo_ref[:, 512:]
    trail_ref[...] = local_ref[...] - (lax.dot_general(rh, ch, TT, preferred_element_type=F32)
                                       + lax.dot_general(rh, cl, TT, preferred_element_type=F32)
                                       + lax.dot_general(rl, ch, TT, preferred_element_type=F32))
    pcol = lax.axis_index("pcol")
    panel_ref[...] = p_ref[pl.ds(pl.multiple_of(pcol * NB, NB), NB), :].T


def solve(rest, inv_hi, inv_lo, low_hi, low_lo, local):
    return pl.pallas_call(
        solve_kernel,
        out_shape=(jax.ShapeDtypeStruct((512, 256), F32), jax.ShapeDtypeStruct((512, NB), F32)),
        in_specs=[pl.BlockSpec(memory_space=pltpu.VMEM)] * 6,
        out_specs=[pl.BlockSpec(memory_space=pltpu.VMEM)] * 2,
        scratch_shapes=[pltpu.VMEM((KK, 768), BF16)] * 2 + [pltpu.VMEM((KK, 512), F32)],
        compiler_params=pltpu.CompilerParams(vmem_limit_bytes=40 << 20),
        name="solve",
    )(rest, inv_hi, inv_lo, low_hi, low_lo, local)


def pair_kernel(rows_ref, mats_ref, local_ref, front_ref, tile_ref, x_ref, z_ref):
    depth = mats_ref.shape[0]
    for r in range(RANK):
        images = jnp.dot(rows_ref[:, r * depth:(r + 1) * depth], mats_ref[...], preferred_element_type=F32).astype(BF16)
        x_ref[r] = images[:, :depth]
        z_ref[r] = images[:, depth:]

    def pair(base, m, other, n):
        acc = None
        for r in range(RANK):
            for q in range(RANK):
                inner_x = lax.dot_general(x_ref[r, pl.ds(base, m), :], x_ref[q, other:other + n, :], TN, preferred_element_type=F32)
                inner_z = lax.dot_general(z_ref[r, pl.ds(base, m), :], z_ref[q, other:other + n, :], TN, preferred_element_type=F32)
                term = inner_x * inner_z
                if acc is None:
                    acc = term
                elif SIGNS[r] * SIGNS[q] > 0:
                    acc = acc + term
                else:
                    acc = acc - term
        return acc

    tile_ref[...] = pair(512, 64, 768, 128)

    def chunk(i, carry):
        base = pl.multiple_of(i * 128, 128)
        block = pair(base, 128, 512, 256)
        local_ref[pl.ds(base, 128), :] = block
        front_ref[:, pl.ds(base, 128)] = block[:, :128].T[:NB, :]
        return carry
    lax.fori_loop(0, 4, chunk, 0)


def pair_blocks(rows, mats):
    n, d = rows.shape[0], mats.shape[0]
    return pl.pallas_call(
        pair_kernel,
        out_shape=(
            jax.ShapeDtypeStruct((512, 256), F32),
            jax.ShapeDtypeStruct((NB, 512), F32),
            jax.ShapeDtypeStruct((NB, 128), F32),
        ),
        in_specs=[pl.BlockSpec(memory_space=pltpu.VMEM)] * 2,
        out_specs=[pl.BlockSpec(memory_space=pltpu.VMEM)] * 3,
        scratch_shapes=[pltpu.VMEM((RANK, n, d), BF16)] * 2,
        compiler_params=pltpu.CompilerParams(vmem_limit_bytes=48 << 20),
        name="pairs",
    )(rows, mats)


def per_device(factors, x_factor, zinv_factor, placement):
    rows_dev = factors.shape[1]
    total_rows = placement.shape[0]
    prow, pcol = lax.axis_index("prow"), lax.axis_index("pcol")
    flat = factors.transpose(1, 0, 2).reshape(rows_dev, -1)
    everything = gather_all(flat, F_COLORS, 1).reshape(total_rows, -1)
    k = jnp.arange(512)
    kc = jnp.arange(256)
    wanted = jnp.concatenate([
        k // NB * (NB * 8) + prow * NB + k % NB,
        kc // NB * (NB * 16) + pcol * NB + kc % NB,
        prow * 128 + jnp.arange(128),
    ])
    slot = jnp.arange(total_rows)
    device = slot // rows_dev
    place = (device % 16 * 8 + device // 16) * rows_dev + slot % rows_dev
    where = jnp.sum(jnp.where(wanted[:, None] == placement[None, :], place[None, :], 0), axis=1)
    rows = everything[where]
    mats = jnp.concatenate([x_factor, zinv_factor], axis=1)
    local, front, tile = pair_blocks(rows, mats)
    tiles = gather_all(tile, S_COLORS, 2).reshape(128, NB, 128)
    rest, inv_hi, inv_lo, low_hi, low_lo = factor(tiles, front, local[:128])
    return solve(rest, inv_hi, inv_lo, low_hi, low_lo, local)


def solution(mesh):
    in_specs = (P(None, ("prow", "pcol"), None), P(), P(), P())
    out_specs = (P("prow", "pcol"), P("prow", "pcol"))
    return jax.shard_map(per_device, mesh=mesh, in_specs=in_specs, out_specs=out_specs, check_vma=False)
```

time: 325 us -> 193 us (0.59)
  waiting for transfers between devices: 157 us -> 0 us
  Pallas kernels: 85.5 us -> 165 us
  local copies, waits for them, and re-layouts: 61.7 us -> 24.2 us
  between operations: 13.9 us -> 0.76 us
    all_gather x4 -> x0, waiting for transfers between devices: 157 us -> none  [the longest x1 65.1 us: per_device(): everything = lax.all_gather(factors, ('prow', 'pcol'), axis=1, tiled=True)]
    pallas_call x2 -> x5, Pallas kernels: 85.5 us -> 165 us  [the longest x2 86.5 us: gather_all(): pl.pallas_call(functools.partial(gather_kernel, colors), out_shape=jax.Sh...]
    scatter x1 -> x0, local copies, waits for them, and re-layouts: 15.5 us -> none  [per_device(): jnp.zeros((total_rows,), jnp.int32).at[placement]]
    gather x6 -> x1, local copies, waits for them, and re-layouts: 26.1 us -> 17 us  [per_device(): rows = everything[where]]
    transpose x1 -> x0, local copies, waits for them, and re-layouts: 4.73 us -> none  [natural_rows(): return stacked.reshape(prow_count, lead_rows // NB, NB, stacked.shape[1])...]
    slice x6 -> x1, local copies, waits for them, and re-layouts: 4.26 us -> 0.01 us  [per_device(): rest, inv_hi, inv_lo, low_hi, low_lo = factor(tiles, front, local[:128])]
    reshape x2 -> x1, local copies, waits for them, and re-layouts: 4.84 us -> 1.57 us  [per_device(): flat = factors.transpose(1, 0, 2).reshape(rows_dev, -1)]
  transfers between devices with their start and end apart: 4 -> 0, of which waited for: 4 -> 0; matrix products, arithmetic and copies ran while one was open for 10% -> 0% of each run, Pallas kernels for 0% -> 0%
where the time goes in v2:
time: 193 us; the launch traced here: 192 us
  Pallas kernels  165 us (85%)
  local copies, waits for them, and re-layouts  24.2 us (13%)
  other arithmetic  2.53 us (1%)
    pallas_call x2, Pallas kernels, gather_all(): pl.pallas_call(functools.partial(gather_kernel, colors), out_shape=jax.Sh...  86.5 us
    pallas_call x1, Pallas kernels, factor(): pl.pallas_call(factor_kernel, out_shape=(jax.ShapeDtypeStruct((KK, 768),...  53.2 us
    gather x1, local copies, waits for them, and re-layouts, per_device(): rows = everything[where]  17 us
    pallas_call x1, Pallas kernels, pair_blocks(): pl.pallas_call(pair_kernel, out_shape=(jax.ShapeDtypeStruct((512, 256), F...  16.9 us
    pallas_call x1, Pallas kernels, solve(): pl.pallas_call(solve_kernel, out_shape=(jax.ShapeDtypeStruct((512, 256),...  8.35 us
    unnamed x10, local copies, waits for them, and re-layouts  4.85 us

profile of v2, /device:TPU:1, one launch (start us, length us, event | category | flops | bytes accessed | tf_op | source)
XLA Modules:
  0.0 192.4 jit_solution(13137146154953770775)
XLA Ops:
  0.7 2.3 %select_reduce_fusion = s32[896]{0:T(1024)S(1)} fusion(s32[4096]{0:T(1024)S(1)} %fusion.9, s32[4096]{0:T(1024)} %param.7, s32[896]{0:T(1024)S(1)} %pad_add_fusion), kind=kLoop, calls=%fused_computation.1 | loop fusion | flops 11009152 | bytes 39936 | tf_op jit(solution)/shard_map/reduce_sum | solution.py:427
  3.1 1.6 copy.12
  4.7 55.1 %gather_all_1.1 = bf16[4,4,4,2,32,2048]{5,4,3,2,1,0:T(8,128)(2,1)} custom-call(bf16[32,2048]{1,0:T(8,128)(2,1)} %bitcast.7), custom_call_target="tpu_custom_call" | custom-call | tf_op jit(solution)/shard_map/gather_all_1/pallas_call | solution.py:173
  59.7 0.0 copy-start.3
  59.7 0.0 copy-start.4
  59.7 17.0 %gather_fusion = bf16[896,2048]{1,0:T(8,128)(2,1)} fusion(bf16[4096,2048]{1,0:T(8,128)(2,1)} %bitcast.6, s32[1024]{0:T(1024)S(1)} %pad_clamp_fusion), kind=kCustom, calls=%fused_computation | custom fusion | bytes 7343616 | tf_op jit(solution)/shard_map/gather | solution.py:428
  76.7 0.0 copy-done.3
  76.7 0.0 copy-done.4
  76.7 0.1 pad_maximum_fusion.mats_ref
  76.9 0.0 copy-start.1
  76.9 2.0 %copy-done.1 = bf16[896,2048]{1,0:T(8,128)(2,1)S(1)} copy-done((bf16[896,2048]{1,0:T(8,128)(2,1)S(1)}, bf16[896,2048]{1,0:T(8,128)(2,1)}, u32[]{:S(2)}) %copy-start.1) | copy-done | bytes 3670040
  78.9 16.9 %pairs.1 = (f32[512,256]{1,0:T(8,128)S(1)}, f32[64,512]{1,0:T(8,128)S(1)}, f32[64,128]{1,0:T(8,128)S(1)}) custom-call(bf16[896,2048]{1,0:T(8,128)(2,1)S(1)} %copy-done.1, bf16[512,1024]{1,0:T(8,128)(2,1)S(1)} %pad_maximum_fusion.mats_ref), custom_call_target="tpu_custom_call" | custom-call | tf_op jit(solution)/shard_map/pairs/pallas_call | solution.py:396
  95.8 0.0 copy-start.2
  95.8 0.6 copy-done.2
  96.4 31.5 %gather_all_2.1 = f32[4,4,4,2,64,128]{5,4,3,2,1,0:T(8,128)} custom-call(f32[64,128]{1,0:T(8,128)} %copy-done.2), custom_call_target="tpu_custom_call" | custom-call | tf_op jit(solution)/shard_map/gather_all_2/pallas_call | solution.py:173
  127.9 0.0 copy-start
  127.9 2.2 %copy-done = f32[4,4,4,2,64,128]{5,4,3,2,1,0:T(8,128)S(1)} copy-done((f32[4,4,4,2,64,128]{5,4,3,2,1,0:T(8,128)S(1)}, f32[4,4,4,2,64,128]{5,4,3,2,1,0:T(8,128)}, u32[]{:S(2)}) %copy-start) | copy-done | bytes 4194328
  130.1 53.2 %factor.1 = (f32[1024,768]{1,0:T(8,128)S(1)}, bf16[1024,128]{1,0:T(8,128)(2,1)S(1)}, bf16[1024,128]{1,0:T(8,128)(2,1)S(1)}, bf16[1024,1024]{1,0:T(8,128)(2,1)S(1)}, bf16[1024,1024]{1,0:T(8,128)(2,1)S(1)}) custom-call(f32[128,64,128]{2,1,0:T(8,128)S(1)} %bitcast.5, f32[64,512]{1,0:T(8,128)S(1)} %get-tuple-element.11.front_ref, f32[128,256]{1,0:T(8,128)S(1)} %slice.3.top_ref), custom_call_target="tpu_custom_call" | custom-call | tf_op jit(solution)/shard_map/factor/pallas_call | solution.py:294
  183.3 8.3 %solve.1 = (f32[512,256]{1,0:T(8,128)}, f32[512,64]{1,0:T(8,128)S(1)}) custom-call(f32[1024,768]{1,0:T(8,128)S(1)} %get-tuple-element.13.rest_ref, bf16[1024,128]{1,0:T(8,128)(2,1)S(1)} %get-tuple-element.14.inv_hi_ref, bf16[1024,128]{1,0:T(8,128)(2,1)S(1)} %get-tuple-element.15.inv_lo_ref, bf16[1024,1024]{1,0:T(8,128)(2,1)S(1)} %get-tuple-element.16.low_hi_ref, ...), custom_call_target="tpu_custom_call" | custom-call | tf_op jit(solution)/shard_map/solve/pallas_call | solution.py:350
  191.6 0.8 copy.11
  (8 shorter events, 0.1 us)
Async XLA Ops:
  59.7 17.0 %copy-start.3 = (bf16[512,512]{1,0:T(8,128)(2,1)S(1)}, bf16[512,512]{1,0:T(8,128)(2,1)}, u32[]{:S(2)}) copy-start(bf16[512,512]{1,0:T(8,128)(2,1)} %param.6) | copy-start | bytes 1572868
  59.7 17.0 %copy-start.4 = (bf16[512,512]{1,0:T(8,128)(2,1)S(1)}, bf16[512,512]{1,0:T(8,128)(2,1)}, u32[]{:S(2)}) copy-start(bf16[512,512]{1,0:T(8,128)(2,1)} %param.5) | copy-start | bytes 1572868
  76.9 2.0 %copy-start.1 = (bf16[896,2048]{1,0:T(8,128)(2,1)S(1)}, bf16[896,2048]{1,0:T(8,128)(2,1)}, u32[]{:S(2)}) copy-start(bf16[896,2048]{1,0:T(8,128)(2,1)} %gather_fusion) | copy-start | bytes 11010052
  95.8 0.6 copy-start.2
  127.9 2.2 %copy-start = (f32[4,4,4,2,64,128]{5,4,3,2,1,0:T(8,128)S(1)}, f32[4,4,4,2,64,128]{5,4,3,2,1,0:T(8,128)}, u32[]{:S(2)}) copy-start(f32[4,4,4,2,64,128]{5,4,3,2,1,0:T(8,128)} %gather_all_2.1) | copy-start | bytes 12582916

commit v3 on v2

--- a/solution.py
+++ b/solution.py
@@ -79,9 +79,171 @@
 
 
 ORDERS = ((0, 1, 2), (1, 2, 0), (2, 0, 1))
-
-
-def gather_kernel(colors, in_ref, out_ref, own_sem, send, recv, psend, precv):
+COLORS = (((0, 16, 24), (0, 128)), ((24, 32, 48), (0, 128)), ((48, 56, 64), (0, 128)))
+
+
+W = 2176
+
+
+def before(n):
+    return (lax.broadcasted_iota(jnp.int32, (n, n), 0) > lax.broadcasted_iota(jnp.int32, (n, n), 1)).astype(BF16)
+
+
+def earlier(mask):
+    n = mask.shape[0]
+    wide = jnp.broadcast_to(mask.astype(F32), (n, 128)).astype(BF16)
+    return jnp.dot(before(n), wide, preferred_element_type=F32)[:, 0:1].astype(jnp.int32)
+
+
+def pick(index, valid, n):
+    lane = lax.broadcasted_iota(jnp.int32, (index.shape[0], n), 1)
+    hit = lane == index
+    if valid is not None:
+        hit = hit & valid
+    return hit.astype(F32).astype(BF16)
+
+
+def route_kernel(flat_ref, mine_ref, order_ref, rows_ref, cols_ref,
+                 send_a, got_a, send_b, got_b, piece_ref, ss, rs):
+    prow, pcol = lax.axis_index("prow"), lax.axis_index("pcol")
+    twin = (lax.rem(pcol, 8), prow + 8 * (pcol // 8))
+    at_home = prow == lax.rem(pcol, 8)
+    barrier = pltpu.get_barrier_semaphore()
+    for s in range(1, 16):
+        pl.semaphore_signal(barrier, inc=1, device_id=(prow, lax.rem(pcol + s, 16)), device_id_type=MESH)
+    for s in range(1, 8):
+        pl.semaphore_signal(barrier, inc=1, device_id=(lax.rem(prow + s, 8), pcol), device_id_type=MESH)
+
+    @pl.when(jnp.logical_not(at_home))
+    def _():
+        pl.semaphore_signal(barrier, inc=1, device_id=twin, device_id_type=MESH)
+
+    group = (mine_ref[...] >> 6) & 7
+    row = lax.broadcasted_iota(jnp.int32, (64, 32), 0)
+    match = group == (row >> 3)
+    ahead = (lax.broadcasted_iota(jnp.int32, (32, 32), 0) < lax.broadcasted_iota(jnp.int32, (32, 32), 1)).astype(BF16)
+    rank = jnp.dot(match.astype(F32).astype(BF16), ahead, preferred_element_type=F32).astype(jnp.int32)
+    sel = (match & (rank == (row & 7))).astype(F32).astype(BF16)
+    send_a[...] = jnp.dot(sel, flat_ref[...], preferred_element_type=F32).reshape(8, 8, W).astype(BF16)
+    got_a[prow] = send_a[prow]
+
+    kind = (order_ref[...] >> 6) & 15
+    prior = lax.broadcasted_iota(jnp.int32, kind.shape, 0) < pcol
+    base = [jnp.sum((prior & (kind == prow + 8 * h)).astype(F32), keepdims=True).astype(jnp.int32) for h in range(2)]
+
+    pl.semaphore_wait(barrier, jnp.where(at_home, 22, 23))
+
+    def copy(src, dst, n, to):
+        return pltpu.make_async_remote_copy(src, dst, ss.at[n], rs.at[n], device_id=to, device_id_type=MESH)
+
+    def along_prow(s):
+        return (lax.rem(prow + s, 8), pcol)
+
+    def along_pcol(s):
+        return (prow, lax.rem(pcol + s, 16))
+
+    def slab(ref, i, n):
+        return ref.at[pl.ds(pl.multiple_of(i * n, n), n)]
+
+    def a_copy(s):
+        return copy(send_a.at[lax.rem(prow + s, 8)], got_a.at[prow], s - 1, along_prow(s))
+
+    def b_copy(s):
+        return copy(send_b.at[lax.rem(pcol + s, 16)], got_b.at[pcol], 7 + s - 1, along_pcol(s))
+
+    def row_copy(s):
+        return copy(piece_ref, slab(rows_ref, pcol, 32), 22 + s - 1, along_pcol(s))
+
+    def twin_copy():
+        return copy(piece_ref, slab(cols_ref, twin[0], 32), 37, twin)
+
+    def col_copy(s):
+        return copy(slab(cols_ref, prow, 32), slab(cols_ref, prow, 32), 38 + s - 1, along_prow(s))
+
+    for s in range(1, 8):
+        a_copy(s).start()
+    for s in range(1, 8):
+        spot = got_a.at[lax.rem(prow + 8 - s, 8)]
+        copy(spot, spot, s - 1, along_prow(1)).wait_recv()
+
+    got = got_a[...].astype(F32).reshape(64, W).astype(BF16)
+    tags = got[:, 2048:].astype(F32)
+    valid = tags[:, 2:3] > 0.5
+    half = (tags[:, 0:1].astype(jnp.int32) >> 3) & 1
+    slot = jnp.zeros((64, 1), jnp.int32)
+    for h in range(2):
+        li = earlier(valid & (half == h))
+        slot = jnp.where(half == h, (8 * h + ((base[h] + li) & 7)) * 8 + (li >> 3), slot)
+    send_b[...] = lax.dot_general(pick(slot, valid, 128), got, TT, preferred_element_type=F32).reshape(16, 8, W).astype(BF16)
+    got_b[pcol] = send_b[pcol]
+    for s in range(1, 16):
+        b_copy(s).start()
+    for s in range(1, 16):
+        spot = got_b.at[lax.rem(pcol + 16 - s, 16)]
+        copy(spot, spot, 7 + s - 1, along_prow(1)).wait_recv()
+
+    got = got_b[...].astype(F32).reshape(128, W).astype(BF16)
+    valid = got[:, 2048:].astype(F32)[:, 2:3] > 0.5
+    piece = lax.dot_general(pick(earlier(valid), valid, 32), got, TT, preferred_element_type=F32).astype(BF16)
+    piece_ref[...] = piece
+    rows_ref[pl.ds(pl.multiple_of(pcol * 32, 32), 32), :] = piece
+
+    @pl.when(at_home)
+    def _():
+        cols_ref[pl.ds(pl.multiple_of(prow * 32, 32), 32), :] = piece
+
+    @pl.when(jnp.logical_not(at_home))
+    def _():
+        twin_copy().start()
+    for s in range(1, 16):
+        row_copy(s).start()
+
+    @pl.when(jnp.logical_not(at_home))
+    def _():
+        spot = slab(cols_ref, prow, 32)
+        copy(spot, spot, 37, twin).wait_recv()
+    for s in range(1, 8):
+        col_copy(s).start()
+    for s in range(1, 8):
+        spot = slab(cols_ref, lax.rem(prow + 8 - s, 8), 32)
+        copy(spot, spot, 38 + s - 1, along_prow(1)).wait_recv()
+    for s in range(1, 16):
+        spot = slab(rows_ref, lax.rem(pcol + 16 - s, 16), 32)
+        copy(spot, spot, 22 + s - 1, along_prow(1)).wait_recv()
+    for s in range(1, 8):
+        a_copy(s).wait_send()
+        col_copy(s).wait_send()
+    for s in range(1, 16):
+        b_copy(s).wait_send()
+        row_copy(s).wait_send()
+
+    @pl.when(jnp.logical_not(at_home))
+    def _():
+        twin_copy().wait_send()
+
+
+def route(flat, mine, order):
+    return pl.pallas_call(
+        route_kernel,
+        out_shape=(jax.ShapeDtypeStruct((512, W), BF16), jax.ShapeDtypeStruct((256, W), BF16)),
+        in_specs=[pl.BlockSpec(memory_space=pltpu.VMEM)] * 3,
+        out_specs=[pl.BlockSpec(memory_space=pltpu.VMEM)] * 2,
+        scratch_shapes=[
+            pltpu.VMEM((8, 8, W), BF16),
+            pltpu.VMEM((8, 8, W), BF16),
+            pltpu.VMEM((16, 8, W), BF16),
+            pltpu.VMEM((16, 8, W), BF16),
+            pltpu.VMEM((32, W), BF16),
+            pltpu.SemaphoreType.DMA((45,)),
+            pltpu.SemaphoreType.DMA((45,)),
+        ],
+        compiler_params=pltpu.CompilerParams(collective_id=1, has_side_effects=True, vmem_limit_bytes=24 << 20),
+        name="route",
+    )(flat, mine, order)
+
+
+def pair_kernel(rows_ref, cols_ref, mats_ref, local_ref, front_ref, out_ref, in_ref, x_ref, z_ref, own_sem, send, recv, psend, precv):
+    colors = COLORS
     prow, pcol = lax.axis_index("prow"), lax.axis_index("pcol")
     me = (pcol // 4, pcol % 4, prow // 2)
     core = prow % 2
@@ -95,6 +257,40 @@
         for shift in (1, -1):
             pl.semaphore_signal(barrier, inc=1, device_id=device(dim, shift), device_id_type=MESH)
     pl.semaphore_signal(barrier, inc=1, device_id=partner, device_id_type=MESH)
+    depth = mats_ref.shape[0]
+
+    def load(src, first, count, shift, at):
+        tags = src[:, 2048:].astype(F32).astype(jnp.int32)
+        spot = (tags[:, 0:1] >> shift) * NB + tags[:, 1:2] - first
+        rows = lax.dot_general(pick(spot, None, count), src[:, :2048], TT, preferred_element_type=F32).astype(BF16)
+        for r in range(RANK):
+            images = jnp.dot(rows[:, r * depth:(r + 1) * depth], mats_ref[...], preferred_element_type=F32).astype(BF16)
+            x_ref[r, at:at + count, :] = images[:, :depth]
+            z_ref[r, at:at + count, :] = images[:, depth:]
+
+    def pair(base, m, other, n):
+        acc = None
+        for r in range(RANK):
+            for q in range(RANK):
+                inner_x = lax.dot_general(x_ref[r, base:base + m, :], x_ref[q, other:other + n, :], TN, preferred_element_type=F32)
+                inner_z = lax.dot_general(z_ref[r, base:base + m, :], z_ref[q, other:other + n, :], TN, preferred_element_type=F32)
+                term = inner_x * inner_z
+                if acc is None:
+                    acc = term
+                elif SIGNS[r] * SIGNS[q] > 0:
+                    acc = acc + term
+                else:
+                    acc = acc - term
+        return acc
+
+    def chunk(base):
+        block = pair(base, 128, 512, 256)
+        local_ref[base:base + 128, :] = block
+        front_ref[:, base:base + 128] = block[:, :128].T[:NB, :]
+
+    load(cols_ref, 0, 64, 4, 512)
+    load(rows_ref, 0, 128, 3, 0)
+    in_ref[...] = pair(512, 64, 0, 128)
     own = pltpu.make_async_copy(in_ref, out_ref.at[me[0], me[1], me[2], core], own_sem)
     own.start()
     pl.semaphore_wait(barrier, 7)
@@ -136,7 +332,16 @@
     for c in range(3):
         ring(c, 0, 0).start()
         ring(c, 0, 1).start()
+    jobs = [
+        lambda: load(cols_ref, 64, 192, 4, 576),
+        lambda: load(rows_ref, 128, 384, 3, 128),
+        lambda: chunk(0),
+        lambda: chunk(128),
+        lambda: chunk(256),
+        lambda: chunk(384),
+    ]
     for phase in range(3):
+        jobs[2 * phase]()
         for c in range(3):
             landed(c, phase, 0)
             ring(c, phase, 2).start()
@@ -148,6 +353,7 @@
                 across(c, 2, core).start()
         if phase == 0:
             own.wait()
+        jobs[2 * phase + 1]()
         for c in range(3):
             landed(c, phase, 2)
             if phase == 2:
@@ -169,26 +375,30 @@
                 ring(c, phase, which).wait_send()
 
 
-def gather_all(block, colors, ident):
+def pair_blocks(rows, cols, mats):
+    d = mats.shape[0]
     return pl.pallas_call(
-        functools.partial(gather_kernel, colors),
-        out_shape=jax.ShapeDtypeStruct((4, 4, 4, 2) + block.shape, block.dtype),
-        in_specs=[pl.BlockSpec(memory_space=pltpu.VMEM)],
-        out_specs=pl.BlockSpec(memory_space=pl.ANY),
+        pair_kernel,
+        out_shape=(
+            jax.ShapeDtypeStruct((512, 256), F32),
+            jax.ShapeDtypeStruct((NB, 512), F32),
+            jax.ShapeDtypeStruct((4, 4, 4, 2, NB, 128), F32),
+        ),
+        in_specs=[pl.BlockSpec(memory_space=pltpu.VMEM)] * 3,
+        out_specs=[pl.BlockSpec(memory_space=pltpu.VMEM)] * 3,
         scratch_shapes=[
+            pltpu.VMEM((NB, 128), F32),
+            pltpu.VMEM((RANK, 768, d), BF16),
+            pltpu.VMEM((RANK, 768, d), BF16),
             pltpu.SemaphoreType.DMA,
             pltpu.SemaphoreType.DMA((36,)),
             pltpu.SemaphoreType.DMA((36,)),
             pltpu.SemaphoreType.DMA((15,)),
             pltpu.SemaphoreType.DMA((15,)),
         ],
-        compiler_params=pltpu.CompilerParams(collective_id=ident, has_side_effects=True),
-        name="gather_all_%d" % ident,
-    )(block)
-
-
-F_COLORS = (((0, 16, 32), (0, 640)), ((0, 16, 32), (640, 1280)), ((0, 16, 32), (1280, 2048)))
-S_COLORS = (((0, 16, 24), (0, 128)), ((24, 32, 48), (0, 128)), ((48, 56, 64), (0, 128)))
+        compiler_params=pltpu.CompilerParams(collective_id=2, has_side_effects=True, vmem_limit_bytes=40 << 20),
+        name="pairs",
+    )(rows, cols, mats)
 
 
 def factor_kernel(tiles_ref, front_ref, top_ref, rest_ref, inv_hi_ref, inv_lo_ref, low_hi_ref, low_lo_ref,
@@ -228,9 +438,14 @@
         for h in range(2):
             top_copy(s, h).start()
 
+    left = lax.broadcasted_iota(jnp.int32, (NB, 128), 1) < NB
+
     def fill(i, carry):
-        for k in range(8):
-            a_ref[pl.ds(pl.multiple_of(i * NB, NB), NB), 128 * k:128 * k + 128] = tiles_ref[i * 8 + k]
+        at = pl.ds(pl.multiple_of(i * NB, NB), NB)
+        for k in range(4):
+            even, odd = tiles_ref[i * 8 + 2 * k], tiles_ref[i * 8 + 2 * k + 1]
+            a_ref[at, 128 * k:128 * k + 128] = jnp.where(left, even, pltpu.roll(odd, NB, 1))
+            a_ref[at, 512 + 128 * k:640 + 128 * k] = jnp.where(left, pltpu.roll(even, NB, 1), odd)
         return carry
     lax.fori_loop(0, 16, fill, 0)
 
@@ -358,78 +573,18 @@
     )(rest, inv_hi, inv_lo, low_hi, low_lo, local)
 
 
-def pair_kernel(rows_ref, mats_ref, local_ref, front_ref, tile_ref, x_ref, z_ref):
-    depth = mats_ref.shape[0]
-    for r in range(RANK):
-        images = jnp.dot(rows_ref[:, r * depth:(r + 1) * depth], mats_ref[...], preferred_element_type=F32).astype(BF16)
-        x_ref[r] = images[:, :depth]
-        z_ref[r] = images[:, depth:]
-
-    def pair(base, m, other, n):
-        acc = None
-        for r in range(RANK):
-            for q in range(RANK):
-                inner_x = lax.dot_general(x_ref[r, pl.ds(base, m), :], x_ref[q, other:other + n, :], TN, preferred_element_type=F32)
-                inner_z = lax.dot_general(z_ref[r, pl.ds(base, m), :], z_ref[q, other:other + n, :], TN, preferred_element_type=F32)
-                term = inner_x * inner_z
-                if acc is None:
-                    acc = term
-                elif SIGNS[r] * SIGNS[q] > 0:
-                    acc = acc + term
-                else:
-                    acc = acc - term
-        return acc
-
-    tile_ref[...] = pair(512, 64, 768, 128)
-
-    def chunk(i, carry):
-        base = pl.multiple_of(i * 128, 128)
-        block = pair(base, 128, 512, 256)
-        local_ref[pl.ds(base, 128), :] = block
-        front_ref[:, pl.ds(base, 128)] = block[:, :128].T[:NB, :]
-        return carry
-    lax.fori_loop(0, 4, chunk, 0)
-
-
-def pair_blocks(rows, mats):
-    n, d = rows.shape[0], mats.shape[0]
-    return pl.pallas_call(
-        pair_kernel,
-        out_shape=(
-            jax.ShapeDtypeStruct((512, 256), F32),
-            jax.ShapeDtypeStruct((NB, 512), F32),
-            jax.ShapeDtypeStruct((NB, 128), F32),
-        ),
-        in_specs=[pl.BlockSpec(memory_space=pltpu.VMEM)] * 2,
-        out_specs=[pl.BlockSpec(memory_space=pltpu.VMEM)] * 3,
-        scratch_shapes=[pltpu.VMEM((RANK, n, d), BF16)] * 2,
-        compiler_params=pltpu.CompilerParams(vmem_limit_bytes=48 << 20),
-        name="pairs",
-    )(rows, mats)
-
-
 def per_device(factors, x_factor, zinv_factor, placement):
     rows_dev = factors.shape[1]
-    total_rows = placement.shape[0]
     prow, pcol = lax.axis_index("prow"), lax.axis_index("pcol")
-    flat = factors.transpose(1, 0, 2).reshape(rows_dev, -1)
-    everything = gather_all(flat, F_COLORS, 1).reshape(total_rows, -1)
-    k = jnp.arange(512)
-    kc = jnp.arange(256)
-    wanted = jnp.concatenate([
-        k // NB * (NB * 8) + prow * NB + k % NB,
-        kc // NB * (NB * 16) + pcol * NB + kc % NB,
-        prow * 128 + jnp.arange(128),
-    ])
-    slot = jnp.arange(total_rows)
-    device = slot // rows_dev
-    place = (device % 16 * 8 + device // 16) * rows_dev + slot % rows_dev
-    where = jnp.sum(jnp.where(wanted[:, None] == placement[None, :], place[None, :], 0), axis=1)
-    rows = everything[where]
+    mine = lax.dynamic_slice_in_dim(placement, (prow * 16 + pcol) * rows_dev, rows_dev)
+    lane = jnp.arange(128)[None, :]
+    tags = jnp.where(lane == 0, (mine >> 6)[:, None], jnp.where(lane == 1, (mine & 63)[:, None], (lane == 2).astype(jnp.int32)))
+    flat = jnp.concatenate([factors.transpose(1, 0, 2).reshape(rows_dev, -1), tags.astype(BF16)], axis=1)
+    order = placement.reshape(8, 16, rows_dev).transpose(1, 0, 2).reshape(16, 8 * rows_dev)
+    rows, cols = route(flat, mine[None, :], order)
     mats = jnp.concatenate([x_factor, zinv_factor], axis=1)
-    local, front, tile = pair_blocks(rows, mats)
-    tiles = gather_all(tile, S_COLORS, 2).reshape(128, NB, 128)
-    rest, inv_hi, inv_lo, low_hi, low_lo = factor(tiles, front, local[:128])
+    local, front, tiles = pair_blocks(rows, cols, mats)
+    rest, inv_hi, inv_lo, low_hi, low_lo = factor(tiles.reshape(128, NB, 128), front, local[:128])
     return solve(rest, inv_hi, inv_lo, low_hi, low_lo, local)
 
 

time: 193 us -> 172 us (0.89)
  local copies, waits for them, and re-layouts: 24.2 us -> 2.6 us
    pallas_call x2 -> x1, Pallas kernels: 86.5 us -> 55.6 us  [route(): pl.pallas_call(route_kernel, out_shape=(jax.ShapeDtypeStruct((512, W), BF...]
    pallas_call x1, Pallas kernels: 16.9 us -> 46.8 us  [pair_blocks(): pl.pallas_call(pair_kernel, out_shape=(jax.ShapeDtypeStruct((512, 256), F...]
    gather x1 -> x0, local copies, waits for them, and re-layouts: 17 us -> none  [per_device(): rows = everything[where]]
    unnamed x10 -> x0, local copies, waits for them, and re-layouts: 4.85 us -> none
    reduce_sum x1 -> x0, other arithmetic: 2.33 us -> none  [per_device(): jnp.sum(jnp.where(wanted[:, None] == placement[None, :], place[None, :],...]
    pallas_call x1, Pallas kernels: 53.2 us -> 55.2 us  [factor(): pl.pallas_call(factor_kernel, out_shape=(jax.ShapeDtypeStruct((KK, 768),...]
where the time goes in v3:
time: 172 us; the launch traced here: 171 us
  Pallas kernels  166 us (97%)
  local copies, waits for them, and re-layouts  2.6 us (2%)
  other arithmetic  2.18 us (1%)
    pallas_call x1, Pallas kernels, route(): pl.pallas_call(route_kernel, out_shape=(jax.ShapeDtypeStruct((512, W), BF...  55.6 us
    pallas_call x1, Pallas kernels, factor(): pl.pallas_call(factor_kernel, out_shape=(jax.ShapeDtypeStruct((KK, 768),...  55.2 us
    pallas_call x1, Pallas kernels, pair_blocks(): pl.pallas_call(pair_kernel, out_shape=(jax.ShapeDtypeStruct((512, 256), F...  46.8 us
    pallas_call x1, Pallas kernels, solve(): pl.pallas_call(solve_kernel, out_shape=(jax.ShapeDtypeStruct((512, 256),...  8.35 us

profile of v3, /device:TPU:1, one launch (start us, length us, event | category | flops | bytes accessed | tf_op | source)
XLA Modules:
  0.0 171.4 jit_solution(112827348110281561)
XLA Ops:
  0.6 0.8 dynamic-slice_bitcast_fusion
  1.4 0.1 select_convert_fusion
  1.5 0.8 reshape.36
  2.3 0.1 reshape.37.order_ref
  2.4 0.9 copy.11
  3.3 1.3 pad_maximum_fusion.mats_ref
  4.7 55.6 %route.1 = (bf16[512,2176]{1,0:T(8,128)(2,1)S(1)}, bf16[256,2176]{1,0:T(8,128)(2,1)S(1)}) custom-call(bf16[32,2176]{1,0:T(8,128)(2,1)S(1)} %pad_maximum_fusion.1.flat_ref, s32[1,32]{1,0:T(1,128)S(1)} %get-tuple-element.26.mine_ref, s32[16,256]{1,0:T(8,128)S(1)} %reshape.37.order_ref), custom_call_target="tpu_custom_call" | custom-call | tf_op jit(solution)/shard_map/route/pallas_call | solution.py:226
  60.3 46.8 %pairs.1 = (f32[512,256]{1,0:T(8,128)S(1)}, f32[64,512]{1,0:T(8,128)S(1)}, f32[4,4,4,2,64,128]{5,4,3,2,1,0:T(8,128)S(1)}) custom-call(bf16[512,2176]{1,0:T(8,128)(2,1)S(1)} %get-tuple-element.12.rows_ref, bf16[256,2176]{1,0:T(8,128)(2,1)S(1)} %get-tuple-element.13.cols_ref, bf16[512,1024]{1,0:T(8,128)(2,1)S(1)} %pad_maximum_fusion.mats_ref), custom_call_target="tpu_custom_call" | custom-call | tf_op jit(solution)/shard_map/pairs/pallas_call | solution.py:380
  107.1 55.2 %factor.1 = (f32[1024,768]{1,0:T(8,128)S(1)}, bf16[1024,128]{1,0:T(8,128)(2,1)S(1)}, bf16[1024,128]{1,0:T(8,128)(2,1)S(1)}, bf16[1024,1024]{1,0:T(8,128)(2,1)S(1)}, bf16[1024,1024]{1,0:T(8,128)(2,1)S(1)}) custom-call(f32[128,64,128]{2,1,0:T(8,128)S(1)} %bitcast.7, f32[64,512]{1,0:T(8,128)S(1)} %get-tuple-element.15.front_ref, f32[128,256]{1,0:T(8,128)S(1)} %slice.3.top_ref), custom_call_target="tpu_custom_call" | custom-call | tf_op jit(solution)/shard_map/factor/pallas_call | solution.py:509
  162.3 8.3 %solve.1 = (f32[512,256]{1,0:T(8,128)}, f32[512,64]{1,0:T(8,128)S(1)}) custom-call(f32[1024,768]{1,0:T(8,128)S(1)} %get-tuple-element.17.rest_ref, bf16[1024,128]{1,0:T(8,128)(2,1)S(1)} %get-tuple-element.18.inv_hi_ref, bf16[1024,128]{1,0:T(8,128)(2,1)S(1)} %get-tuple-element.19.inv_lo_ref, bf16[1024,1024]{1,0:T(8,128)(2,1)S(1)} %get-tuple-element.20.low_hi_ref, ...), custom_call_target="tpu_custom_call" | custom-call | tf_op jit(solution)/shard_map/solve/pallas_call | solution.py:565
  170.7 0.8 copy.10
  (5 shorter events, 0.1 us)

commit v4 on v3

--- a/solution.py
+++ b/solution.py
@@ -78,8 +78,126 @@
             aug[i] = aug[i] - acce
 
 
-ORDERS = ((0, 1, 2), (1, 2, 0), (2, 0, 1))
-COLORS = (((0, 16, 24), (0, 128)), ((24, 32, 48), (0, 128)), ((48, 56, 64), (0, 128)))
+OFFS = 4
+
+
+class Plane:
+    def __init__(self, view, send, recv, arrived):
+        self.prow, self.pcol = lax.axis_index("prow"), lax.axis_index("pcol")
+        self.me = (self.pcol // 4, lax.rem(self.pcol, 4))
+        self.sign = 1 - 2 * lax.rem(self.prow, 2)
+        self.offs = (0, -self.sign, self.sign, 2)
+        self.raw, self.send, self.recv, self.arrived = view, send, recv, arrived
+
+    def view(self, colour, first, second):
+        steps = (first, second) if colour == 0 else (second, first)
+        at = [lax.rem(v + s + OFFS, 4) for v, s in zip(self.me, steps)]
+        return self.raw(colour, at[0], at[1])
+
+    def peer(self, colour, leg, step):
+        dim = leg if colour == 0 else 1 - leg
+        at = [lax.rem(v + step + OFFS, 4) if d == dim else v for d, v in enumerate(self.me)]
+        return (self.prow, at[0] * 4 + at[1])
+
+    def message(self, colour, leg, o, kind):
+        n = colour * 15 + (kind if leg == 0 else 3 + o * 3 + kind)
+        carried = -self.sign if kind == 2 else 0
+        part = self.view(colour, carried, 0) if leg == 0 else self.view(colour, self.offs[o], carried)
+        to = self.peer(colour, leg, -self.sign if kind == 1 else self.sign)
+        return pltpu.make_async_remote_copy(part, part, self.send.at[n], self.recv.at[n], device_id=to, device_id_type=MESH)
+
+    def landed(self, colour, leg, o, kind):
+        n = colour * 15 + (kind if leg == 0 else 3 + o * 3 + kind)
+        come = (-self.sign, self.sign, 2)[kind]
+        part = self.view(colour, come, 0) if leg == 0 else self.view(colour, self.offs[o], come)
+        pltpu.make_async_remote_copy(part, part, self.send.at[n], self.recv.at[n],
+                                     device_id=self.peer(colour, leg, 1), device_id_type=MESH).wait_recv()
+        if self.arrived is not None:
+            self.arrived(colour, part, 1 + (kind if leg == 0 else 3 + o * 3 + kind))
+
+    def both(self, colour, leg, o):
+        self.message(colour, leg, o, 0).start()
+        self.message(colour, leg, o, 1).start()
+
+    def stages(self):
+        def relay(c, leg, o):
+            self.landed(c, leg, o, 0)
+            self.message(c, leg, o, 2).start()
+
+        def s0():
+            for c in range(2):
+                self.both(c, 0, 0)
+            for c in range(2):
+                self.both(c, 1, 0)
+
+        def s1():
+            for c in range(2):
+                relay(c, 0, 0)
+                self.both(c, 1, 1)
+
+        def s2():
+            for c in range(2):
+                self.landed(c, 0, 0, 1)
+                self.both(c, 1, 2)
+
+        def s3():
+            for c in range(2):
+                relay(c, 1, 0)
+
+        def s4():
+            for c in range(2):
+                self.landed(c, 0, 0, 2)
+                self.both(c, 1, 3)
+
+        def s5():
+            for o in (1, 2):
+                for c in range(2):
+                    relay(c, 1, o)
+
+        def s6():
+            for c in range(2):
+                relay(c, 1, 3)
+
+        def s7():
+            for o in range(4):
+                for c in range(2):
+                    self.landed(c, 1, o, 1)
+            for o in range(4):
+                for c in range(2):
+                    self.landed(c, 1, o, 2)
+        return [s0, s1, s2, s3, s4, s5, s6, s7]
+
+    def drain(self):
+        for c in range(2):
+            for kind in range(3):
+                self.message(c, 0, 0, kind).wait_send()
+                for o in range(4):
+                    self.message(c, 1, o, kind).wait_send()
+
+
+class Column:
+    def __init__(self, view, send, recv):
+        self.prow, self.pcol = lax.axis_index("prow"), lax.axis_index("pcol")
+        self.z, self.core = self.prow // 2, lax.rem(self.prow, 2)
+        self.sign = 1 - 2 * self.core
+        self.raw, self.send, self.recv = view, send, recv
+
+    def message(self, kind):
+        part = self.raw(lax.rem(self.z + (-self.sign if kind == 2 else 0) + OFFS, 4), self.core)
+        to = lax.rem(self.z + (-self.sign if kind == 1 else self.sign) + OFFS, 4)
+        return pltpu.make_async_remote_copy(part, part, self.send.at[kind], self.recv.at[kind],
+                                            device_id=(to * 2 + self.core, self.pcol), device_id_type=MESH)
+
+    def landed(self, kind):
+        at = lax.rem(self.z + (-self.sign, self.sign, 2)[kind] + OFFS, 4)
+        part = self.raw(at, self.core)
+        pltpu.make_async_remote_copy(part, part, self.send.at[kind], self.recv.at[kind],
+                                     device_id=(self.prow, self.pcol), device_id_type=MESH).wait_recv()
+        return at
+
+    def drain(self):
+        for kind in range(3):
+            self.message(kind).wait_send()
 
 
 W = 2176
@@ -104,7 +222,7 @@
 
 
 def route_kernel(flat_ref, mine_ref, order_ref, rows_ref, cols_ref,
-                 send_a, got_a, send_b, got_b, piece_ref, ss, rs):
+                 send_a, got_a, send_b, got_b, piece_ref, ss, rs, ps, pr, zs, zr, xs, xr):
     prow, pcol = lax.axis_index("prow"), lax.axis_index("pcol")
     twin = (lax.rem(pcol, 8), prow + 8 * (pcol // 8))
     at_home = prow == lax.rem(pcol, 8)
@@ -151,14 +269,14 @@
     def b_copy(s):
         return copy(send_b.at[lax.rem(pcol + s, 16)], got_b.at[pcol], 7 + s - 1, along_pcol(s))
 
-    def row_copy(s):
-        return copy(piece_ref, slab(rows_ref, pcol, 32), 22 + s - 1, along_pcol(s))
-
     def twin_copy():
-        return copy(piece_ref, slab(cols_ref, twin[0], 32), 37, twin)
-
-    def col_copy(s):
-        return copy(slab(cols_ref, prow, 32), slab(cols_ref, prow, 32), 38 + s - 1, along_prow(s))
+        return copy(piece_ref, cols_ref.at[twin[0]], 22, twin)
+
+    def rows_view(colour, x, y):
+        return rows_ref.at[x, y, :, pl.ds(1152 * colour, 1152 if colour == 0 else 1024)]
+
+    def cols_view(z, core):
+        return cols_ref.at[z * 2 + core]
 
     for s in range(1, 8):
         a_copy(s).start()
@@ -186,36 +304,56 @@
     valid = got[:, 2048:].astype(F32)[:, 2:3] > 0.5
     piece = lax.dot_general(pick(earlier(valid), valid, 32), got, TT, preferred_element_type=F32).astype(BF16)
     piece_ref[...] = piece
-    rows_ref[pl.ds(pl.multiple_of(pcol * 32, 32), 32), :] = piece
+    rows_ref[pcol // 4, lax.rem(pcol, 4)] = piece
 
     @pl.when(at_home)
     def _():
-        cols_ref[pl.ds(pl.multiple_of(prow * 32, 32), 32), :] = piece
+        cols_ref[prow] = piece
 
     @pl.when(jnp.logical_not(at_home))
     def _():
         twin_copy().start()
-    for s in range(1, 16):
-        row_copy(s).start()
+    plane = Plane(rows_view, ps, pr, None)
+    column = Column(cols_view, zs, zr)
+    core = lax.rem(prow, 2)
+    other = prow + 1 - 2 * core
+
+    def across(n, z, whose):
+        part = cols_view(z, whose)
+        return pltpu.make_async_remote_copy(part, part, xs.at[n], xr.at[n], device_id=(other, pcol), device_id_type=MESH)
+    todo = plane.stages()
+    todo[0]()
+    todo[1]()
 
     @pl.when(jnp.logical_not(at_home))
     def _():
-        spot = slab(cols_ref, prow, 32)
-        copy(spot, spot, 37, twin).wait_recv()
-    for s in range(1, 8):
-        col_copy(s).start()
-    for s in range(1, 8):
-        spot = slab(cols_ref, lax.rem(prow + 8 - s, 8), 32)
-        copy(spot, spot, 38 + s - 1, along_prow(1)).wait_recv()
-    for s in range(1, 16):
-        spot = slab(rows_ref, lax.rem(pcol + 16 - s, 16), 32)
-        copy(spot, spot, 22 + s - 1, along_prow(1)).wait_recv()
+        copy(cols_ref.at[prow], cols_ref.at[prow], 22, twin).wait_recv()
+    column.message(0).start()
+    column.message(1).start()
+    across(0, prow // 2, core).start()
+    todo[2]()
+    todo[3]()
+    at = [prow // 2, column.landed(0)]
+    column.message(2).start()
+    across(1, at[1], core).start()
+    todo[4]()
+    at.append(column.landed(1))
+    across(2, at[2], core).start()
+    todo[5]()
+    at.append(column.landed(2))
+    across(3, at[3], core).start()
+    todo[6]()
+    todo[7]()
+    sign = 1 - 2 * core
+    for n, shift in enumerate((0, sign, -sign, 2)):
+        across(n, lax.rem(prow // 2 + shift + OFFS, 4), 1 - core).wait_recv()
+        across(n, at[n], core).wait_send()
+    plane.drain()
+    column.drain()
     for s in range(1, 8):
         a_copy(s).wait_send()
-        col_copy(s).wait_send()
     for s in range(1, 16):
         b_copy(s).wait_send()
-        row_copy(s).wait_send()
 
     @pl.when(jnp.logical_not(at_home))
     def _():
@@ -225,7 +363,7 @@
 def route(flat, mine, order):
     return pl.pallas_call(
         route_kernel,
-        out_shape=(jax.ShapeDtypeStruct((512, W), BF16), jax.ShapeDtypeStruct((256, W), BF16)),
+        out_shape=(jax.ShapeDtypeStruct((4, 4, 32, W), BF16), jax.ShapeDtypeStruct((8, 32, W), BF16)),
         in_specs=[pl.BlockSpec(memory_space=pltpu.VMEM)] * 3,
         out_specs=[pl.BlockSpec(memory_space=pltpu.VMEM)] * 2,
         scratch_shapes=[
@@ -234,29 +372,42 @@
             pltpu.VMEM((16, 8, W), BF16),
             pltpu.VMEM((16, 8, W), BF16),
             pltpu.VMEM((32, W), BF16),
-            pltpu.SemaphoreType.DMA((45,)),
-            pltpu.SemaphoreType.DMA((45,)),
+            pltpu.SemaphoreType.DMA((23,)),
+            pltpu.SemaphoreType.DMA((23,)),
+            pltpu.SemaphoreType.DMA((30,)),
+            pltpu.SemaphoreType.DMA((30,)),
+            pltpu.SemaphoreType.DMA((3,)),
+            pltpu.SemaphoreType.DMA((3,)),
+            pltpu.SemaphoreType.DMA((4,)),
+            pltpu.SemaphoreType.DMA((4,)),
         ],
         compiler_params=pltpu.CompilerParams(collective_id=1, has_side_effects=True, vmem_limit_bytes=24 << 20),
         name="route",
     )(flat, mine, order)
 
 
-def pair_kernel(rows_ref, cols_ref, mats_ref, local_ref, front_ref, out_ref, in_ref, x_ref, z_ref, own_sem, send, recv, psend, precv):
-    colors = COLORS
+def pair_kernel(rows_ref, cols_ref, mats_ref, local_ref, front_ref, out_ref, x_ref, z_ref, send, recv, zsend, zrecv, psend, precv):
     prow, pcol = lax.axis_index("prow"), lax.axis_index("pcol")
-    me = (pcol // 4, pcol % 4, prow // 2)
-    core = prow % 2
-
-    def device(dim, shift):
-        at = [lax.rem(v + shift + 4, 4) if d == dim else v for d, v in enumerate(me)]
-        return (at[2] * 2 + core, at[0] * 4 + at[1])
-    partner = (me[2] * 2 + 1 - core, pcol)
+    z, core = prow // 2, lax.rem(prow, 2)
+    other = (prow + 1 - 2 * core, pcol)
+
+    def tile_view(at, whose):
+        return out_ref.at[pcol // 4, lax.rem(pcol, 4), at, whose]
+
+    def block_view(colour, x, y):
+        return out_ref.at[x, y, :, core, pl.ds(32 * colour, 32)]
+
+    def across(colour, part, n):
+        return pltpu.make_async_remote_copy(part, part, psend.at[colour * 16 + n], precv.at[colour * 16 + n],
+                                            device_id=other, device_id_type=MESH)
+    plane = Plane(block_view, send, recv, lambda colour, part, n: across(colour, part, n).start())
+    column = Column(tile_view, zsend, zrecv)
     barrier = pltpu.get_barrier_semaphore()
-    for dim in range(3):
-        for shift in (1, -1):
-            pl.semaphore_signal(barrier, inc=1, device_id=device(dim, shift), device_id_type=MESH)
-    pl.semaphore_signal(barrier, inc=1, device_id=partner, device_id_type=MESH)
+    for step in (1, -1):
+        pl.semaphore_signal(barrier, inc=1, device_id=plane.peer(0, 0, step), device_id_type=MESH)
+        pl.semaphore_signal(barrier, inc=1, device_id=plane.peer(0, 1, step), device_id_type=MESH)
+        pl.semaphore_signal(barrier, inc=1, device_id=(lax.rem(z + step + OFFS, 4) * 2 + core, pcol), device_id_type=MESH)
+    pl.semaphore_signal(barrier, inc=1, device_id=other, device_id_type=MESH)
     depth = mats_ref.shape[0]
 
     def load(src, first, count, shift, at):
@@ -290,89 +441,38 @@
 
     load(cols_ref, 0, 64, 4, 512)
     load(rows_ref, 0, 128, 3, 0)
-    in_ref[...] = pair(512, 64, 0, 128)
-    own = pltpu.make_async_copy(in_ref, out_ref.at[me[0], me[1], me[2], core], own_sem)
-    own.start()
+    out_ref[pcol // 4, lax.rem(pcol, 4), z, core] = pair(512, 64, 0, 128)
     pl.semaphore_wait(barrier, 7)
-
-    def view(c, phase, shift, half, whose=core):
-        order = ORDERS[c]
-        (r0, rm, r1), (c0, c1) = colors[c]
-        at = list(me)
-        for j in range(phase):
-            at[order[j]] = slice(None)
-        at[order[phase]] = lax.rem(me[order[phase]] + shift + 4, 4)
-        rows = {0: (r0, rm), 1: (rm, r1), 2: (r0, r1)}[half]
-        return out_ref.at[at[0], at[1], at[2], whose, pl.ds(rows[0], rows[1] - rows[0]), pl.ds(c0, c1 - c0)]
-
-    def ring(c, phase, which):
-        dim = ORDERS[c][phase]
-        shift, half, to = ((0, 2, 1), (0, 2, -1), (-1, 0, 1), (1, 1, -1))[which]
-        src = view(c, phase, shift, half)
-        dst = src
-        if phase == 0 and which < 2:
-            (r0, rm, r1), (c0, c1) = colors[c]
-            src = in_ref.at[pl.ds(r0, r1 - r0), pl.ds(c0, c1 - c0)]
-        n = (c * 3 + phase) * 4 + which
-        return pltpu.make_async_remote_copy(src, dst, send.at[n], recv.at[n], device_id=device(dim, to), device_id_type=MESH)
-
-    def landed(c, phase, which):
-        dim = ORDERS[c][phase]
-        shift, half = ((-1, 2), (1, 2), (2, 0), (2, 1))[which]
-        got = view(c, phase, shift, half)
-        n = (c * 3 + phase) * 4 + which
-        pltpu.make_async_remote_copy(got, got, send.at[n], recv.at[n], device_id=device(dim, 1), device_id_type=MESH).wait_recv()
-
-    def across(c, which, whose):
-        shift, half = ((0, 2), (-1, 2), (1, 2), (2, 0), (2, 1))[which]
-        part = view(c, 2, shift, half, whose)
-        n = c * 5 + which
-        return pltpu.make_async_remote_copy(part, part, psend.at[n], precv.at[n], device_id=partner, device_id_type=MESH)
-
-    for c in range(3):
-        ring(c, 0, 0).start()
-        ring(c, 0, 1).start()
-    jobs = [
-        lambda: load(cols_ref, 64, 192, 4, 576),
-        lambda: load(rows_ref, 128, 384, 3, 128),
-        lambda: chunk(0),
-        lambda: chunk(128),
-        lambda: chunk(256),
-        lambda: chunk(384),
-    ]
-    for phase in range(3):
-        jobs[2 * phase]()
-        for c in range(3):
-            landed(c, phase, 0)
-            ring(c, phase, 2).start()
-            if phase == 2:
-                across(c, 1, core).start()
-            landed(c, phase, 1)
-            ring(c, phase, 3).start()
-            if phase == 2:
-                across(c, 2, core).start()
-        if phase == 0:
-            own.wait()
-        jobs[2 * phase + 1]()
-        for c in range(3):
-            landed(c, phase, 2)
-            if phase == 2:
-                across(c, 3, core).start()
-            landed(c, phase, 3)
-            if phase == 2:
-                across(c, 4, core).start()
-            else:
-                ring(c, phase + 1, 0).start()
-                ring(c, phase + 1, 1).start()
-                if phase == 1:
-                    across(c, 0, core).start()
-    for c in range(3):
-        for which in range(5):
-            across(c, which, core).wait_send()
-            across(c, which, 1 - core).wait_recv()
-        for phase in range(3):
-            for which in range(4):
-                ring(c, phase, which).wait_send()
+    column.message(0).start()
+    column.message(1).start()
+    load(cols_ref, 64, 192, 4, 576)
+    column.landed(0)
+    column.message(2).start()
+    column.landed(1)
+    load(rows_ref, 128, 384, 3, 128)
+    column.landed(2)
+    todo = plane.stages()
+    todo[0]()
+    for colour in range(2):
+        across(colour, plane.view(colour, 0, 0), 0).start()
+    for n in range(4):
+        chunk(128 * n)
+        todo[1 + n]()
+    for n in range(5, 8):
+        todo[n]()
+    plane.drain()
+    column.drain()
+    mirror = Plane(lambda colour, x, y: out_ref.at[x, y, :, 1 - core, pl.ds(32 * colour, 32)], send, recv, None)
+    for colour in range(2):
+        for n in range(16):
+            leg, o, kind = (0, 0, n - 1) if n < 4 else (1, (n - 4) // 3, (n - 4) % 3)
+            come = (-plane.sign, plane.sign, 2)[kind]
+            first, second = (0, 0) if n == 0 else ((come, 0) if leg == 0 else (plane.offs[o], come))
+            across(colour, plane.view(colour, first, second), n).wait_send()
+            come = (plane.sign, -plane.sign, 2)[kind]
+            hop = (0, plane.sign, -plane.sign, 2)[o]
+            first, second = (0, 0) if n == 0 else ((come, 0) if leg == 0 else (hop, come))
+            across(colour, mirror.view(colour, first, second), n).wait_recv()
 
 
 def pair_blocks(rows, cols, mats):
@@ -387,14 +487,14 @@
         in_specs=[pl.BlockSpec(memory_space=pltpu.VMEM)] * 3,
         out_specs=[pl.BlockSpec(memory_space=pltpu.VMEM)] * 3,
         scratch_shapes=[
-            pltpu.VMEM((NB, 128), F32),
             pltpu.VMEM((RANK, 768, d), BF16),
             pltpu.VMEM((RANK, 768, d), BF16),
-            pltpu.SemaphoreType.DMA,
-            pltpu.SemaphoreType.DMA((36,)),
-            pltpu.SemaphoreType.DMA((36,)),
-            pltpu.SemaphoreType.DMA((15,)),
-            pltpu.SemaphoreType.DMA((15,)),
+            pltpu.SemaphoreType.DMA((30,)),
+            pltpu.SemaphoreType.DMA((30,)),
+            pltpu.SemaphoreType.DMA((3,)),
+            pltpu.SemaphoreType.DMA((3,)),
+            pltpu.SemaphoreType.DMA((32,)),
+            pltpu.SemaphoreType.DMA((32,)),
         ],
         compiler_params=pltpu.CompilerParams(collective_id=2, has_side_effects=True, vmem_limit_bytes=40 << 20),
         name="pairs",
@@ -583,7 +683,7 @@
     order = placement.reshape(8, 16, rows_dev).transpose(1, 0, 2).reshape(16, 8 * rows_dev)
     rows, cols = route(flat, mine[None, :], order)
     mats = jnp.concatenate([x_factor, zinv_factor], axis=1)
-    local, front, tiles = pair_blocks(rows, cols, mats)
+    local, front, tiles = pair_blocks(rows.reshape(512, W), cols.reshape(256, W), mats)
     rest, inv_hi, inv_lo, low_hi, low_lo = factor(tiles.reshape(128, NB, 128), front, local[:128])
     return solve(rest, inv_hi, inv_lo, low_hi, low_lo, local)
 

time: 172 us -> 153 us (0.89)
  Pallas kernels: 166 us -> 147 us
    pallas_call x1, Pallas kernels: 55.6 us -> 46 us  [route(): pl.pallas_call(route_kernel, out_shape=(jax.ShapeDtypeStruct((4, 4, 32, W...]
    pallas_call x1, Pallas kernels: 46.8 us -> 38.3 us  [pair_blocks(): pl.pallas_call(pair_kernel, out_shape=(jax.ShapeDtypeStruct((512, 256), F...]
where the time goes in v4:
time: 153 us
  Pallas kernels  147 us (96%)
  local copies, waits for them, and re-layouts  2.6 us (2%)
  other arithmetic  2.18 us (1%)
    pallas_call x1, Pallas kernels, factor(): pl.pallas_call(factor_kernel, out_shape=(jax.ShapeDtypeStruct((KK, 768),...  54.7 us
    pallas_call x1, Pallas kernels, route(): pl.pallas_call(route_kernel, out_shape=(jax.ShapeDtypeStruct((4, 4, 32, W...  46 us
    pallas_call x1, Pallas kernels, pair_blocks(): pl.pallas_call(pair_kernel, out_shape=(jax.ShapeDtypeStruct((512, 256), F...  38.3 us
    pallas_call x1, Pallas kernels, solve(): pl.pallas_call(solve_kernel, out_shape=(jax.ShapeDtypeStruct((512, 256),...  8.35 us

profile of v4, /device:TPU:1, one launch (start us, length us, event | category | flops | bytes accessed | tf_op | source)
XLA Modules:
  0.0 152.8 jit_solution(12092316573522643700)
XLA Ops:
  0.6 0.8 dynamic-slice_bitcast_fusion
  1.4 0.1 select_convert_fusion
  1.5 0.8 reshape.42
  2.3 0.1 reshape.43.order_ref
  2.4 0.9 copy.11
  3.3 1.3 pad_maximum_fusion.mats_ref
  4.7 46.0 %route.1 = (bf16[4,4,32,2176]{3,2,1,0:T(8,128)(2,1)S(1)}, bf16[8,32,2176]{2,1,0:T(8,128)(2,1)S(1)}) custom-call(bf16[32,2176]{1,0:T(8,128)(2,1)S(1)} %pad_maximum_fusion.1.flat_ref, s32[1,32]{1,0:T(1,128)S(1)} %get-tuple-element.26.mine_ref, s32[16,256]{1,0:T(8,128)S(1)} %reshape.43.order_ref), custom_call_target="tpu_custom_call" | custom-call | tf_op jit(solution)/shard_map/route/pallas_call | solution.py:364
  50.6 38.3 %pairs.1 = (f32[512,256]{1,0:T(8,128)S(1)}, f32[64,512]{1,0:T(8,128)S(1)}, f32[4,4,4,2,64,128]{5,4,3,2,1,0:T(8,128)S(1)}) custom-call(bf16[512,2176]{1,0:T(8,128)(2,1)S(1)} %bitcast.10, bf16[256,2176]{1,0:T(8,128)(2,1)S(1)} %bitcast.11, bf16[512,1024]{1,0:T(8,128)(2,1)S(1)} %pad_maximum_fusion.mats_ref), custom_call_target="tpu_custom_call" | custom-call | tf_op jit(solution)/shard_map/pairs/pallas_call | solution.py:480
  88.9 54.7 %factor.1 = (f32[1024,768]{1,0:T(8,128)S(1)}, bf16[1024,128]{1,0:T(8,128)(2,1)S(1)}, bf16[1024,128]{1,0:T(8,128)(2,1)S(1)}, bf16[1024,1024]{1,0:T(8,128)(2,1)S(1)}, bf16[1024,1024]{1,0:T(8,128)(2,1)S(1)}) custom-call(f32[128,64,128]{2,1,0:T(8,128)S(1)} %bitcast.9, f32[64,512]{1,0:T(8,128)S(1)} %get-tuple-element.15.front_ref, f32[128,256]{1,0:T(8,128)S(1)} %slice.3.top_ref), custom_call_target="tpu_custom_call" | custom-call | tf_op jit(solution)/shard_map/factor/pallas_call | solution.py:609
  143.7 8.3 %solve.1 = (f32[512,256]{1,0:T(8,128)}, f32[512,64]{1,0:T(8,128)S(1)}) custom-call(f32[1024,768]{1,0:T(8,128)S(1)} %get-tuple-element.17.rest_ref, bf16[1024,128]{1,0:T(8,128)(2,1)S(1)} %get-tuple-element.18.inv_hi_ref, bf16[1024,128]{1,0:T(8,128)(2,1)S(1)} %get-tuple-element.19.inv_lo_ref, bf16[1024,1024]{1,0:T(8,128)(2,1)S(1)} %get-tuple-element.20.low_hi_ref, ...), custom_call_target="tpu_custom_call" | custom-call | tf_op jit(solution)/shard_map/solve/pallas_call | solution.py:665
  152.0 0.8 copy.10
  (5 shorter events, 0.1 us)

commit v5 on v4

--- a/solution.py
+++ b/solution.py
@@ -26,56 +26,60 @@
     return jnp.broadcast_to(v, (8, 128))
 
 
-def invert_block(block_ref, inv_ref):
+def invert_block(block_ref, inv_ref, tmp_ref):
     lane = lax.broadcasted_iota(jnp.int32, (8, 128), 1)
     sub = lax.broadcasted_iota(jnp.int32, (8, 128), 0)
     rows = [block_ref[8 * i:8 * i + 8, :] for i in range(16)]
-    aug = [(lane == sub + 8 * i).astype(F32) for i in range(16)]
     for j in range(16):
-        mine, extra = rows[j], aug[j]
-        cols = [spread(mine[:, 8 * j + q:8 * j + q + 1]) for q in range(8)]
+        here = (lane >= 8 * j) & (lane < 8 * j + 8)
+        mine = rows[j]
+        spot = 72 * (j % 2)
+        for q in range(8):
+            tmp_ref[spot + 8 * q:spot + 8 * q + 8, :] = spread(mine[:, 8 * j + q:8 * j + q + 1])
+        tmp_ref[spot + 64:spot + 72, :] = jnp.where(here, (lane == sub + 8 * j).astype(F32), mine)
         a = [[None] * 8 for _ in range(8)]
         for q in range(8):
             for s in range(q, 8):
-                a[s][q] = spread(cols[q][s:s + 1, :])
-        r = [spread(mine[t:t + 1, :]) for t in range(8)] if j < 15 else None
-        e = [spread(extra[t:t + 1, :]) for t in range(8)]
-        rinv = [None] * 8
-        low = [[None] * 8 for _ in range(8)]
-        for t in range(8):
-            rinv[t] = 1.0 / a[t][t]
-            for s in range(t + 1, 8):
-                low[s][t] = a[s][t] * rinv[t]
-            for s in range(t + 1, 8):
-                for k in range(t + 1, s + 1):
-                    a[s][k] = a[s][k] - low[s][t] * a[k][t]
-            for s in range(t + 1, 8):
-                if r is not None:
-                    r[s] = r[s] - low[s][t] * r[t]
-                e[s] = e[s] - low[s][t] * e[t]
-        packed_d = a[0][0]
-        packed_e = e[0]
+                a[s][q] = tmp_ref[pl.ds(spot + 8 * q + s, 8, stride=0), :]
+        r = [tmp_ref[pl.ds(spot + 64 + t, 8, stride=0), :] for t in range(8)]
+        pivots, low = [], []
+        for t in range(0, 8, 2):
+            u = t + 1
+            det = a[t][t] * a[u][u] - a[u][t] * a[u][t]
+            inv_det = 1.0 / det
+            p00, p01, p11 = a[u][u] * inv_det, -a[u][t] * inv_det, a[t][t] * inv_det
+            pivots.append((p00, p01, p11, a[t][t], a[u][t], det))
+            m = [[None] * 2 for _ in range(8)]
+            for s in range(t + 2, 8):
+                m[s][0] = a[s][t] * p00 + a[s][u] * p01
+                m[s][1] = a[s][t] * p01 + a[s][u] * p11
+            for s in range(t + 2, 8):
+                for k in range(t + 2, s + 1):
+                    a[s][k] = a[s][k] - (m[s][0] * a[k][t] + m[s][1] * a[k][u])
+                r[s] = r[s] - (m[s][0] * r[t] + m[s][1] * r[u])
+            low.append(m)
+        packed, packed_d = r[0], pivots[0][3]
         for t in range(1, 8):
-            packed_d = jnp.where(sub == t, a[t][t], packed_d)
-            packed_e = jnp.where(sub == t, e[t], packed_e)
-        inv_ref[8 * j:8 * j + 8, :] = packed_e * lax.rsqrt(packed_d)
+            p00, p01, p11, a00, a10, det = pivots[t // 2]
+            row = a00 * r[t] - a10 * r[t - 1] if t % 2 else r[t]
+            packed = jnp.where(sub == t, row, packed)
+            packed_d = jnp.where(sub == t, a00 * det if t % 2 else a00, packed_d)
+        inv_ref[8 * j:8 * j + 8, :] = jnp.where(lane < 8 * j + 8, packed * lax.rsqrt(packed_d), 0.0)
         if j == 15:
             break
-        w = [r[t] * rinv[t] for t in range(8)]
-        we = [e[t] * rinv[t] for t in range(8)]
-        for s in range(7, 0, -1):
-            for t in range(s):
-                w[t] = w[t] - low[s][t] * w[s]
-                we[t] = we[t] - low[s][t] * we[s]
+        w = [None] * 8
+        for t in (6, 4, 2, 0):
+            p00, p01, p11 = pivots[t // 2][:3]
+            w[t] = r[t] * p00 + r[t + 1] * p01
+            w[t + 1] = r[t] * p01 + r[t + 1] * p11
+            for s in range(t + 2, 8):
+                w[t] = w[t] - low[t // 2][s][0] * w[s]
+                w[t + 1] = w[t + 1] - low[t // 2][s][1] * w[s]
         for i in range(j + 1, 16):
-            c = [spread(rows[i][:, 8 * j + q:8 * j + q + 1]) for q in range(8)]
-            acc = c[0] * w[0]
-            acce = c[0] * we[0]
-            for q in range(1, 8):
-                acc = acc + c[q] * w[q]
-                acce = acce + c[q] * we[q]
-            rows[i] = rows[i] - acc
-            aug[i] = aug[i] - acce
+            acc = jnp.where(here, 0.0, rows[i])
+            for q in range(8):
+                acc = acc - spread(rows[i][:, 8 * j + q:8 * j + q + 1]) * w[q]
+            rows[i] = acc
 
 
 OFFS = 4
@@ -502,7 +506,7 @@
 
 
 def factor_kernel(tiles_ref, front_ref, top_ref, rest_ref, inv_hi_ref, inv_lo_ref, low_hi_ref, low_lo_ref,
-                  a_ref, diag_ref, inv_ref, pcat_ref, qcat_ref, icat_ref, own_sem, send, recv):
+                  a_ref, diag_ref, inv_ref, tmp_ref, pcat_ref, qcat_ref, icat_ref, own_sem, send, recv):
     prow, pcol = lax.axis_index("prow"), lax.axis_index("pcol")
     barrier = pltpu.get_barrier_semaphore()
     for s in range(1, 16):
@@ -552,7 +556,7 @@
     def step(j, carry):
         off = pl.multiple_of(j * 128, 128)
         diag_ref[...] = a_ref[pl.ds(off, 128), pl.ds(off, 128)]
-        invert_block(diag_ref, inv_ref)
+        invert_block(diag_ref, inv_ref, tmp_ref)
         hi, lo = split(inv_ref[...])
         inv_hi_ref[pl.ds(off, 128), :] = hi
         inv_lo_ref[pl.ds(off, 128), :] = lo
@@ -621,6 +625,7 @@
             pltpu.VMEM((KK, KK), F32),
             pltpu.VMEM((128, 128), F32),
             pltpu.VMEM((128, 128), F32),
+            pltpu.VMEM((144, 128), F32),
             pltpu.VMEM((KK, 384), BF16),
             pltpu.VMEM((KK, 384), BF16),
             pltpu.VMEM((128, 384), BF16),

time: 153 us -> 147 us (0.961)
  the two profiles are of different devices: /device:TPU:1 before, /device:TPU:28 now
where the time goes in v5:
time: 147 us
  Pallas kernels  142 us (97%)
  local copies, waits for them, and re-layouts  2.6 us (2%)
  other arithmetic  2.18 us (1%)
    pallas_call x1, Pallas kernels, factor(): pl.pallas_call(factor_kernel, out_shape=(jax.ShapeDtypeStruct((KK, 768),...  54.2 us
    pallas_call x1, Pallas kernels, route(): pl.pallas_call(route_kernel, out_shape=(jax.ShapeDtypeStruct((4, 4, 32, W...  41.9 us
    pallas_call x1, Pallas kernels, pair_blocks(): pl.pallas_call(pair_kernel, out_shape=(jax.ShapeDtypeStruct((512, 256), F...  37.2 us
    pallas_call x1, Pallas kernels, solve(): pl.pallas_call(solve_kernel, out_shape=(jax.ShapeDtypeStruct((512, 256),...  8.35 us

profile of v5, /device:TPU:28, one launch (start us, length us, event | category | flops | bytes accessed | tf_op | source)
XLA Modules:
  0.0 147.1 jit_solution(14636888359341536175)
XLA Ops:
  0.6 0.8 dynamic-slice_bitcast_fusion
  1.4 0.1 select_convert_fusion
  1.5 0.8 reshape.42
  2.3 0.1 reshape.43.order_ref
  2.4 0.9 copy.11
  3.3 1.3 pad_maximum_fusion.mats_ref
  4.7 41.9 %route.1 = (bf16[4,4,32,2176]{3,2,1,0:T(8,128)(2,1)S(1)}, bf16[8,32,2176]{2,1,0:T(8,128)(2,1)S(1)}) custom-call(bf16[32,2176]{1,0:T(8,128)(2,1)S(1)} %pad_maximum_fusion.1.flat_ref, s32[1,32]{1,0:T(1,128)S(1)} %get-tuple-element.26.mine_ref, s32[16,256]{1,0:T(8,128)S(1)} %reshape.43.order_ref), custom_call_target="tpu_custom_call" | custom-call | tf_op jit(solution)/shard_map/route/pallas_call | solution.py:368
  46.6 37.2 %pairs.1 = (f32[512,256]{1,0:T(8,128)S(1)}, f32[64,512]{1,0:T(8,128)S(1)}, f32[4,4,4,2,64,128]{5,4,3,2,1,0:T(8,128)S(1)}) custom-call(bf16[512,2176]{1,0:T(8,128)(2,1)S(1)} %bitcast.10, bf16[256,2176]{1,0:T(8,128)(2,1)S(1)} %bitcast.11, bf16[512,1024]{1,0:T(8,128)(2,1)S(1)} %pad_maximum_fusion.mats_ref), custom_call_target="tpu_custom_call" | custom-call | tf_op jit(solution)/shard_map/pairs/pallas_call | solution.py:484
  83.8 54.2 %factor.1 = (f32[1024,768]{1,0:T(8,128)S(1)}, bf16[1024,128]{1,0:T(8,128)(2,1)S(1)}, bf16[1024,128]{1,0:T(8,128)(2,1)S(1)}, bf16[1024,1024]{1,0:T(8,128)(2,1)S(1)}, bf16[1024,1024]{1,0:T(8,128)(2,1)S(1)}) custom-call(f32[128,64,128]{2,1,0:T(8,128)S(1)} %bitcast.9, f32[64,512]{1,0:T(8,128)S(1)} %get-tuple-element.15.front_ref, f32[128,256]{1,0:T(8,128)S(1)} %slice.3.top_ref), custom_call_target="tpu_custom_call" | custom-call | tf_op jit(solution)/shard_map/factor/pallas_call | solution.py:613
  138.0 8.4 %solve.1 = (f32[512,256]{1,0:T(8,128)}, f32[512,64]{1,0:T(8,128)S(1)}) custom-call(f32[1024,768]{1,0:T(8,128)S(1)} %get-tuple-element.17.rest_ref, bf16[1024,128]{1,0:T(8,128)(2,1)S(1)} %get-tuple-element.18.inv_hi_ref, bf16[1024,128]{1,0:T(8,128)(2,1)S(1)} %get-tuple-element.19.inv_lo_ref, bf16[1024,1024]{1,0:T(8,128)(2,1)S(1)} %get-tuple-element.20.low_hi_ref, ...), custom_call_target="tpu_custom_call" | custom-call | tf_op jit(solution)/shard_map/solve/pallas_call | solution.py:670
  146.3 0.8 copy.10
  (5 shorter events, 0.1 us)

commit v6 on v5

--- a/solution.py
+++ b/solution.py
@@ -225,7 +225,7 @@
     return hit.astype(F32).astype(BF16)
 
 
-def route_kernel(flat_ref, mine_ref, order_ref, rows_ref, cols_ref,
+def route_kernel(factors_ref, placed_ref, rows_ref, cols_ref,
                  send_a, got_a, send_b, got_b, piece_ref, ss, rs, ps, pr, zs, zr, xs, xr):
     prow, pcol = lax.axis_index("prow"), lax.axis_index("pcol")
     twin = (lax.rem(pcol, 8), prow + 8 * (pcol // 8))
@@ -240,17 +240,29 @@
     def _():
         pl.semaphore_signal(barrier, inc=1, device_id=twin, device_id_type=MESH)
 
-    group = (mine_ref[...] >> 6) & 7
+    device = prow * 16 + pcol
+    line = jnp.broadcast_to(placed_ref[pl.ds(device // 4, 1), :], (8, 128))
+    mine = pltpu.roll(line, lax.rem(4 - lax.rem(device, 4), 4) * 32, 1)[0:1, :32]
+    group = (mine >> 6) & 7
     row = lax.broadcasted_iota(jnp.int32, (64, 32), 0)
     match = group == (row >> 3)
     ahead = (lax.broadcasted_iota(jnp.int32, (32, 32), 0) < lax.broadcasted_iota(jnp.int32, (32, 32), 1)).astype(BF16)
     rank = jnp.dot(match.astype(F32).astype(BF16), ahead, preferred_element_type=F32).astype(jnp.int32)
-    sel = (match & (rank == (row & 7))).astype(F32).astype(BF16)
-    send_a[...] = jnp.dot(sel, flat_ref[...], preferred_element_type=F32).reshape(8, 8, W).astype(BF16)
+    chosen = match & (rank == (row & 7))
+    sel = chosen.astype(F32).astype(BF16)
+    for r in range(RANK):
+        send_a[:, :, 512 * r:512 * r + 512] = jnp.dot(sel, factors_ref[r], preferred_element_type=F32).reshape(8, 8, 512).astype(BF16)
+
+    def total(v):
+        return jnp.sum(jnp.where(chosen, v.astype(F32), 0.0), axis=1, keepdims=True)
+    lane = lax.broadcasted_iota(jnp.int32, (64, 128), 1)
+    tags = jnp.where(lane == 0, total(mine >> 6), jnp.where(lane == 1, total(mine & 63), jnp.where(lane == 2, total(mine * 0 + 1), 0.0)))
+    send_a[:, :, 2048:] = tags.reshape(8, 8, 128).astype(BF16)
     got_a[prow] = send_a[prow]
 
-    kind = (order_ref[...] >> 6) & 15
-    prior = lax.broadcasted_iota(jnp.int32, kind.shape, 0) < pcol
+    kind = (placed_ref[...] >> 6) & 15
+    spot = lax.broadcasted_iota(jnp.int32, kind.shape, 0) * 4 + (lax.broadcasted_iota(jnp.int32, kind.shape, 1) >> 5)
+    prior = (spot & 15) < pcol
     base = [jnp.sum((prior & (kind == prow + 8 * h)).astype(F32), keepdims=True).astype(jnp.int32) for h in range(2)]
 
     pl.semaphore_wait(barrier, jnp.where(at_home, 22, 23))
@@ -364,11 +376,11 @@
         twin_copy().wait_send()
 
 
-def route(flat, mine, order):
+def route(factors, placed):
     return pl.pallas_call(
         route_kernel,
         out_shape=(jax.ShapeDtypeStruct((4, 4, 32, W), BF16), jax.ShapeDtypeStruct((8, 32, W), BF16)),
-        in_specs=[pl.BlockSpec(memory_space=pltpu.VMEM)] * 3,
+        in_specs=[pl.BlockSpec(memory_space=pltpu.VMEM)] * 2,
         out_specs=[pl.BlockSpec(memory_space=pltpu.VMEM)] * 2,
         scratch_shapes=[
             pltpu.VMEM((8, 8, W), BF16),
@@ -387,10 +399,10 @@
         ],
         compiler_params=pltpu.CompilerParams(collective_id=1, has_side_effects=True, vmem_limit_bytes=24 << 20),
         name="route",
-    )(flat, mine, order)
-
-
-def pair_kernel(rows_ref, cols_ref, mats_ref, local_ref, front_ref, out_ref, x_ref, z_ref, send, recv, zsend, zrecv, psend, precv):
+    )(factors, placed)
+
+
+def pair_kernel(rows_ref, cols_ref, xf_ref, zf_ref, local_ref, front_ref, out_ref, x_ref, z_ref, send, recv, zsend, zrecv, psend, precv):
     prow, pcol = lax.axis_index("prow"), lax.axis_index("pcol")
     z, core = prow // 2, lax.rem(prow, 2)
     other = (prow + 1 - 2 * core, pcol)
@@ -412,16 +424,16 @@
         pl.semaphore_signal(barrier, inc=1, device_id=plane.peer(0, 1, step), device_id_type=MESH)
         pl.semaphore_signal(barrier, inc=1, device_id=(lax.rem(z + step + OFFS, 4) * 2 + core, pcol), device_id_type=MESH)
     pl.semaphore_signal(barrier, inc=1, device_id=other, device_id_type=MESH)
-    depth = mats_ref.shape[0]
+    depth = xf_ref.shape[0]
 
     def load(src, first, count, shift, at):
         tags = src[:, 2048:].astype(F32).astype(jnp.int32)
         spot = (tags[:, 0:1] >> shift) * NB + tags[:, 1:2] - first
         rows = lax.dot_general(pick(spot, None, count), src[:, :2048], TT, preferred_element_type=F32).astype(BF16)
         for r in range(RANK):
-            images = jnp.dot(rows[:, r * depth:(r + 1) * depth], mats_ref[...], preferred_element_type=F32).astype(BF16)
-            x_ref[r, at:at + count, :] = images[:, :depth]
-            z_ref[r, at:at + count, :] = images[:, depth:]
+            mine = rows[:, r * depth:(r + 1) * depth]
+            x_ref[r, at:at + count, :] = jnp.dot(mine, xf_ref[...], preferred_element_type=F32).astype(BF16)
+            z_ref[r, at:at + count, :] = jnp.dot(mine, zf_ref[...], preferred_element_type=F32).astype(BF16)
 
     def pair(base, m, other, n):
         acc = None
@@ -479,8 +491,8 @@
             across(colour, mirror.view(colour, first, second), n).wait_recv()
 
 
-def pair_blocks(rows, cols, mats):
-    d = mats.shape[0]
+def pair_blocks(rows, cols, x_factor, z_factor):
+    d = x_factor.shape[0]
     return pl.pallas_call(
         pair_kernel,
         out_shape=(
@@ -488,7 +500,7 @@
             jax.ShapeDtypeStruct((NB, 512), F32),
             jax.ShapeDtypeStruct((4, 4, 4, 2, NB, 128), F32),
         ),
-        in_specs=[pl.BlockSpec(memory_space=pltpu.VMEM)] * 3,
+        in_specs=[pl.BlockSpec(memory_space=pltpu.VMEM)] * 4,
         out_specs=[pl.BlockSpec(memory_space=pltpu.VMEM)] * 3,
         scratch_shapes=[
             pltpu.VMEM((RANK, 768, d), BF16),
@@ -502,45 +514,36 @@
         ],
         compiler_params=pltpu.CompilerParams(collective_id=2, has_side_effects=True, vmem_limit_bytes=40 << 20),
         name="pairs",
-    )(rows, cols, mats)
+    )(rows, cols, x_factor, z_factor)
 
 
 def factor_kernel(tiles_ref, front_ref, top_ref, rest_ref, inv_hi_ref, inv_lo_ref, low_hi_ref, low_lo_ref,
-                  a_ref, diag_ref, inv_ref, tmp_ref, pcat_ref, qcat_ref, icat_ref, own_sem, send, recv):
+                  a_ref, diag_ref, inv_ref, tmp_ref, pcat_ref, qcat_ref, icat_ref, send, recv, ps, pr):
     prow, pcol = lax.axis_index("prow"), lax.axis_index("pcol")
+
+    def front_view(colour, x, y):
+        return rest_ref.at[pl.ds(pl.multiple_of((x * 4 + y) * NB, NB), NB), pl.ds(256 * colour, 256)]
+
+    def top_place(p, h):
+        return rest_ref.at[pl.ds(pl.multiple_of(h * 512 + p * NB, NB), NB), pl.ds(512, 256)]
+
+    plane = Plane(front_view, ps, pr, None)
+    todo = plane.stages()
     barrier = pltpu.get_barrier_semaphore()
-    for s in range(1, 16):
-        pl.semaphore_signal(barrier, inc=1, device_id=(prow, lax.rem(pcol + s, 16)), device_id_type=MESH)
+    for leg in range(2):
+        for step in (1, -1):
+            pl.semaphore_signal(barrier, inc=1, device_id=plane.peer(0, leg, step), device_id_type=MESH)
     for s in range(1, 8):
         pl.semaphore_signal(barrier, inc=1, device_id=(lax.rem(prow + s, 8), pcol), device_id_type=MESH)
-    pl.semaphore_wait(barrier, 22)
-
-    def front_place(c):
-        return rest_ref.at[pl.ds(pl.multiple_of(c * NB, NB), NB), pl.ds(0, 512)]
-
-    def top_place(p, h):
-        return rest_ref.at[pl.ds(pl.multiple_of(h * 512 + p * NB, NB), NB), pl.ds(512, 256)]
-
-    def front_copy(s):
-        return pltpu.make_async_remote_copy(
-            front_ref, front_place(pcol), send.at[s - 1], recv.at[s - 1],
-            device_id=(prow, lax.rem(pcol + s, 16)), device_id_type=MESH)
+    rest_ref[pl.ds(pl.multiple_of(pcol * NB, NB), NB), 0:512] = front_ref[...]
+    for h in range(2):
+        rest_ref[pl.ds(pl.multiple_of(h * 512 + prow * NB, NB), NB), 512:768] = top_ref[h * NB:h * NB + NB]
 
     def top_copy(s, h):
-        n = 15 + (s - 1) * 2 + h
+        n = (s - 1) * 2 + h
         return pltpu.make_async_remote_copy(
             top_ref.at[pl.ds(h * NB, NB)], top_place(prow, h), send.at[n], recv.at[n],
             device_id=(lax.rem(prow + s, 8), pcol), device_id_type=MESH)
-    own = [pltpu.make_async_copy(front_ref, front_place(pcol), own_sem.at[0])]
-    for h in range(2):
-        own.append(pltpu.make_async_copy(top_ref.at[pl.ds(h * NB, NB)], top_place(prow, h), own_sem.at[1 + h]))
-    for c in own:
-        c.start()
-    for s in range(1, 16):
-        front_copy(s).start()
-    for s in range(1, 8):
-        for h in range(2):
-            top_copy(s, h).start()
 
     left = lax.broadcasted_iota(jnp.int32, (NB, 128), 1) < NB
 
@@ -552,8 +555,16 @@
             a_ref[at, 512 + 128 * k:640 + 128 * k] = jnp.where(left, pltpu.roll(even, NB, 1), odd)
         return carry
     lax.fori_loop(0, 16, fill, 0)
+    pl.semaphore_wait(barrier, 11)
+    for s in range(1, 8):
+        for h in range(2):
+            top_copy(s, h).start()
 
     def step(j, carry):
+        for n in range(8):
+            @pl.when(j == n)
+            def _(n=n):
+                todo[n]()
         off = pl.multiple_of(j * 128, 128)
         diag_ref[...] = a_ref[pl.ds(off, 128), pl.ds(off, 128)]
         invert_block(diag_ref, inv_ref, tmp_ref)
@@ -593,16 +604,10 @@
         lax.fori_loop(first, KK // 256, update, 0)
         return carry
     lax.fori_loop(0, KK // 128, step, 0)
-    for c in own:
-        c.wait()
-    for s in range(1, 16):
-        front_copy(s).wait_send()
-        place = front_place(lax.rem(pcol + 16 - s, 16))
-        pltpu.make_async_remote_copy(place, place, send.at[s - 1], recv.at[s - 1],
-                                     device_id=(prow, pcol), device_id_type=MESH).wait_recv()
+    plane.drain()
     for s in range(1, 8):
         for h in range(2):
-            n = 15 + (s - 1) * 2 + h
+            n = (s - 1) * 2 + h
             top_copy(s, h).wait_send()
             place = top_place(lax.rem(prow + 8 - s, 8), h)
             pltpu.make_async_remote_copy(place, place, send.at[n], recv.at[n],
@@ -629,9 +634,10 @@
             pltpu.VMEM((KK, 384), BF16),
             pltpu.VMEM((KK, 384), BF16),
             pltpu.VMEM((128, 384), BF16),
-            pltpu.SemaphoreType.DMA((3,)),
-            pltpu.SemaphoreType.DMA((29,)),
-            pltpu.SemaphoreType.DMA((29,)),
+            pltpu.SemaphoreType.DMA((14,)),
+            pltpu.SemaphoreType.DMA((14,)),
+            pltpu.SemaphoreType.DMA((30,)),
+            pltpu.SemaphoreType.DMA((30,)),
         ],
         compiler_params=pltpu.CompilerParams(collective_id=3, has_side_effects=True, vmem_limit_bytes=40 << 20),
         name="factor",
@@ -679,16 +685,8 @@
 
 
 def per_device(factors, x_factor, zinv_factor, placement):
-    rows_dev = factors.shape[1]
-    prow, pcol = lax.axis_index("prow"), lax.axis_index("pcol")
-    mine = lax.dynamic_slice_in_dim(placement, (prow * 16 + pcol) * rows_dev, rows_dev)
-    lane = jnp.arange(128)[None, :]
-    tags = jnp.where(lane == 0, (mine >> 6)[:, None], jnp.where(lane == 1, (mine & 63)[:, None], (lane == 2).astype(jnp.int32)))
-    flat = jnp.concatenate([factors.transpose(1, 0, 2).reshape(rows_dev, -1), tags.astype(BF16)], axis=1)
-    order = placement.reshape(8, 16, rows_dev).transpose(1, 0, 2).reshape(16, 8 * rows_dev)
-    rows, cols = route(flat, mine[None, :], order)
-    mats = jnp.concatenate([x_factor, zinv_factor], axis=1)
-    local, front, tiles = pair_blocks(rows.reshape(512, W), cols.reshape(256, W), mats)
+    rows, cols = route(factors, placement.reshape(32, 128))
+    local, front, tiles = pair_blocks(rows.reshape(512, W), cols.reshape(256, W), x_factor, zinv_factor)
     rest, inv_hi, inv_lo, low_hi, low_lo = factor(tiles.reshape(128, NB, 128), front, local[:128])
     return solve(rest, inv_hi, inv_lo, low_hi, low_lo, local)
 

time: 147 us -> 139 us (0.946)
  the two profiles are of different devices: /device:TPU:28 before, /device:TPU:1 now
where the time goes in v6:
time: 139 us
  Pallas kernels  134 us (96%)
  local copies, waits for them, and re-layouts  4.47 us (3%)
    pallas_call x1, Pallas kernels, route(): pl.pallas_call(route_kernel, out_shape=(jax.ShapeDtypeStruct((4, 4, 32, W...  45.8 us
    pallas_call x1, Pallas kernels, factor(): pl.pallas_call(factor_kernel, out_shape=(jax.ShapeDtypeStruct((KK, 768),...  42 us
    pallas_call x1, Pallas kernels, pair_blocks(): pl.pallas_call(pair_kernel, out_shape=(jax.ShapeDtypeStruct((512, 256), F...  37.9 us
    pallas_call x1, Pallas kernels, solve(): pl.pallas_call(solve_kernel, out_shape=(jax.ShapeDtypeStruct((512, 256),...  8.35 us
    unnamed x8, local copies, waits for them, and re-layouts  3.69 us

profile of v6, /device:TPU:1, one launch (start us, length us, event | category | flops | bytes accessed | tf_op | source)
XLA Modules:
  0.0 139.2 jit_solution(1285650897427851490)
XLA Ops:
  0.6 0.0 copy-start.2
  0.6 0.9 copy-done.2
  1.5 0.0 copy-start.3
  1.5 0.7 copy-done.3
  2.3 45.8 %route.1 = (bf16[4,4,32,2176]{3,2,1,0:T(8,128)(2,1)S(1)}, bf16[8,32,2176]{2,1,0:T(8,128)(2,1)S(1)}) custom-call(bf16[4,32,512]{2,1,0:T(8,128)(2,1)S(1)} %copy-done.2, s32[32,128]{1,0:T(8,128)S(1)} %bitcast.7), custom_call_target="tpu_custom_call" | custom-call | tf_op jit(solution)/shard_map/route/pallas_call | solution.py:380
  48.1 0.0 copy-start
  48.1 1.0 copy-done
  49.1 0.0 copy-start.1
  49.1 1.0 copy-done.1
  50.2 37.9 %pairs.1 = (f32[512,256]{1,0:T(8,128)S(1)}, f32[64,512]{1,0:T(8,128)S(1)}, f32[4,4,4,2,64,128]{5,4,3,2,1,0:T(8,128)S(1)}) custom-call(bf16[512,2176]{1,0:T(8,128)(2,1)S(1)} %bitcast.5, bf16[256,2176]{1,0:T(8,128)(2,1)S(1)} %bitcast.6, bf16[512,512]{1,0:T(8,128)(2,1)S(1)} %copy-done, bf16[512,512]{1,0:T(8,128)(2,1)S(1)} %copy-done.1), custom_call_target="tpu_custom_call" | custom-call | tf_op jit(solution)/shard_map/pairs/pallas_call | solution.py:496
  88.1 42.0 %factor.1 = (f32[1024,768]{1,0:T(8,128)S(1)}, bf16[1024,128]{1,0:T(8,128)(2,1)S(1)}, bf16[1024,128]{1,0:T(8,128)(2,1)S(1)}, bf16[1024,1024]{1,0:T(8,128)(2,1)S(1)}, bf16[1024,1024]{1,0:T(8,128)(2,1)S(1)}) custom-call(f32[128,64,128]{2,1,0:T(8,128)S(1)} %bitcast.4, f32[64,512]{1,0:T(8,128)S(1)} %get-tuple-element.15.front_ref, f32[128,256]{1,0:T(8,128)S(1)} %slice.3.top_ref), custom_call_target="tpu_custom_call" | custom-call | tf_op jit(solution)/shard_map/factor/pallas_call | solution.py:618
  130.0 8.4 %solve.1 = (f32[512,256]{1,0:T(8,128)}, f32[512,64]{1,0:T(8,128)S(1)}) custom-call(f32[1024,768]{1,0:T(8,128)S(1)} %get-tuple-element.17.rest_ref, bf16[1024,128]{1,0:T(8,128)(2,1)S(1)} %get-tuple-element.18.inv_hi_ref, bf16[1024,128]{1,0:T(8,128)(2,1)S(1)} %get-tuple-element.19.inv_lo_ref, bf16[1024,1024]{1,0:T(8,128)(2,1)S(1)} %get-tuple-element.20.low_hi_ref, ...), custom_call_target="tpu_custom_call" | custom-call | tf_op jit(solution)/shard_map/solve/pallas_call | solution.py:676
  138.4 0.8 copy.6
  (1 shorter events, 0.0 us)
Async XLA Ops:
  0.6 0.9 copy-start.2
  1.5 0.7 copy-start.3
  48.1 1.0 copy-start
  49.1 1.0 copy-start.1

commit v7 on v6

--- a/solution.py
+++ b/solution.py
@@ -430,30 +430,34 @@
         tags = src[:, 2048:].astype(F32).astype(jnp.int32)
         spot = (tags[:, 0:1] >> shift) * NB + tags[:, 1:2] - first
         rows = lax.dot_general(pick(spot, None, count), src[:, :2048], TT, preferred_element_type=F32).astype(BF16)
-        for r in range(RANK):
-            mine = rows[:, r * depth:(r + 1) * depth]
-            x_ref[r, at:at + count, :] = jnp.dot(mine, xf_ref[...], preferred_element_type=F32).astype(BF16)
-            z_ref[r, at:at + count, :] = jnp.dot(mine, zf_ref[...], preferred_element_type=F32).astype(BF16)
+        stack = jnp.concatenate([rows[:, r * depth:(r + 1) * depth] for r in range(RANK)], axis=0)
+        for dst, mat in ((x_ref, xf_ref), (z_ref, zf_ref)):
+            images = jnp.dot(stack, mat[...], preferred_element_type=F32).astype(BF16)
+            for r in range(RANK):
+                dst[r, at:at + count, :] = images[r * count:(r + 1) * count, :]
 
     def pair(base, m, other, n):
         acc = None
-        for r in range(RANK):
-            for q in range(RANK):
-                inner_x = lax.dot_general(x_ref[r, base:base + m, :], x_ref[q, other:other + n, :], TN, preferred_element_type=F32)
-                inner_z = lax.dot_general(z_ref[r, base:base + m, :], z_ref[q, other:other + n, :], TN, preferred_element_type=F32)
-                term = inner_x * inner_z
-                if acc is None:
-                    acc = term
-                elif SIGNS[r] * SIGNS[q] > 0:
-                    acc = acc + term
-                else:
-                    acc = acc - term
+        for q in range(RANK):
+            left_x = jnp.concatenate([x_ref[r, base:base + m, :] for r in range(RANK)], axis=0)
+            left_z = jnp.concatenate([z_ref[r, base:base + m, :] for r in range(RANK)], axis=0)
+            term = (lax.dot_general(left_x, x_ref[q, other:other + n, :], TN, preferred_element_type=F32)
+                    * lax.dot_general(left_z, z_ref[q, other:other + n, :], TN, preferred_element_type=F32))
+            term = (term[:m] + term[m:2 * m]) - (term[2 * m:3 * m] + term[3 * m:])
+            if acc is None:
+                acc = term
+            elif SIGNS[q] > 0:
+                acc = acc + term
+            else:
+                acc = acc - term
         return acc
 
     def chunk(base):
-        block = pair(base, 128, 512, 256)
-        local_ref[base:base + 128, :] = block
-        front_ref[:, base:base + 128] = block[:, :128].T[:NB, :]
+        block = pair(base, 64, 512, 256)
+        local_ref[base:base + 64, :] = block
+
+    def turn(base):
+        front_ref[:, base:base + 128] = local_ref[base:base + 128, 0:128].T[:NB, :]
 
     load(cols_ref, 0, 64, 4, 512)
     load(rows_ref, 0, 128, 3, 0)
@@ -465,17 +469,22 @@
     column.landed(0)
     column.message(2).start()
     column.landed(1)
-    load(rows_ref, 128, 384, 3, 128)
+    load(rows_ref, 128, 128, 3, 128)
     column.landed(2)
     todo = plane.stages()
     todo[0]()
     for colour in range(2):
         across(colour, plane.view(colour, 0, 0), 0).start()
+    load(rows_ref, 256, 256, 3, 256)
+    todo[1]()
+    for n in range(5):
+        chunk(64 * n)
+        todo[2 + n]()
+    for n in range(5, 8):
+        chunk(64 * n)
     for n in range(4):
-        chunk(128 * n)
-        todo[1 + n]()
-    for n in range(5, 8):
-        todo[n]()
+        turn(128 * n)
+    todo[7]()
     plane.drain()
     column.drain()
     mirror = Plane(lambda colour, x, y: out_ref.at[x, y, :, 1 - core, pl.ds(32 * colour, 32)], send, recv, None)
@@ -560,50 +569,64 @@
         for h in range(2):
             top_copy(s, h).start()
 
-    def step(j, carry):
-        for n in range(8):
-            @pl.when(j == n)
-            def _(n=n):
-                todo[n]()
-        off = pl.multiple_of(j * 128, 128)
-        diag_ref[...] = a_ref[pl.ds(off, 128), pl.ds(off, 128)]
-        invert_block(diag_ref, inv_ref, tmp_ref)
+    def bulk(j, off):
+        done = j * 128
+        cat = icat_ref[...]
+        for r in range(4):
+            hi, lo = split(a_ref[256 * r:256 * r + 256, pl.ds(off, 128)])
+            v = lax.dot_general(jnp.concatenate([hi, lo, hi], axis=1), cat, TN, preferred_element_type=F32)
+            row = lax.broadcasted_iota(jnp.int32, (256, 128), 0) + 256 * r
+            hi, lo = split(jnp.where(row >= done, v, 0.0))
+            pcat_ref[256 * r:256 * r + 256, 0:128] = hi
+            pcat_ref[256 * r:256 * r + 256, 128:256] = lo
+            pcat_ref[256 * r:256 * r + 256, 256:384] = hi
+            qcat_ref[256 * r:256 * r + 256, 0:128] = hi
+            qcat_ref[256 * r:256 * r + 256, 128:256] = hi
+            qcat_ref[256 * r:256 * r + 256, 256:384] = lo
+            low_hi_ref[256 * r:256 * r + 256, pl.ds(off, 128)] = hi
+            low_lo_ref[256 * r:256 * r + 256, pl.ds(off, 128)] = lo
+        for r in range(4):
+            for k in range(r + 1):
+                a_ref[256 * r:256 * r + 256, 256 * k:256 * k + 256] -= lax.dot_general(
+                    pcat_ref[256 * r:256 * r + 256, :], qcat_ref[256 * k:256 * k + 256, :], TN, preferred_element_type=F32)
+
+    def keep(off):
         hi, lo = split(inv_ref[...])
         inv_hi_ref[pl.ds(off, 128), :] = hi
         inv_lo_ref[pl.ds(off, 128), :] = lo
         icat_ref[:, 0:128] = hi
         icat_ref[:, 128:256] = hi
         icat_ref[:, 256:384] = lo
-        first = (j + 1) // 2
-
-        def panel(r, c):
-            base = pl.multiple_of(r * 256, 256)
-            hi, lo = split(a_ref[pl.ds(base, 256), pl.ds(off, 128)])
-            v = lax.dot_general(jnp.concatenate([hi, lo, hi], axis=1), icat_ref[...], TN, preferred_element_type=F32)
-            hi, lo = split(v)
-            pcat_ref[pl.ds(base, 256), 0:128] = hi
-            pcat_ref[pl.ds(base, 256), 128:256] = lo
-            pcat_ref[pl.ds(base, 256), 256:384] = hi
-            qcat_ref[pl.ds(base, 256), 0:128] = hi
-            qcat_ref[pl.ds(base, 256), 128:256] = hi
-            qcat_ref[pl.ds(base, 256), 256:384] = lo
-            low_hi_ref[pl.ds(base, 256), pl.ds(off, 128)] = hi
-            low_lo_ref[pl.ds(base, 256), pl.ds(off, 128)] = lo
-            return c
-        lax.fori_loop(first, KK // 256, panel, 0)
-
-        def update(r, c):
-            base = pl.multiple_of(r * 256, 256)
-
-            def inner(k, c):
-                cb = pl.multiple_of(k * 256, 256)
-                a_ref[pl.ds(base, 256), pl.ds(cb, 256)] -= lax.dot_general(
-                    pcat_ref[pl.ds(base, 256), :], qcat_ref[pl.ds(cb, 256), :], TN, preferred_element_type=F32)
-                return c
-            return lax.fori_loop(first, r + 1, inner, c)
-        lax.fori_loop(first, KK // 256, update, 0)
+
+    def ahead(off):
+        nxt = pl.multiple_of(off + 128, 128)
+        hi, lo = split(a_ref[pl.ds(nxt, 128), pl.ds(off, 128)])
+        v = lax.dot_general(jnp.concatenate([hi, lo, hi], axis=1), icat_ref[...], TN, preferred_element_type=F32)
+        hi, lo = split(v)
+        diag_ref[...] = a_ref[pl.ds(nxt, 128), pl.ds(nxt, 128)] - lax.dot_general(
+            jnp.concatenate([hi, lo, hi], axis=1), jnp.concatenate([hi, hi, lo], axis=1), TN, preferred_element_type=F32)
+
+    todo[0]()
+    diag_ref[...] = a_ref[0:128, 0:128]
+    invert_block(diag_ref, inv_ref, tmp_ref)
+    keep(0)
+    ahead(0)
+
+    def step(j, carry):
+        off = pl.multiple_of(j * 128, 128)
+        for n in range(1, 8):
+            @pl.when(j == n)
+            def _(n=n):
+                todo[n]()
+        invert_block(diag_ref, inv_ref, tmp_ref)
+        bulk(j, pl.multiple_of(off - 128, 128))
+        keep(off)
+
+        @pl.when(j < 7)
+        def _():
+            ahead(off)
         return carry
-    lax.fori_loop(0, KK // 128, step, 0)
+    lax.fori_loop(1, 8, step, 0)
     plane.drain()
     for s in range(1, 8):
         for h in range(2):
@@ -687,7 +710,7 @@
 def per_device(factors, x_factor, zinv_factor, placement):
     rows, cols = route(factors, placement.reshape(32, 128))
     local, front, tiles = pair_blocks(rows.reshape(512, W), cols.reshape(256, W), x_factor, zinv_factor)
-    rest, inv_hi, inv_lo, low_hi, low_lo = factor(tiles.reshape(128, NB, 128), front, local[:128])
+    rest, inv_hi, inv_lo, low_hi, low_lo = factor(tiles.reshape(128, NB, 128), front, local)
     return solve(rest, inv_hi, inv_lo, low_hi, low_lo, local)
 
 

time: 139 us -> 124 us (0.89)
  Pallas kernels: 134 us -> 119 us
    pallas_call x1, Pallas kernels: 42 us -> 34.3 us  [factor(): pl.pallas_call(factor_kernel, out_shape=(jax.ShapeDtypeStruct((KK, 768),...]
    pallas_call x1, Pallas kernels: 37.9 us -> 30.5 us  [pair_blocks(): pl.pallas_call(pair_kernel, out_shape=(jax.ShapeDtypeStruct((512, 256), F...]
where the time goes in v7:
time: 124 us
  Pallas kernels  119 us (96%)
  local copies, waits for them, and re-layouts  4.46 us (4%)
    pallas_call x1, Pallas kernels, route(): pl.pallas_call(route_kernel, out_shape=(jax.ShapeDtypeStruct((4, 4, 32, W...  45.8 us
    pallas_call x1, Pallas kernels, factor(): pl.pallas_call(factor_kernel, out_shape=(jax.ShapeDtypeStruct((KK, 768),...  34.3 us
    pallas_call x1, Pallas kernels, pair_blocks(): pl.pallas_call(pair_kernel, out_shape=(jax.ShapeDtypeStruct((512, 256), F...  30.5 us
    pallas_call x1, Pallas kernels, solve(): pl.pallas_call(solve_kernel, out_shape=(jax.ShapeDtypeStruct((512, 256),...  8.35 us
    unnamed x8, local copies, waits for them, and re-layouts  3.69 us

profile of v7, /device:TPU:1, one launch (start us, length us, event | category | flops | bytes accessed | tf_op | source)
XLA Modules:
  0.0 124.1 jit_solution(12530294940679978135)
XLA Ops:
  0.6 0.0 copy-start.2
  0.6 0.9 copy-done.2
  1.5 0.0 copy-start.3
  1.5 0.7 copy-done.3
  2.3 45.8 %route.1 = (bf16[4,4,32,2176]{3,2,1,0:T(8,128)(2,1)S(1)}, bf16[8,32,2176]{2,1,0:T(8,128)(2,1)S(1)}) custom-call(bf16[4,32,512]{2,1,0:T(8,128)(2,1)S(1)} %copy-done.2, s32[32,128]{1,0:T(8,128)S(1)} %bitcast.7), custom_call_target="tpu_custom_call" | custom-call | tf_op jit(solution)/shard_map/route/pallas_call | solution.py:380
  48.1 0.0 copy-start
  48.1 1.0 copy-done
  49.1 0.0 copy-start.1
  49.1 1.0 copy-done.1
  50.2 30.5 %pairs.1 = (f32[512,256]{1,0:T(8,128)S(1)}, f32[64,512]{1,0:T(8,128)S(1)}, f32[4,4,4,2,64,128]{5,4,3,2,1,0:T(8,128)S(1)}) custom-call(bf16[512,2176]{1,0:T(8,128)(2,1)S(1)} %bitcast.5, bf16[256,2176]{1,0:T(8,128)(2,1)S(1)} %bitcast.6, bf16[512,512]{1,0:T(8,128)(2,1)S(1)} %copy-done, bf16[512,512]{1,0:T(8,128)(2,1)S(1)} %copy-done.1), custom_call_target="tpu_custom_call" | custom-call | tf_op jit(solution)/shard_map/pairs/pallas_call | solution.py:505
  80.7 34.3 %factor.1 = (f32[1024,768]{1,0:T(8,128)S(1)}, bf16[1024,128]{1,0:T(8,128)(2,1)S(1)}, bf16[1024,128]{1,0:T(8,128)(2,1)S(1)}, bf16[1024,1024]{1,0:T(8,128)(2,1)S(1)}, bf16[1024,1024]{1,0:T(8,128)(2,1)S(1)}) custom-call(f32[128,64,128]{2,1,0:T(8,128)S(1)} %bitcast.4, f32[64,512]{1,0:T(8,128)S(1)} %get-tuple-element.15.front_ref, ...), custom_call_target="tpu_custom_call" | custom-call | tf_op jit(solution)/shard_map/factor/pallas_call | solution.py:641
  114.9 8.4 %solve.1 = (f32[512,256]{1,0:T(8,128)}, f32[512,64]{1,0:T(8,128)S(1)}) custom-call(f32[1024,768]{1,0:T(8,128)S(1)} %get-tuple-element.17.rest_ref, bf16[1024,128]{1,0:T(8,128)(2,1)S(1)} %get-tuple-element.18.inv_hi_ref, bf16[1024,128]{1,0:T(8,128)(2,1)S(1)} %get-tuple-element.19.inv_lo_ref, bf16[1024,1024]{1,0:T(8,128)(2,1)S(1)} %get-tuple-element.20.low_hi_ref, ...), custom_call_target="tpu_custom_call" | custom-call | tf_op jit(solution)/shard_map/solve/pallas_call | solution.py:699
  123.3 0.8 copy.6
Async XLA Ops:
  0.6 0.9 copy-start.2
  1.5 0.7 copy-start.3
  48.1 1.0 copy-start
  49.1 1.0 copy-start.1

commit v8 on v7

--- a/solution.py
+++ b/solution.py
@@ -225,11 +225,14 @@
     return hit.astype(F32).astype(BF16)
 
 
-def route_kernel(factors_ref, placed_ref, rows_ref, cols_ref,
+def route_kernel(factors_hbm, placed_hbm, rows_ref, cols_ref, factors_ref, placed_ref, ls,
                  send_a, got_a, send_b, got_b, piece_ref, ss, rs, ps, pr, zs, zr, xs, xr):
     prow, pcol = lax.axis_index("prow"), lax.axis_index("pcol")
     twin = (lax.rem(pcol, 8), prow + 8 * (pcol // 8))
     at_home = prow == lax.rem(pcol, 8)
+    fetch = [pltpu.make_async_copy(placed_hbm, placed_ref, ls.at[0]), pltpu.make_async_copy(factors_hbm, factors_ref, ls.at[1])]
+    for f in fetch:
+        f.start()
     barrier = pltpu.get_barrier_semaphore()
     for s in range(1, 16):
         pl.semaphore_signal(barrier, inc=1, device_id=(prow, lax.rem(pcol + s, 16)), device_id_type=MESH)
@@ -241,6 +244,7 @@
         pl.semaphore_signal(barrier, inc=1, device_id=twin, device_id_type=MESH)
 
     device = prow * 16 + pcol
+    fetch[0].wait()
     line = jnp.broadcast_to(placed_ref[pl.ds(device // 4, 1), :], (8, 128))
     mine = pltpu.roll(line, lax.rem(4 - lax.rem(device, 4), 4) * 32, 1)[0:1, :32]
     group = (mine >> 6) & 7
@@ -250,6 +254,7 @@
     rank = jnp.dot(match.astype(F32).astype(BF16), ahead, preferred_element_type=F32).astype(jnp.int32)
     chosen = match & (rank == (row & 7))
     sel = chosen.astype(F32).astype(BF16)
+    fetch[1].wait()
     for r in range(RANK):
         send_a[:, :, 512 * r:512 * r + 512] = jnp.dot(sel, factors_ref[r], preferred_element_type=F32).reshape(8, 8, 512).astype(BF16)
 
@@ -380,9 +385,12 @@
     return pl.pallas_call(
         route_kernel,
         out_shape=(jax.ShapeDtypeStruct((4, 4, 32, W), BF16), jax.ShapeDtypeStruct((8, 32, W), BF16)),
-        in_specs=[pl.BlockSpec(memory_space=pltpu.VMEM)] * 2,
+        in_specs=[pl.BlockSpec(memory_space=pltpu.HBM)] * 2,
         out_specs=[pl.BlockSpec(memory_space=pltpu.VMEM)] * 2,
         scratch_shapes=[
+            pltpu.VMEM(factors.shape, BF16),
+            pltpu.VMEM((32, 128), jnp.int32),
+            pltpu.SemaphoreType.DMA((2,)),
             pltpu.VMEM((8, 8, W), BF16),
             pltpu.VMEM((8, 8, W), BF16),
             pltpu.VMEM((16, 8, W), BF16),
@@ -402,7 +410,7 @@
     )(factors, placed)
 
 
-def pair_kernel(rows_ref, cols_ref, xf_ref, zf_ref, local_ref, front_ref, out_ref, x_ref, z_ref, send, recv, zsend, zrecv, psend, precv):
+def pair_kernel(rows_ref, cols_ref, xf_hbm, zf_hbm, local_ref, front_ref, out_ref, xf_ref, zf_ref, ls, x_ref, z_ref, send, recv, zsend, zrecv, psend, precv):
     prow, pcol = lax.axis_index("prow"), lax.axis_index("pcol")
     z, core = prow // 2, lax.rem(prow, 2)
     other = (prow + 1 - 2 * core, pcol)
@@ -416,6 +424,9 @@
     def across(colour, part, n):
         return pltpu.make_async_remote_copy(part, part, psend.at[colour * 16 + n], precv.at[colour * 16 + n],
                                             device_id=other, device_id_type=MESH)
+    fetch = [pltpu.make_async_copy(xf_hbm, xf_ref, ls.at[0]), pltpu.make_async_copy(zf_hbm, zf_ref, ls.at[1])]
+    for f in fetch:
+        f.start()
     plane = Plane(block_view, send, recv, lambda colour, part, n: across(colour, part, n).start())
     column = Column(tile_view, zsend, zrecv)
     barrier = pltpu.get_barrier_semaphore()
@@ -426,11 +437,14 @@
     pl.semaphore_signal(barrier, inc=1, device_id=other, device_id_type=MESH)
     depth = xf_ref.shape[0]
 
-    def load(src, first, count, shift, at):
+    def load(src, first, count, shift, at, wait=False):
         tags = src[:, 2048:].astype(F32).astype(jnp.int32)
         spot = (tags[:, 0:1] >> shift) * NB + tags[:, 1:2] - first
         rows = lax.dot_general(pick(spot, None, count), src[:, :2048], TT, preferred_element_type=F32).astype(BF16)
         stack = jnp.concatenate([rows[:, r * depth:(r + 1) * depth] for r in range(RANK)], axis=0)
+        if wait:
+            for f in fetch:
+                f.wait()
         for dst, mat in ((x_ref, xf_ref), (z_ref, zf_ref)):
             images = jnp.dot(stack, mat[...], preferred_element_type=F32).astype(BF16)
             for r in range(RANK):
@@ -459,7 +473,7 @@
     def turn(base):
         front_ref[:, base:base + 128] = local_ref[base:base + 128, 0:128].T[:NB, :]
 
-    load(cols_ref, 0, 64, 4, 512)
+    load(cols_ref, 0, 64, 4, 512, True)
     load(rows_ref, 0, 128, 3, 0)
     out_ref[pcol // 4, lax.rem(pcol, 4), z, core] = pair(512, 64, 0, 128)
     pl.semaphore_wait(barrier, 7)
@@ -509,9 +523,12 @@
             jax.ShapeDtypeStruct((NB, 512), F32),
             jax.ShapeDtypeStruct((4, 4, 4, 2, NB, 128), F32),
         ),
-        in_specs=[pl.BlockSpec(memory_space=pltpu.VMEM)] * 4,
+        in_specs=[pl.BlockSpec(memory_space=pltpu.VMEM)] * 2 + [pl.BlockSpec(memory_space=pltpu.HBM)] * 2,
         out_specs=[pl.BlockSpec(memory_space=pltpu.VMEM)] * 3,
         scratch_shapes=[
+            pltpu.VMEM(x_factor.shape, BF16),
+            pltpu.VMEM(z_factor.shape, BF16),
+            pltpu.SemaphoreType.DMA((2,)),
             pltpu.VMEM((RANK, 768, d), BF16),
             pltpu.VMEM((RANK, 768, d), BF16),
             pltpu.SemaphoreType.DMA((30,)),

time: 124 us -> 125 us (level)
  no operation moved by 1% of the time
where the time goes in v8:
time: 125 us; the launch traced here: 124 us
  Pallas kernels  119 us (95%)
  local copies, waits for them, and re-layouts  4.46 us (4%)
    pallas_call x1, Pallas kernels, route(): pl.pallas_call(route_kernel, out_shape=(jax.ShapeDtypeStruct((4, 4, 32, W...  46.1 us
    pallas_call x1, Pallas kernels, factor(): pl.pallas_call(factor_kernel, out_shape=(jax.ShapeDtypeStruct((KK, 768),...  34.3 us
    pallas_call x1, Pallas kernels, pair_blocks(): pl.pallas_call(pair_kernel, out_shape=(jax.ShapeDtypeStruct((512, 256), F...  30.6 us
    pallas_call x1, Pallas kernels, solve(): pl.pallas_call(solve_kernel, out_shape=(jax.ShapeDtypeStruct((512, 256),...  8.35 us
    unnamed x8, local copies, waits for them, and re-layouts  3.69 us

profile of v8, /device:TPU:1, one launch (start us, length us, event | category | flops | bytes accessed | tf_op | source)
XLA Modules:
  0.0 124.5 jit_solution(17303296703859679392)
XLA Ops:
  0.6 0.0 copy-start.2
  0.6 0.9 copy-done.2
  1.5 0.0 copy-start.3
  1.5 0.7 copy-done.3
  2.3 46.1 %route.1 = (bf16[4,4,32,2176]{3,2,1,0:T(8,128)(2,1)S(1)}, bf16[8,32,2176]{2,1,0:T(8,128)(2,1)S(1)}) custom-call(bf16[4,32,512]{2,1,0:T(8,128)(2,1)S(1)} %copy-done.2, s32[32,128]{1,0:T(8,128)S(1)} %bitcast.7), custom_call_target="tpu_custom_call" | custom-call | tf_op jit(solution)/shard_map/route/pallas_call | solution.py:385
  48.3 0.0 copy-start
  48.3 1.0 copy-done
  49.4 0.0 copy-start.1
  49.4 1.0 copy-done.1
  50.4 30.6 %pairs.1 = (f32[512,256]{1,0:T(8,128)S(1)}, f32[64,512]{1,0:T(8,128)S(1)}, f32[4,4,4,2,64,128]{5,4,3,2,1,0:T(8,128)S(1)}) custom-call(bf16[512,2176]{1,0:T(8,128)(2,1)S(1)} %bitcast.5, bf16[256,2176]{1,0:T(8,128)(2,1)S(1)} %bitcast.6, bf16[512,512]{1,0:T(8,128)(2,1)S(1)} %copy-done, bf16[512,512]{1,0:T(8,128)(2,1)S(1)} %copy-done.1), custom_call_target="tpu_custom_call" | custom-call | tf_op jit(solution)/shard_map/pairs/pallas_call | solution.py:519
  81.0 34.3 %factor.1 = (f32[1024,768]{1,0:T(8,128)S(1)}, bf16[1024,128]{1,0:T(8,128)(2,1)S(1)}, bf16[1024,128]{1,0:T(8,128)(2,1)S(1)}, bf16[1024,1024]{1,0:T(8,128)(2,1)S(1)}, bf16[1024,1024]{1,0:T(8,128)(2,1)S(1)}) custom-call(f32[128,64,128]{2,1,0:T(8,128)S(1)} %bitcast.4, f32[64,512]{1,0:T(8,128)S(1)} %get-tuple-element.15.front_ref, ...), custom_call_target="tpu_custom_call" | custom-call | tf_op jit(solution)/shard_map/factor/pallas_call | solution.py:658
  115.3 8.4 %solve.1 = (f32[512,256]{1,0:T(8,128)}, f32[512,64]{1,0:T(8,128)S(1)}) custom-call(f32[1024,768]{1,0:T(8,128)S(1)} %get-tuple-element.17.rest_ref, bf16[1024,128]{1,0:T(8,128)(2,1)S(1)} %get-tuple-element.18.inv_hi_ref, bf16[1024,128]{1,0:T(8,128)(2,1)S(1)} %get-tuple-element.19.inv_lo_ref, bf16[1024,1024]{1,0:T(8,128)(2,1)S(1)} %get-tuple-element.20.low_hi_ref, ...), custom_call_target="tpu_custom_call" | custom-call | tf_op jit(solution)/shard_map/solve/pallas_call | solution.py:716
  123.7 0.8 copy.6
Async XLA Ops:
  0.6 0.9 copy-start.2
  1.5 0.7 copy-start.3
  48.3 1.0 copy-start
  49.4 1.0 copy-start.1

commit v9 on v7

--- a/solution.py
+++ b/solution.py
@@ -526,7 +526,7 @@
     )(rows, cols, x_factor, z_factor)
 
 
-def factor_kernel(tiles_ref, front_ref, top_ref, rest_ref, inv_hi_ref, inv_lo_ref, low_hi_ref, low_lo_ref,
+def factor_kernel(tiles_ref, front_ref, top_ref, rest_ref, inv_hi_ref, inv_lo_ref, low_hi_ref, low_lo_ref, sol_hi_ref, sol_lo_ref,
                   a_ref, diag_ref, inv_ref, tmp_ref, pcat_ref, qcat_ref, icat_ref, send, recv, ps, pr):
     prow, pcol = lax.axis_index("prow"), lax.axis_index("pcol")
 
@@ -612,13 +612,58 @@
     keep(0)
     ahead(0)
 
+    def thin(hi, lo, vh, vl):
+        return (lax.dot_general(hi, vh, NN, preferred_element_type=F32) + lax.dot_general(hi, vl, NN, preferred_element_type=F32)
+                + lax.dot_general(lo, vh, NN, preferred_element_type=F32))
+
+    def panel_rows(e):
+        top_at = pl.multiple_of(e * 256, 256)
+        low_at = pl.multiple_of(e * 256 + 128, 128)
+        top, low = pl.ds(top_at, 128), pl.ds(low_at, 128)
+        xh, xl = split(rest_ref[top, :])
+        th, tl = split(thin(inv_hi_ref[top, :], inv_lo_ref[top, :], xh, xl))
+        x = rest_ref[low, :] - thin(low_hi_ref[low, pl.ds(top_at, 128)], low_lo_ref[low, pl.ds(top_at, 128)], th, tl)
+        xh, xl = split(x)
+        bh, bl = split(thin(inv_hi_ref[low, :], inv_lo_ref[low, :], xh, xl))
+        sol_hi_ref[top, :] = th
+        sol_lo_ref[top, :] = tl
+        sol_hi_ref[low, :] = bh
+        sol_lo_ref[low, :] = bl
+        vh = jnp.concatenate([th, bh], axis=0)
+        vl = jnp.concatenate([tl, bl], axis=0)
+        for t in range(1, 4):
+            lh = low_hi_ref[256 * t:256 * t + 256, pl.ds(top_at, 256)]
+            ll = low_lo_ref[256 * t:256 * t + 256, pl.ds(top_at, 256)]
+            v = thin(lh, ll, vh, vl)
+            rest_ref[256 * t:256 * t + 256, :] -= jnp.where(e < t, v, 0.0)
+
     def step(j, carry):
         off = pl.multiple_of(j * 128, 128)
-        for n in range(1, 8):
+        for n in range(1, 5):
             @pl.when(j == n)
             def _(n=n):
-                todo[n]()
+                todo[2 * n - 1]()
+                if n < 4:
+                    todo[2 * n]()
         invert_block(diag_ref, inv_ref, tmp_ref)
+        bulk(j, pl.multiple_of(off - 128, 128))
+        keep(off)
+        ahead(off)
+        return carry
+    lax.fori_loop(1, 5, step, 0)
+    for s in range(1, 8):
+        for h in range(2):
+            n = (s - 1) * 2 + h
+            place = top_place(lax.rem(prow + 8 - s, 8), h)
+            pltpu.make_async_remote_copy(place, place, send.at[n], recv.at[n],
+                                         device_id=(prow, pcol), device_id_type=MESH).wait_recv()
+            top_copy(s, h).wait_send()
+    plane.drain()
+
+    def last(j, carry):
+        off = pl.multiple_of(j * 128, 128)
+        invert_block(diag_ref, inv_ref, tmp_ref)
+        panel_rows(j - 5)
         bulk(j, pl.multiple_of(off - 128, 128))
         keep(off)
 
@@ -626,15 +671,7 @@
         def _():
             ahead(off)
         return carry
-    lax.fori_loop(1, 8, step, 0)
-    plane.drain()
-    for s in range(1, 8):
-        for h in range(2):
-            n = (s - 1) * 2 + h
-            top_copy(s, h).wait_send()
-            place = top_place(lax.rem(prow + 8 - s, 8), h)
-            pltpu.make_async_remote_copy(place, place, send.at[n], recv.at[n],
-                                         device_id=(prow, pcol), device_id_type=MESH).wait_recv()
+    lax.fori_loop(5, 8, last, 0)
 
 
 def factor(tiles, front, top):
@@ -646,9 +683,11 @@
             jax.ShapeDtypeStruct((KK, 128), BF16),
             jax.ShapeDtypeStruct((KK, KK), BF16),
             jax.ShapeDtypeStruct((KK, KK), BF16),
+            jax.ShapeDtypeStruct((768, 768), BF16),
+            jax.ShapeDtypeStruct((768, 768), BF16),
         ),
         in_specs=[pl.BlockSpec(memory_space=pltpu.VMEM)] * 3,
-        out_specs=[pl.BlockSpec(memory_space=pltpu.VMEM)] * 5,
+        out_specs=[pl.BlockSpec(memory_space=pltpu.VMEM)] * 7,
         scratch_shapes=[
             pltpu.VMEM((KK, KK), F32),
             pltpu.VMEM((128, 128), F32),
@@ -662,56 +701,55 @@
             pltpu.SemaphoreType.DMA((30,)),
             pltpu.SemaphoreType.DMA((30,)),
         ],
-        compiler_params=pltpu.CompilerParams(collective_id=3, has_side_effects=True, vmem_limit_bytes=40 << 20),
+        compiler_params=pltpu.CompilerParams(collective_id=3, has_side_effects=True, vmem_limit_bytes=18 << 20),
         name="factor",
     )(tiles, front, top)
 
 
-def solve_kernel(rest_ref, inv_hi_ref, inv_lo_ref, low_hi_ref, low_lo_ref, local_ref, trail_ref, panel_ref,
-                 hi_ref, lo_ref, p_ref):
-    for j in range(KK // 128):
-        x = rest_ref[128 * j:128 * j + 128, :]
-        if j:
-            lh, ll = low_hi_ref[128 * j:128 * j + 128, :128 * j], low_lo_ref[128 * j:128 * j + 128, :128 * j]
-            ph, pw = hi_ref[:128 * j, :], lo_ref[:128 * j, :]
-            x = x - (lax.dot_general(lh, ph, NN, preferred_element_type=F32)
-                     + lax.dot_general(lh, pw, NN, preferred_element_type=F32)
-                     + lax.dot_general(ll, ph, NN, preferred_element_type=F32))
+def solve_kernel(rest_ref, inv_hi_ref, inv_lo_ref, low_hi_ref, low_lo_ref, sol_hi_ref, sol_lo_ref, local_ref, trail_ref, panel_ref,
+                 hi_ref, lo_ref):
+    def thin(hi, lo, vh, vl):
+        return (lax.dot_general(hi, vh, NN, preferred_element_type=F32) + lax.dot_general(hi, vl, NN, preferred_element_type=F32)
+                + lax.dot_general(lo, vh, NN, preferred_element_type=F32))
+    hi_ref[:768, :] = sol_hi_ref[...]
+    lo_ref[:768, :] = sol_lo_ref[...]
+    for j in (6, 7):
+        at = slice(128 * j, 128 * j + 128)
+        x = rest_ref[at, :]
+        if j == 7:
+            x = x - thin(low_hi_ref[896:, 768:896], low_lo_ref[896:, 768:896], hi_ref[768:896, :], lo_ref[768:896, :])
         xh, xl = split(x)
-        ih, il = inv_hi_ref[128 * j:128 * j + 128, :], inv_lo_ref[128 * j:128 * j + 128, :]
-        v = (lax.dot_general(ih, xh, NN, preferred_element_type=F32)
-             + lax.dot_general(ih, xl, NN, preferred_element_type=F32)
-             + lax.dot_general(il, xh, NN, preferred_element_type=F32))
-        p_ref[128 * j:128 * j + 128, :] = v[:, :512]
-        vh, vl = split(v)
-        hi_ref[128 * j:128 * j + 128, :] = vh
-        lo_ref[128 * j:128 * j + 128, :] = vl
+        vh, vl = split(thin(inv_hi_ref[at, :], inv_lo_ref[at, :], xh, xl))
+        hi_ref[at, :] = vh
+        lo_ref[at, :] = vl
     rh, rl = hi_ref[:, :512], lo_ref[:, :512]
     ch, cl = hi_ref[:, 512:], lo_ref[:, 512:]
     trail_ref[...] = local_ref[...] - (lax.dot_general(rh, ch, TT, preferred_element_type=F32)
                                        + lax.dot_general(rh, cl, TT, preferred_element_type=F32)
                                        + lax.dot_general(rl, ch, TT, preferred_element_type=F32))
     pcol = lax.axis_index("pcol")
-    panel_ref[...] = p_ref[pl.ds(pl.multiple_of(pcol * NB, NB), NB), :].T
-
-
-def solve(rest, inv_hi, inv_lo, low_hi, low_lo, local):
+    at = pl.ds(pl.multiple_of(pcol * NB, NB), NB)
+    panel_ref[...] = hi_ref[at, :512].astype(F32) + lo_ref[at, :512].astype(F32)
+
+
+def solve(rest, inv_hi, inv_lo, low_hi, low_lo, ahead_hi, ahead_lo, local):
     return pl.pallas_call(
         solve_kernel,
-        out_shape=(jax.ShapeDtypeStruct((512, 256), F32), jax.ShapeDtypeStruct((512, NB), F32)),
-        in_specs=[pl.BlockSpec(memory_space=pltpu.VMEM)] * 6,
+        out_shape=(jax.ShapeDtypeStruct((512, 256), F32), jax.ShapeDtypeStruct((NB, 512), F32)),
+        in_specs=[pl.BlockSpec(memory_space=pltpu.VMEM)] * 8,
         out_specs=[pl.BlockSpec(memory_space=pltpu.VMEM)] * 2,
-        scratch_shapes=[pltpu.VMEM((KK, 768), BF16)] * 2 + [pltpu.VMEM((KK, 512), F32)],
-        compiler_params=pltpu.CompilerParams(vmem_limit_bytes=40 << 20),
+        scratch_shapes=[pltpu.VMEM((KK, 768), BF16)] * 2,
+        compiler_params=pltpu.CompilerParams(vmem_limit_bytes=18 << 20),
         name="solve",
-    )(rest, inv_hi, inv_lo, low_hi, low_lo, local)
+    )(rest, inv_hi, inv_lo, low_hi, low_lo, ahead_hi, ahead_lo, local)
 
 
 def per_device(factors, x_factor, zinv_factor, placement):
     rows, cols = route(factors, placement.reshape(32, 128))
     local, front, tiles = pair_blocks(rows.reshape(512, W), cols.reshape(256, W), x_factor, zinv_factor)
-    rest, inv_hi, inv_lo, low_hi, low_lo = factor(tiles.reshape(128, NB, 128), front, local)
-    return solve(rest, inv_hi, inv_lo, low_hi, low_lo, local)
+    rest, inv_hi, inv_lo, low_hi, low_lo, ahead_hi, ahead_lo = factor(tiles.reshape(128, NB, 128), front, local)
+    trailing, panel = solve(rest, inv_hi, inv_lo, low_hi, low_lo, ahead_hi, ahead_lo, local)
+    return (trailing, panel.T)
 
 
 def solution(mesh):

time: 124 us -> 120 us (0.968)
  Pallas kernels: 119 us -> 115 us
    pallas_call x1, Pallas kernels: 8.35 us -> 2.71 us  [solve(): pl.pallas_call(solve_kernel, out_shape=(jax.ShapeDtypeStruct((512, 256),...]
    pallas_call x1, Pallas kernels: 34.3 us -> 35.7 us  [factor(): pl.pallas_call(factor_kernel, out_shape=(jax.ShapeDtypeStruct((KK, 768),...]
where the time goes in v9:
time: 120 us; the launch traced here: 119 us
  Pallas kernels  115 us (96%)
  local copies, waits for them, and re-layouts  3.69 us (3%)
    pallas_call x1, Pallas kernels, route(): pl.pallas_call(route_kernel, out_shape=(jax.ShapeDtypeStruct((4, 4, 32, W...  45.8 us
    pallas_call x1, Pallas kernels, factor(): pl.pallas_call(factor_kernel, out_shape=(jax.ShapeDtypeStruct((KK, 768),...  35.7 us
    pallas_call x1, Pallas kernels, pair_blocks(): pl.pallas_call(pair_kernel, out_shape=(jax.ShapeDtypeStruct((512, 256), F...  30.5 us
    unnamed x8, local copies, waits for them, and re-layouts  3.69 us
    pallas_call x1, Pallas kernels, solve(): pl.pallas_call(solve_kernel, out_shape=(jax.ShapeDtypeStruct((512, 256),...  2.71 us

profile of v9, /device:TPU:1, one launch (start us, length us, event | category | flops | bytes accessed | tf_op | source)
XLA Modules:
  0.0 119.1 jit_solution(7521565389426270946)
XLA Ops:
  0.6 0.0 copy-start.2
  0.6 0.9 copy-done.2
  1.5 0.0 copy-start.3
  1.5 0.7 copy-done.3
  2.3 45.8 %route.1 = (bf16[4,4,32,2176]{3,2,1,0:T(8,128)(2,1)S(1)}, bf16[8,32,2176]{2,1,0:T(8,128)(2,1)S(1)}) custom-call(bf16[4,32,512]{2,1,0:T(8,128)(2,1)S(1)} %copy-done.2, s32[32,128]{1,0:T(8,128)S(1)} %bitcast.8), custom_call_target="tpu_custom_call" | custom-call | tf_op jit(solution)/shard_map/route/pallas_call | solution.py:380
  48.1 0.0 copy-start
  48.1 1.0 copy-done
  49.1 0.0 copy-start.1
  49.1 1.0 copy-done.1
  50.2 30.5 %pairs.1 = (f32[512,256]{1,0:T(8,128)S(1)}, f32[64,512]{1,0:T(8,128)S(1)}, f32[4,4,4,2,64,128]{5,4,3,2,1,0:T(8,128)S(1)}) custom-call(bf16[512,2176]{1,0:T(8,128)(2,1)S(1)} %bitcast.6, bf16[256,2176]{1,0:T(8,128)(2,1)S(1)} %bitcast.7, bf16[512,512]{1,0:T(8,128)(2,1)S(1)} %copy-done, bf16[512,512]{1,0:T(8,128)(2,1)S(1)} %copy-done.1), custom_call_target="tpu_custom_call" | custom-call | tf_op jit(solution)/shard_map/pairs/pallas_call | solution.py:505
  80.7 35.7 %factor.1 = (f32[1024,768]{1,0:T(8,128)S(1)}, bf16[1024,128]{1,0:T(8,128)(2,1)S(1)}, bf16[1024,128]{1,0:T(8,128)(2,1)S(1)}, bf16[1024,1024]{1,0:T(8,128)(2,1)S(1...) custom-call(f32[128,64,128]{2,1,0:T(8,128)S(1)} %bitcast.5, ...), custom_call_target="tpu_custom_call" | custom-call | tf_op jit(solution)/shard_map/factor/pallas_call | solution.py:678
  116.4 2.7 %solve.1 = (f32[512,256]{1,0:T(8,128)}, f32[64,512]{1,0:T(8,128)}) custom-call(f32[1024,768]{1,0:T(8,128)S(1)} %get-tuple-element.21.rest_ref, bf16[1024,128]{1,0:T(8,128)(2,1)S(1)} %get-tuple-element.22.inv_hi_ref, bf16[1024,128]{1,0:T(8,128)(2,1)S(1)} %get-tuple-element.23.inv_lo_ref, bf16[1024,1024]{1,0:T(8,128)(2,1)S(1)} %get-tuple-element.24.low_hi_ref, ...), custom_call_target="tpu_custom_call" | custom-call | tf_op jit(solution)/shard_map/solve/pallas_call | solution.py:736
Async XLA Ops:
  0.6 0.9 copy-start.2
  1.5 0.7 copy-start.3
  48.1 1.0 copy-start
  49.1 1.0 copy-start.1

commit v10 on v9

--- a/solution.py
+++ b/solution.py
@@ -469,18 +469,18 @@
     column.landed(0)
     column.message(2).start()
     column.landed(1)
-    load(rows_ref, 128, 128, 3, 128)
+    chunk(0)
     column.landed(2)
     todo = plane.stages()
     todo[0]()
     for colour in range(2):
         across(colour, plane.view(colour, 0, 0), 0).start()
-    load(rows_ref, 256, 256, 3, 256)
+    load(rows_ref, 128, 384, 3, 128)
     todo[1]()
-    for n in range(5):
+    for n in range(1, 6):
         chunk(64 * n)
-        todo[2 + n]()
-    for n in range(5, 8):
+        todo[1 + n]()
+    for n in range(6, 8):
         chunk(64 * n)
     for n in range(4):
         turn(128 * n)

time: 120 us -> 120 us (level)
  no operation moved by 1% of the time
where the time goes in v10:
time: 120 us; the launch traced here: 119 us
  Pallas kernels  115 us (96%)
  local copies, waits for them, and re-layouts  3.69 us (3%)
    pallas_call x1, Pallas kernels, route(): pl.pallas_call(route_kernel, out_shape=(jax.ShapeDtypeStruct((4, 4, 32, W...  45.8 us
    pallas_call x1, Pallas kernels, factor(): pl.pallas_call(factor_kernel, out_shape=(jax.ShapeDtypeStruct((KK, 768),...  35.7 us
    pallas_call x1, Pallas kernels, pair_blocks(): pl.pallas_call(pair_kernel, out_shape=(jax.ShapeDtypeStruct((512, 256), F...  30.5 us
    unnamed x8, local copies, waits for them, and re-layouts  3.69 us
    pallas_call x1, Pallas kernels, solve(): pl.pallas_call(solve_kernel, out_shape=(jax.ShapeDtypeStruct((512, 256),...  2.71 us

profile of v10, /device:TPU:1, one launch (start us, length us, event | category | flops | bytes accessed | tf_op | source)
XLA Modules:
  0.0 119.1 jit_solution(55298773225491996)
XLA Ops:
  0.6 0.0 copy-start.2
  0.6 0.9 copy-done.2
  1.5 0.0 copy-start.3
  1.5 0.7 copy-done.3
  2.3 45.8 %route.1 = (bf16[4,4,32,2176]{3,2,1,0:T(8,128)(2,1)S(1)}, bf16[8,32,2176]{2,1,0:T(8,128)(2,1)S(1)}) custom-call(bf16[4,32,512]{2,1,0:T(8,128)(2,1)S(1)} %copy-done.2, s32[32,128]{1,0:T(8,128)S(1)} %bitcast.8), custom_call_target="tpu_custom_call" | custom-call | tf_op jit(solution)/shard_map/route/pallas_call | solution.py:380
  48.1 0.0 copy-start
  48.1 1.0 copy-done
  49.1 0.0 copy-start.1
  49.1 1.0 copy-done.1
  50.2 30.5 %pairs.1 = (f32[512,256]{1,0:T(8,128)S(1)}, f32[64,512]{1,0:T(8,128)S(1)}, f32[4,4,4,2,64,128]{5,4,3,2,1,0:T(8,128)S(1)}) custom-call(bf16[512,2176]{1,0:T(8,128)(2,1)S(1)} %bitcast.6, bf16[256,2176]{1,0:T(8,128)(2,1)S(1)} %bitcast.7, bf16[512,512]{1,0:T(8,128)(2,1)S(1)} %copy-done, bf16[512,512]{1,0:T(8,128)(2,1)S(1)} %copy-done.1), custom_call_target="tpu_custom_call" | custom-call | tf_op jit(solution)/shard_map/pairs/pallas_call | solution.py:505
  80.7 35.7 %factor.1 = (f32[1024,768]{1,0:T(8,128)S(1)}, bf16[1024,128]{1,0:T(8,128)(2,1)S(1)}, bf16[1024,128]{1,0:T(8,128)(2,1)S(1)}, bf16[1024,1024]{1,0:T(8,128)(2,1)S(1...) custom-call(f32[128,64,128]{2,1,0:T(8,128)S(1)} %bitcast.5, ...), custom_call_target="tpu_custom_call" | custom-call | tf_op jit(solution)/shard_map/factor/pallas_call | solution.py:678
  116.4 2.7 %solve.1 = (f32[512,256]{1,0:T(8,128)}, f32[64,512]{1,0:T(8,128)}) custom-call(f32[1024,768]{1,0:T(8,128)S(1)} %get-tuple-element.21.rest_ref, bf16[1024,128]{1,0:T(8,128)(2,1)S(1)} %get-tuple-element.22.inv_hi_ref, bf16[1024,128]{1,0:T(8,128)(2,1)S(1)} %get-tuple-element.23.inv_lo_ref, bf16[1024,1024]{1,0:T(8,128)(2,1)S(1)} %get-tuple-element.24.low_hi_ref, ...), custom_call_target="tpu_custom_call" | custom-call | tf_op jit(solution)/shard_map/solve/pallas_call | solution.py:736
Async XLA Ops:
  0.6 0.9 copy-start.2
  1.5 0.7 copy-start.3
  48.1 1.0 copy-start
  49.1 1.0 copy-start.1

commit v11 on v9

--- a/solution.py
+++ b/solution.py
@@ -294,7 +294,7 @@
     def cols_view(z, core):
         return cols_ref.at[z * 2 + core]
 
-    for s in range(1, 8):
+    for s in (4, 3, 5, 2, 6, 7, 1):
         a_copy(s).start()
     for s in range(1, 8):
         spot = got_a.at[lax.rem(prow + 8 - s, 8)]
@@ -310,7 +310,7 @@
         slot = jnp.where(half == h, (8 * h + ((base[h] + li) & 7)) * 8 + (li >> 3), slot)
     send_b[...] = lax.dot_general(pick(slot, valid, 128), got, TT, preferred_element_type=F32).reshape(16, 8, W).astype(BF16)
     got_b[pcol] = send_b[pcol]
-    for s in range(1, 16):
+    for s in (10, 9, 11, 6, 14, 8, 2, 7, 13, 5, 15, 12, 4, 3, 1):
         b_copy(s).start()
     for s in range(1, 16):
         spot = got_b.at[lax.rem(pcol + 16 - s, 16)]

time: 120 us -> 118 us (0.983)
  Pallas kernels: 115 us -> 112 us
    pallas_call x1, Pallas kernels: 45.8 us -> 42.8 us  [route(): pl.pallas_call(route_kernel, out_shape=(jax.ShapeDtypeStruct((4, 4, 32, W...]
    pallas_call x1, Pallas kernels: 30.5 us -> 31.9 us  [pair_blocks(): pl.pallas_call(pair_kernel, out_shape=(jax.ShapeDtypeStruct((512, 256), F...]
where the time goes in v11:
time: 118 us; the launch traced here: 117 us
  Pallas kernels  112 us (95%)
  local copies, waits for them, and re-layouts  3.69 us (3%)
    pallas_call x1, Pallas kernels, route(): pl.pallas_call(route_kernel, out_shape=(jax.ShapeDtypeStruct((4, 4, 32, W...  42.8 us
    pallas_call x1, Pallas kernels, factor(): pl.pallas_call(factor_kernel, out_shape=(jax.ShapeDtypeStruct((KK, 768),...  35.1 us
    pallas_call x1, Pallas kernels, pair_blocks(): pl.pallas_call(pair_kernel, out_shape=(jax.ShapeDtypeStruct((512, 256), F...  31.9 us
    unnamed x8, local copies, waits for them, and re-layouts  3.69 us
    pallas_call x1, Pallas kernels, solve(): pl.pallas_call(solve_kernel, out_shape=(jax.ShapeDtypeStruct((512, 256),...  2.71 us

profile of v11, /device:TPU:1, one launch (start us, length us, event | category | flops | bytes accessed | tf_op | source)
XLA Modules:
  0.0 116.9 jit_solution(14033231582189150379)
XLA Ops:
  0.6 0.0 copy-start.2
  0.6 0.9 copy-done.2
  1.5 0.0 copy-start.3
  1.5 0.7 copy-done.3
  2.3 42.8 %route.1 = (bf16[4,4,32,2176]{3,2,1,0:T(8,128)(2,1)S(1)}, bf16[8,32,2176]{2,1,0:T(8,128)(2,1)S(1)}) custom-call(bf16[4,32,512]{2,1,0:T(8,128)(2,1)S(1)} %copy-done.2, s32[32,128]{1,0:T(8,128)S(1)} %bitcast.8), custom_call_target="tpu_custom_call" | custom-call | tf_op jit(solution)/shard_map/route/pallas_call | solution.py:380
  45.1 0.0 copy-start
  45.1 1.0 copy-done
  46.1 0.0 copy-start.1
  46.1 1.0 copy-done.1
  47.1 31.9 %pairs.1 = (f32[512,256]{1,0:T(8,128)S(1)}, f32[64,512]{1,0:T(8,128)S(1)}, f32[4,4,4,2,64,128]{5,4,3,2,1,0:T(8,128)S(1)}) custom-call(bf16[512,2176]{1,0:T(8,128)(2,1)S(1)} %bitcast.6, bf16[256,2176]{1,0:T(8,128)(2,1)S(1)} %bitcast.7, bf16[512,512]{1,0:T(8,128)(2,1)S(1)} %copy-done, bf16[512,512]{1,0:T(8,128)(2,1)S(1)} %copy-done.1), custom_call_target="tpu_custom_call" | custom-call | tf_op jit(solution)/shard_map/pairs/pallas_call | solution.py:505
  79.0 35.1 %factor.1 = (f32[1024,768]{1,0:T(8,128)S(1)}, bf16[1024,128]{1,0:T(8,128)(2,1)S(1)}, bf16[1024,128]{1,0:T(8,128)(2,1)S(1)}, bf16[1024,1024]{1,0:T(8,128)(2,1)S(1...) custom-call(f32[128,64,128]{2,1,0:T(8,128)S(1)} %bitcast.5, ...), custom_call_target="tpu_custom_call" | custom-call | tf_op jit(solution)/shard_map/factor/pallas_call | solution.py:678
  114.1 2.7 %solve.1 = (f32[512,256]{1,0:T(8,128)}, f32[64,512]{1,0:T(8,128)}) custom-call(f32[1024,768]{1,0:T(8,128)S(1)} %get-tuple-element.21.rest_ref, bf16[1024,128]{1,0:T(8,128)(2,1)S(1)} %get-tuple-element.22.inv_hi_ref, bf16[1024,128]{1,0:T(8,128)(2,1)S(1)} %get-tuple-element.23.inv_lo_ref, bf16[1024,1024]{1,0:T(8,128)(2,1)S(1)} %get-tuple-element.24.low_hi_ref, ...), custom_call_target="tpu_custom_call" | custom-call | tf_op jit(solution)/shard_map/solve/pallas_call | solution.py:736
Async XLA Ops:
  0.6 0.9 copy-start.2
  1.5 0.7 copy-start.3
  45.1 1.0 copy-start
  46.1 1.0 copy-start.1
